TPU v7x, 32 devices: a whole 2x2x4 slice. The times are simulated.
32 devices in a mesh: expert: 8 (over y, x, core), shard: 4 (over z).
Axes of the slice: x: 2, y: 2, z: 4, core: 2. Of those that a mesh axis runs over, the one named last changes fastest.
Arguments:
- tokens: bfloat16 [16384, 768], P(('expert', 'shard')), may hold values from -6 to 6
- piece_start: int32 [32], P(('expert', 'shard')), may hold values from 0 to 256, as said below
- routes: int32 [16384, 2], P(('expert', 'shard')), may hold values from 0 to 15, all different within a row; in each aligned block of 512 rows (0 to 511, 512 to 1023, ...) at most 96 rows name the same one
- norm_gains: float32 [4, 768], replicated, may hold values from 0.5 to 1.5
- bias_tables: float32 [2, 12, 44], replicated, may hold values from -4 to 4
- qkv_weight: bfloat16 [2, 768, 2304], P(None, 'shard', 'expert'), may hold values from -0.21875 to 0.21875
- out_weight: bfloat16 [2, 768, 768], P(None, 'shard', 'expert'), may hold values from -1.25 to 1.25
- mlp_up: bfloat16 [768, 3072], P('shard', 'expert'), may hold values from -0.21875 to 0.21875
- mlp_down: bfloat16 [3072, 768], P('shard', 'expert'), may hold values from -0.15625 to 0.15625
- router: bfloat16 [768, 16], P('shard', 'expert'), may hold values from -0.3125 to 0.3125
- expert_up: bfloat16 [16, 768, 3072], P('expert', None, 'shard'), may hold values from -0.21875 to 0.21875
- expert_down: bfloat16 [16, 3072, 768], P('expert', 'shard'), may hold values from -0.15625 to 0.15625
- cotangent: bfloat16 [16384, 768], P(('expert', 'shard')), may hold values from -6 to 6
Outputs:
- output: bfloat16 [16384, 768], P(('expert', 'shard'))
- grad_input: float32 [16384, 768], P(('expert', 'shard'))
- grad_norm_gains: float32 [4, 768], replicated
- grad_bias_tables: float32 [2, 12, 44], replicated
- grad_qkv_weight: float32 [2, 768, 2304], P(None, 'shard', 'expert')
- grad_out_weight: float32 [2, 768, 768], P(None, 'shard', 'expert')
- grad_mlp_up: float32 [768, 3072], P('shard', 'expert')
- grad_mlp_down: float32 [3072, 768], P('shard', 'expert')
- grad_router: float32 [768, 16], P('shard', 'expert')
- grad_expert_up: float32 [16, 768, 3072], P('expert', None, 'shard')
- grad_expert_down: float32 [16, 3072, 768], P('expert', 'shard')
Inputs may be any that keep to these rules, and one draw needn't show every extreme that they name: `routes`: in the rows of one device (aligned blocks of 512 tokens) no expert is named by more than 96 tokens; a token's two experts differ. Sequence s has one picture piece, positions piece_start[s] to piece_start[s] + 255.
All inputs are finite; a program needn't handle non-finite values.
Results may differ from a plain program's by a relative error of at most 0.025.
Values may be sent and summed in bfloat16 or wider, within the bound.
A program may use at most 320 MiB of HBM per device.

v0:
```python
import jax
import jax.numpy as jnp
from jax import lax
from jax.sharding import PartitionSpec as P

HEADS = 12
PIECE = 256


bucket_edges = (
    1,
    2,
    3,
    4,
    6,
    8,
    12,
    16,
    24,
    32,
    48,
    64,
    96,
    128,
    192,
    256,
    384,
    512,
    768,
    1024,
    1536,
)
norm_eps = 1e-06
far_below = -1e30


def bucket_onehot(length, buckets):
    distance = jnp.arange(1 - length, length, dtype=jnp.int32)
    edge_list = jnp.array(bucket_edges, dtype=jnp.int32)
    magnitude = jnp.sum(
        (jnp.abs(distance)[:, None] >= edge_list[None, :]).astype(jnp.int32),
        axis=1,
        dtype=jnp.int32,
    )
    bucket = magnitude + buckets // 2 * (distance > 0).astype(jnp.int32)
    return (bucket[:, None] == jnp.arange(buckets, dtype=jnp.int32)[None, :]).astype(jnp.float32)


def normalize(field, gain):
    return field * lax.rsqrt(jnp.mean(field * field, axis=1, keepdims=True) + norm_eps) * gain


def normalize_back(field, gain, grad):
    inverse = lax.rsqrt(jnp.mean(field * field, axis=1, keepdims=True) + norm_eps)
    unit = field * inverse
    scaled = grad * gain
    field_grad = inverse * (scaled - unit * jnp.mean(scaled * unit, axis=1, keepdims=True))
    return (field_grad, jnp.sum(grad * unit, axis=0))


def gelu_back(pre_act, grad):
    return jax.vjp(jax.nn.gelu, pre_act)[1](grad)[0]


def block_bias(bias_vector, row_count, length):
    heads_count = bias_vector.shape[0]
    width = length + row_count
    segment = bias_vector
    segment = jnp.pad(segment, ((0, 0), (0, 1)))
    tiled = jnp.broadcast_to(segment[:, None, :], (heads_count, row_count, width)).reshape(
        heads_count, row_count * width
    )
    tiled = tiled[:, : row_count * (width - 1)].reshape(heads_count, row_count, width - 1)
    return tiled[:, :, row_count - 1 : row_count - 1 + length]


def diagonal_sums(grid):
    heads_count, row_count, length = grid.shape
    padded = jnp.pad(grid, ((0, 0), (0, 0), (row_count, 0)))
    flat = padded.reshape(heads_count, row_count * (length + row_count))
    flat = jnp.pad(flat, ((0, 0), (0, row_count)))
    skewed = flat.reshape(heads_count, row_count, length + row_count + 1)
    return jnp.sum(skewed[:, :, 1 : length + row_count], axis=1)


def masked_scores(query_block, key_rows, bias_vector, row_first, piece_first):
    row_count = query_block.shape[0]
    length = key_rows.shape[0]
    raw = jnp.einsum("qhd,khd->hqk", query_block, key_rows, preferred_element_type=jnp.float32)
    raw = raw * query_block.shape[2] ** (-0.5) + block_bias(bias_vector, row_count, length)
    query_pos = row_first + jnp.arange(row_count, dtype=jnp.int32)
    key_pos = jnp.arange(length, dtype=jnp.int32)
    query_in = (query_pos >= piece_first) & (query_pos < piece_first + PIECE)
    key_in = (key_pos >= piece_first) & (key_pos < piece_first + PIECE)
    keep_mask = (key_pos[None, :] <= query_pos[:, None]) | query_in[:, None] & key_in[None, :]
    return jnp.where(keep_mask[None, :, :], raw, far_below)


def head_views(qkv_rows):
    length = qkv_rows.shape[0]
    model_width = qkv_rows.shape[1] // 3
    heads_view = qkv_rows.reshape(length, 3, HEADS, model_width // HEADS)
    return (heads_view[:, 0], heads_view[:, 1], heads_view[:, 2])


def attend(qkv_rows, bias_vector, piece_first):
    length = qkv_rows.shape[0]
    model_width = qkv_rows.shape[1] // 3
    queries, key_rows, value_rows = head_views(qkv_rows)
    span_rows = min(512, length)
    span_count = length // span_rows

    def one_span(span_index):
        row_first = span_index * span_rows
        scores = masked_scores(queries, key_rows, bias_vector, row_first, piece_first)
        row_peak = jnp.max(scores, axis=2, keepdims=True)
        exponent = jnp.exp(scores - row_peak)
        summed = jnp.sum(exponent, axis=2, keepdims=True)
        weights = (exponent / summed).astype(jnp.bfloat16)
        mixed_rows = jnp.einsum(
            "hqk,khd->qhd", weights, value_rows, preferred_element_type=jnp.float32
        )
        return (
            mixed_rows.reshape(span_rows, model_width).astype(jnp.bfloat16),
            (row_peak + jnp.log(summed))[:, :, 0],
        )

    mixed_rows, log_totals = lax.map(one_span, jnp.arange(span_count, dtype=jnp.int32))
    return (mixed_rows.reshape(length, model_width), log_totals)


def attend_back(qkv_rows, mixed_grad, log_totals, bias_vector, piece_first):
    length = qkv_rows.shape[0]
    model_width = qkv_rows.shape[1] // 3
    queries, key_rows, value_rows = head_views(qkv_rows)
    head_size = queries.shape[2]
    factor = head_size ** (-0.5)
    grad_view = mixed_grad.reshape(length, HEADS, head_size)
    span_rows = min(512, length)
    span_count = length // span_rows

    def one_span(accum, span_index):
        key_grad, value_grad, vector_grad = accum
        row_first = span_index * span_rows
        scores = masked_scores(queries, key_rows, bias_vector, row_first, piece_first)
        weights = jnp.exp(scores - log_totals[span_index][:, :, None])
        weight_grad = jnp.einsum(
            "qhd,khd->hqk", grad_view, value_rows, preferred_element_type=jnp.float32
        )
        score_grad = weights * (weight_grad - jnp.sum(weights * weight_grad, axis=2, keepdims=True))
        score_grad = score_grad.astype(jnp.bfloat16)
        query_grad = (
            jnp.einsum("hqk,khd->qhd", score_grad, key_rows, preferred_element_type=jnp.float32)
            * factor
        )
        key_grad = (
            key_grad
            + jnp.einsum("hqk,qhd->khd", score_grad, queries, preferred_element_type=jnp.float32)
            * factor
        )
        value_grad = value_grad + jnp.einsum(
            "hqk,qhd->khd",
            weights.astype(jnp.bfloat16),
            grad_view,
            preferred_element_type=jnp.float32,
        )
        offset_sums = diagonal_sums(score_grad.astype(jnp.float32))
        current = vector_grad
        vector_grad = current + offset_sums
        return ((key_grad, value_grad, vector_grad), query_grad.reshape(span_rows, model_width))

    zero_heads = jnp.zeros((length, HEADS, head_size), jnp.float32)
    start_accum = (zero_heads, zero_heads, jnp.zeros(bias_vector.shape, jnp.float32))
    (key_grad, value_grad, vector_grad), query_grads = lax.scan(
        one_span, start_accum, jnp.arange(span_count, dtype=jnp.int32)
    )
    qkv_grad = jnp.concatenate(
        [
            query_grads.reshape(length, model_width),
            key_grad.reshape(length, model_width),
            value_grad.reshape(length, model_width),
        ],
        axis=1,
    )
    return (qkv_grad.astype(jnp.bfloat16), vector_grad)


def attention_layer(residual, gain, qkv_full, out_full, table, onehot, piece_first):
    normed = normalize(residual, gain).astype(jnp.bfloat16)
    qkv_rows = jnp.dot(normed, qkv_full, preferred_element_type=jnp.float32).astype(jnp.bfloat16)
    bias_vector = jnp.dot(table, onehot.T, precision=lax.Precision.HIGHEST)
    mixed_rows, log_totals = attend(qkv_rows, bias_vector, piece_first)
    result = residual + jnp.dot(mixed_rows, out_full, preferred_element_type=jnp.float32)
    return (result, (normed, qkv_rows, mixed_rows, log_totals, bias_vector))


def attention_back(residual, gain, qkv_full, out_full, onehot, piece_first, kept, grad):
    normed, qkv_rows, mixed_rows, log_totals, bias_vector = kept
    grad_low = grad.astype(jnp.bfloat16)
    out_grad = jnp.dot(mixed_rows.T, grad_low, preferred_element_type=jnp.float32)
    mixed_grad = jnp.dot(grad_low, out_full.T, preferred_element_type=jnp.float32).astype(
        jnp.bfloat16
    )
    qkv_grad, vector_grad = attend_back(qkv_rows, mixed_grad, log_totals, bias_vector, piece_first)
    qkv_weight_grad = jnp.dot(normed.T, qkv_grad, preferred_element_type=jnp.float32)
    normed_grad = jnp.dot(qkv_grad, qkv_full.T, preferred_element_type=jnp.float32)
    input_grad, gain_grad = normalize_back(residual, gain, normed_grad)
    table_grad = jnp.dot(vector_grad, onehot, precision=lax.Precision.HIGHEST)
    return (grad + input_grad, gain_grad, table_grad, qkv_weight_grad, out_grad)


def dense_layer(residual, gain, up_full, down_full):
    normed = normalize(residual, gain).astype(jnp.bfloat16)
    hidden_pre = jnp.dot(normed, up_full, preferred_element_type=jnp.float32)
    hidden = jax.nn.gelu(hidden_pre).astype(jnp.bfloat16)
    result = residual + jnp.dot(hidden, down_full, preferred_element_type=jnp.float32)
    return (result, (normed, hidden_pre, hidden))


def dense_back(residual, gain, up_full, down_full, kept, grad):
    normed, hidden_pre, hidden = kept
    grad_low = grad.astype(jnp.bfloat16)
    down_grad = jnp.dot(hidden.T, grad_low, preferred_element_type=jnp.float32)
    hidden_grad = jnp.dot(grad_low, down_full.T, preferred_element_type=jnp.float32)
    pre_grad = gelu_back(hidden_pre, hidden_grad).astype(jnp.bfloat16)
    up_grad = jnp.dot(normed.T, pre_grad, preferred_element_type=jnp.float32)
    normed_grad = jnp.dot(pre_grad, up_full.T, preferred_element_type=jnp.float32)
    input_grad, gain_grad = normalize_back(residual, gain, normed_grad)
    return (grad + input_grad, gain_grad, up_grad, down_grad)


def expert_slots(routes, experts_all, capacity):
    choice_ids = routes.reshape(-1)
    onehot_ids = (choice_ids[:, None] == jnp.arange(experts_all, dtype=jnp.int32)[None, :]).astype(
        jnp.int32
    )
    ranks = jnp.cumsum(onehot_ids, axis=0, dtype=jnp.int32) - 1
    return choice_ids * capacity + jnp.sum(ranks * onehot_ids, axis=1, dtype=jnp.int32)


def expert_layer(residual, gain, router_full, up_experts, down_experts, routes, slot_ids, capacity):
    model_width = residual.shape[1]
    experts_all = router_full.shape[1]
    normed = normalize(residual, gain).astype(jnp.bfloat16)
    logits = jnp.dot(normed, router_full, preferred_element_type=jnp.float32)
    gates = jax.nn.softmax(jnp.take_along_axis(logits, routes, axis=1), axis=1)
    pair_rows = jnp.repeat(normed, routes.shape[1], axis=0)
    outgoing = (
        jnp.zeros((experts_all * capacity, model_width), jnp.bfloat16).at[slot_ids].set(pair_rows)
    )
    arrived = lax.all_to_all(
        outgoing.reshape(experts_all, capacity, model_width),
        "expert",
        split_axis=0,
        concat_axis=1,
        tiled=True,
    )
    up_pre = jnp.einsum("erd,edf->erf", arrived, up_experts, preferred_element_type=jnp.float32)
    hidden = jax.nn.gelu(up_pre).astype(jnp.bfloat16)
    produced = jnp.einsum(
        "erf,efd->erd", hidden, down_experts, preferred_element_type=jnp.float32
    ).astype(jnp.bfloat16)
    returned = lax.all_to_all(produced, "expert", split_axis=1, concat_axis=0, tiled=True)
    picked = returned.reshape(experts_all * capacity, model_width)[slot_ids].astype(jnp.float32)
    picked = picked.reshape(residual.shape[0], routes.shape[1], model_width)
    result = residual + jnp.sum(gates[:, :, None] * picked, axis=1)
    return (result, (normed, gates, arrived, up_pre, hidden, picked))


def expert_back(
    residual,
    gain,
    router_full,
    up_experts,
    down_experts,
    routes,
    slot_ids,
    capacity,
    kept,
    grad_rows,
):
    normed, gates, arrived, up_pre, hidden, picked = kept
    model_width = residual.shape[1]
    experts_all = router_full.shape[1]
    pair_grad = (
        (gates[:, :, None] * grad_rows[:, None, :]).astype(jnp.bfloat16).reshape(-1, model_width)
    )
    gate_grad = jnp.sum(picked * grad_rows[:, None, :], axis=2)
    outgoing = (
        jnp.zeros((experts_all * capacity, model_width), jnp.bfloat16).at[slot_ids].set(pair_grad)
    )
    arrived_grad = lax.all_to_all(
        outgoing.reshape(experts_all, capacity, model_width),
        "expert",
        split_axis=0,
        concat_axis=1,
        tiled=True,
    )
    down_grad = jnp.einsum("erf,erd->efd", hidden, arrived_grad, preferred_element_type=jnp.float32)
    hidden_grad = jnp.einsum(
        "erd,efd->erf", arrived_grad, down_experts, preferred_element_type=jnp.float32
    )
    pre_grad = gelu_back(up_pre, hidden_grad).astype(jnp.bfloat16)
    up_grad = jnp.einsum("erd,erf->edf", arrived, pre_grad, preferred_element_type=jnp.float32)
    row_grad = jnp.einsum(
        "erf,edf->erd", pre_grad, up_experts, preferred_element_type=jnp.float32
    ).astype(jnp.bfloat16)
    returned = lax.all_to_all(row_grad, "expert", split_axis=1, concat_axis=0, tiled=True)
    token_grad = returned.reshape(experts_all * capacity, model_width)[slot_ids].astype(jnp.float32)
    token_grad = jnp.sum(
        token_grad.reshape(residual.shape[0], routes.shape[1], model_width), axis=1
    )
    choice_grad = gates * (gate_grad - jnp.sum(gates * gate_grad, axis=1, keepdims=True))
    expert_ids = jnp.arange(experts_all, dtype=jnp.int32)
    logit_grad = jnp.sum(
        jnp.where(routes[:, :, None] == expert_ids[None, None, :], choice_grad[:, :, None], 0.0),
        axis=1,
    )
    logit_grad = logit_grad.astype(jnp.bfloat16)
    router_grad = jnp.dot(normed.T, logit_grad, preferred_element_type=jnp.float32)
    normed_grad = token_grad + jnp.dot(
        logit_grad, router_full.T, preferred_element_type=jnp.float32
    )
    input_grad, gain_grad = normalize_back(residual, gain, normed_grad)
    return (grad_rows + input_grad, gain_grad, router_grad, up_grad, down_grad)


def gather_dense(qkv_weight, out_weight, mlp_up, mlp_down, router):
    qkv_part, out_part, up_part, down_part, router_part = (
        lax.all_gather(qkv_weight, "shard", axis=1, tiled=True),
        lax.all_gather(out_weight, "shard", axis=1, tiled=True),
        lax.all_gather(mlp_up, "shard", axis=0, tiled=True),
        lax.all_gather(mlp_down, "shard", axis=0, tiled=True),
        lax.all_gather(router, "shard", axis=0, tiled=True),
    )
    return (
        lax.all_gather(qkv_part, "expert", axis=2, tiled=True),
        lax.all_gather(out_part, "expert", axis=2, tiled=True),
        lax.all_gather(up_part, "expert", axis=1, tiled=True),
        lax.all_gather(down_part, "expert", axis=1, tiled=True),
        lax.all_gather(router_part, "expert", axis=1, tiled=True),
    )


def gather_experts(expert_up, expert_down):
    return (
        lax.all_gather(expert_up, "shard", axis=2, tiled=True),
        lax.all_gather(expert_down, "shard", axis=1, tiled=True),
    )


def per_device(
    tokens,
    piece_start,
    routes,
    norm_gains,
    bias_tables,
    qkv_weight,
    out_weight,
    mlp_up,
    mlp_down,
    router,
    expert_up,
    expert_down,
    cotangent,
):
    length = tokens.shape[0]
    piece_first = piece_start[0]
    onehot = bucket_onehot(length, bias_tables.shape[2])
    experts_all = expert_up.shape[0] * lax.axis_size("expert")
    capacity = 3 * routes.shape[1] * length // (2 * experts_all)
    slot_ids = expert_slots(routes, experts_all, capacity)
    dense_full = gather_dense(qkv_weight, out_weight, mlp_up, mlp_down, router)
    expert_full = gather_experts(expert_up, expert_down)
    residual_zero = tokens.astype(jnp.float32)
    residual_one, attend_one = attention_layer(
        residual_zero,
        norm_gains[0],
        dense_full[0][0],
        dense_full[1][0],
        bias_tables[0],
        onehot,
        piece_first,
    )
    residual_two, dense_kept = dense_layer(
        residual_one, norm_gains[1], dense_full[2], dense_full[3]
    )
    residual_three, attend_two = attention_layer(
        residual_two,
        norm_gains[2],
        dense_full[0][1],
        dense_full[1][1],
        bias_tables[1],
        onehot,
        piece_first,
    )
    final_rows, expert_kept = expert_layer(
        residual_three,
        norm_gains[3],
        dense_full[4],
        expert_full[0],
        expert_full[1],
        routes,
        slot_ids,
        capacity,
    )
    grad_final = cotangent.astype(jnp.float32)
    grad_three, gain_three, router_grad, up_grad_experts, down_grad_experts = expert_back(
        residual_three,
        norm_gains[3],
        dense_full[4],
        expert_full[0],
        expert_full[1],
        routes,
        slot_ids,
        capacity,
        expert_kept,
        grad_final,
    )
    grad_two, gain_two, table_one_grad, qkv_one_grad, out_one_grad = attention_back(
        residual_two,
        norm_gains[2],
        dense_full[0][1],
        dense_full[1][1],
        onehot,
        piece_first,
        attend_two,
        grad_three,
    )
    grad_one, gain_one, up_grad, down_grad = dense_back(
        residual_one, norm_gains[1], dense_full[2], dense_full[3], dense_kept, grad_two
    )
    grad_zero, gain_zero, table_zero_grad, qkv_zero_grad, out_zero_grad = attention_back(
        residual_zero,
        norm_gains[0],
        dense_full[0][0],
        dense_full[1][0],
        onehot,
        piece_first,
        attend_one,
        grad_one,
    )
    expert_sums = (
        lax.psum_scatter(
            up_grad_experts.astype(jnp.bfloat16), "shard", scatter_dimension=2, tiled=True
        ).astype(jnp.float32),
        lax.psum_scatter(
            down_grad_experts.astype(jnp.bfloat16), "shard", scatter_dimension=1, tiled=True
        ).astype(jnp.float32),
    )
    qkv_stack = jnp.stack([qkv_zero_grad, qkv_one_grad])
    out_stack = jnp.stack([out_zero_grad, out_one_grad])
    qkv_part, out_part, up_part, down_part, router_part = (
        lax.psum_scatter(
            qkv_stack.astype(jnp.bfloat16), "expert", scatter_dimension=2, tiled=True
        ).astype(jnp.float32),
        lax.psum_scatter(
            out_stack.astype(jnp.bfloat16), "expert", scatter_dimension=2, tiled=True
        ).astype(jnp.float32),
        lax.psum_scatter(
            up_grad.astype(jnp.bfloat16), "expert", scatter_dimension=1, tiled=True
        ).astype(jnp.float32),
        lax.psum_scatter(
            down_grad.astype(jnp.bfloat16), "expert", scatter_dimension=1, tiled=True
        ).astype(jnp.float32),
        lax.psum_scatter(
            router_grad.astype(jnp.bfloat16), "expert", scatter_dimension=1, tiled=True
        ).astype(jnp.float32),
    )
    row_sums = (
        lax.psum_scatter(
            qkv_part.astype(jnp.bfloat16), "shard", scatter_dimension=1, tiled=True
        ).astype(jnp.float32),
        lax.psum_scatter(
            out_part.astype(jnp.bfloat16), "shard", scatter_dimension=1, tiled=True
        ).astype(jnp.float32),
        lax.psum_scatter(
            up_part.astype(jnp.bfloat16), "shard", scatter_dimension=0, tiled=True
        ).astype(jnp.float32),
        lax.psum_scatter(
            down_part.astype(jnp.bfloat16), "shard", scatter_dimension=0, tiled=True
        ).astype(jnp.float32),
        lax.psum_scatter(
            router_part.astype(jnp.bfloat16), "shard", scatter_dimension=0, tiled=True
        ).astype(jnp.float32),
    )
    gain_stack = jnp.stack([gain_zero, gain_one, gain_two, gain_three])
    table_stack = jnp.stack([table_zero_grad, table_one_grad])
    small_sums = lax.psum((gain_stack, table_stack), ("expert", "shard"))
    return (
        final_rows.astype(jnp.bfloat16),
        grad_zero,
        small_sums[0],
        small_sums[1],
        row_sums[0],
        row_sums[1],
        row_sums[2],
        row_sums[3],
        row_sums[4],
        expert_sums[0],
        expert_sums[1],
    )


def solution(mesh):
    in_specs = (
        P(("expert", "shard"), None),
        P(("expert", "shard")),
        P(("expert", "shard"), None),
        P(),
        P(),
        P(None, "shard", "expert"),
        P(None, "shard", "expert"),
        P("shard", "expert"),
        P("shard", "expert"),
        P("shard", "expert"),
        P("expert", None, "shard"),
        P("expert", "shard", None),
        P(("expert", "shard"), None),
    )
    out_specs = (
        P(("expert", "shard"), None),
        P(("expert", "shard"), None),
        P(),
        P(),
        P(None, "shard", "expert"),
        P(None, "shard", "expert"),
        P("shard", "expert"),
        P("shard", "expert"),
        P("shard", "expert"),
        P("expert", None, "shard"),
        P("expert", "shard", None),
    )
    return jax.shard_map(
        per_device, mesh=mesh, in_specs=in_specs, out_specs=out_specs, check_vma=False
    )
```

profile of v0, /device:TPU:0, one launch (start us, length us, event | category | flops | bytes accessed | tf_op | source)
XLA Modules:
  0.0 1673.5 jit_solution(5135969538962950234)
XLA Ops:
  26.9 23.2 %all_gather.36 = bf16[2,768,288]{2,0,1:T(2,128)(2,1)S(1)} all-gather(bf16[2,192,288]{2,0,1:T(2,128)(2,1)S(1)} %copy.335), channel_id=1, replica_groups=mesh['expert'=8,'shard'=4] {'shard'}, dimensions={1}, use_global_device_ids=true | all-gather | bytes 1105920 | tf_op jit(solution)/shard_map/all_gather | solution.py:330
  53.1 17.0 %all_gather.40 = bf16[768,384]{1,0:T(8,128)(2,1)} all-gather(bf16[192,384]{1,0:T(8,128)(2,1)S(1)} %copy-done.68), channel_id=1, replica_groups=mesh['expert'=8,'shard'=4] {'shard'}, dimensions={0}, use_global_device_ids=true | all-gather | bytes 737280 | tf_op jit(solution)/shard_map/all_gather | solution.py:332
  113.4 39.7 %copy.414 = f32[2,8,512,1024]{3,1,2,0:T(8,128)} copy(f32[2,8,512,1024]{3,2,1,0:T(8,128)S(1)} %bitcast.224) | data formatting | bytes 67108864
  153.1 23.1 %slice.142 = f32[12,523776]{1,0:T(8,128)} slice(f32[12,524288]{1,0:T(8,128)} %bitcast.226), slice={[0:12], [0:523776]} | slice | bytes 50282496 | tf_op jit(solution)/shard_map/while/body/eval_jaxpr/slice | solution.py:73
  176.1 44.0 %reshape.422 = f32[12,512,1023]{2,1,0:T(8,128)} reshape(f32[12,523776]{1,0:T(8,128)} %slice.142) | data formatting | bytes 50282496 | tf_op jit(solution)/shard_map/while/body/eval_jaxpr/reshape | solution.py:73
  271.3 39.7 %copy.415 = f32[2,8,512,1024]{3,1,2,0:T(8,128)} copy(f32[2,8,512,1024]{3,2,1,0:T(8,128)S(1)} %bitcast.225) | data formatting | bytes 67108864
  311.0 22.6 %slice.149 = f32[12,523776]{1,0:T(8,128)} slice(f32[12,524288]{1,0:T(8,128)} %bitcast.227), slice={[0:12], [0:523776]} | slice | bytes 50282496 | tf_op jit(solution)/shard_map/while/body/eval_jaxpr/slice | solution.py:73
  333.6 42.0 %reshape.425 = f32[12,512,1023]{2,1,0:T(8,128)} reshape(f32[12,523776]{1,0:T(8,128)} %slice.149) | data formatting | bytes 50282496 | tf_op jit(solution)/shard_map/while/body/eval_jaxpr/reshape | solution.py:73
  622.4 27.9 %all-to-all-done = bf16[16,96,768]{2,1,0:T(8,128)(2,1)} async-done(((bf16[16,96,768]{2,1,0:T(8,128)(2,1)}), bf16[16,96,768]{2,1,0:T(8,128)(2,1)}, u32[]{:S(2)}, u32[]{:S(2)}) %all-to-all-start) | async-done | bytes 2359328 | tf_op jit(solution)/shard_map/all_to_all | solution.py:251
  667.8 27.4 %fusion.6 = (bf16[2,768,3072]{2,1,0:T(8,128)(2,1)}, f32[2,768,3072]{2,1,0:T(8,128)}) fusion(f32[2,768,3072]{2,1,0:T(8,128)} %fusion.104, bf16[2,768,768]{2,1,0:T(8,128)(2,1)} %bitcast.270, bf16[2,768,3072]{2,1,0:T(8,128)(2,1)} %all-gather.17.cloned.1.call-done), kind=kOutput, calls=%fused_computation.15 | convolution fusion | flops 7342129152 | bytes 58982400 | tf_op jit(solution)/shard_map/erd,edf->erf/dot_general | solution.py:258
  893.4 18.2 %copy.379 = bf16[2,768,2304]{1,0,2:T(2,128)(2,1)} copy(bf16[2,768,2304]{2,1,0:T(8,128)(2,1)} %pad_maximum_fusion) | data formatting | bytes 14155776 | tf_op jit(solution)/shard_map/stack | solution.py:451
  944.8 23.4 %all-reduce.8 = bf16[768,16]{0,1:T(8,128)(2,1)S(1)} all-reduce(bf16[768,16]{0,1:T(8,128)(2,1)S(1)} %convolution_convert_fusion.14), channel_id=10, replica_groups=mesh['expert'=8,'shard'=4] {'expert'}, use_global_device_ids=true, to_apply=%region_43.44.clone | all-reduce | flops 12288 | bytes 49152
  969.1 83.8 %all-reduce.13.cloned.1.call-done = (bf16[2,768,2304]{1,0,2:T(2,128)(2,1)}, bf16[2,768,768]{1,0,2:T(2,128)(2,1)}) async-done(((bf16[2,768,2304]{1,0,2:T(2,128)(2,1)}, bf16[2,768,768]{1,0,2:T(2,128)(2,1)}), (bf16[2,768,2304]{1,0,2:T(2,128)(2,1)}, bf16[2,768,768]{1,0,2:T(2,128)(2,1)})) %all-reduce.13.cloned.1.call-update) | async-done | bytes 9437200
  1054.1 29.7 %copy.398 = bf16[2,768,96]{0,2,1:T(8,128)(2,1)} copy(bf16[2,768,96]{1,0,2:T(2,128)(2,1)S(1)} %constant_dynamic-slice_fusion.1) | data formatting | bytes 589824
  1083.8 29.2 %reshape.496 = bf16[768,192]{1,0:T(8,128)(2,1)} reshape(bf16[768,96,2]{2,1,0:T(8,128)(2,1)} %bitcast.230) | data formatting | bytes 589824
  1115.5 42.9 %copy.396 = bf16[2,768,288]{0,2,1:T(8,128)(2,1)} copy(bf16[2,768,288]{1,0,2:T(2,128)(2,1)S(1)} %constant_dynamic-slice_fusion.2) | data formatting | bytes 1769472
  1158.3 82.7 %reshape.494 = bf16[768,576]{1,0:T(8,128)(2,1)} reshape(bf16[768,288,2]{2,1,0:T(8,128)(2,1)} %bitcast.223) | data formatting | bytes 1769472
  1259.2 16.8 %convolution_convert_fusion = bf16[2,3072,768]{2,1,0:T(8,128)(2,1)} fusion(bf16[2,768,768]{2,1,0:T(8,128)(2,1)S(1)} %bitcast.269, f32[2,768,3072]{2,1,0:T(8,128)} %get-tuple-element.258), kind=kOutput, calls=%fused_computation.36 | convolution fusion | flops 7294943232 | bytes 30670848 | tf_op jit(solution)/shard_map/erf,erd->efd/dot_general | solution.py:299
  1304.6 29.2 %copy.418 = bf16[2,8,512,1024]{3,1,2,0:T(8,128)(2,1)S(1)} copy(bf16[2,8,512,1024]{3,2,1,0:T(8,128)(2,1)S(1)} %bitcast.232) | data formatting | bytes 33554432
  1340.5 62.3 %reshape.444 = bf16[12,512,1025]{2,1,0:T(8,128)(2,1)} reshape(bf16[12,524800]{1,0:T(8,128)(2,1)} %pad.40) | data formatting | bytes 25190400 | tf_op jit(solution)/shard_map/while/body/eval_jaxpr/reshape | solution.py:82
  1410.1 29.2 %copy.417 = bf16[2,8,512,1024]{3,1,2,0:T(8,128)(2,1)S(1)} copy(bf16[2,8,512,1024]{3,2,1,0:T(8,128)(2,1)S(1)} %bitcast.234) | data formatting | bytes 33554432
  1446.1 69.9 %reshape.442 = bf16[12,512,1025]{2,1,0:T(8,128)(2,1)} reshape(bf16[12,524800]{1,0:T(8,128)(2,1)} %pad.38) | data formatting | bytes 25190400 | tf_op jit(solution)/shard_map/while/body/eval_jaxpr/reshape | solution.py:82
  1542.5 44.0 %all-reduce.9 = (f32[4,768]{1,0:T(4,128)}, f32[2,12,44]{2,1,0:T(8,128)S(1)}) all-reduce(f32[4,768]{1,0:T(4,128)S(1)} %pad_maximum_fusion.9, f32[2,12,44]{2,1,0:T(8,128)S(1)} %pad_maximum_fusion.8), channel_id=1, replica_groups=mesh['expert'=8,'shard'=4] {'expert','shard'}, use_global_device_ids=true, to_apply=%region_31.32 | all-reduce | flops 4128 | bytes 33024 | tf_op jit(solution)/shard_map/psum | solution.py:489
  1609.6 29.4 %reshape.495 = bf16[192,288,2]{2,1,0:T(8,128)(2,1)} reshape(bf16[192,576]{1,0:T(8,128)(2,1)} %reduce-scatter.28.cloned.1.call-done) | data formatting | bytes 442368
  (498 shorter events, 757.8 us)
Async XLA Ops:
  7.2 427.5 %all-gather.11.cloned.1.call-start = ((), (), s32[]{:S(2)}) async-start(), calls=%async_computation.14 | async-start | bytes 2654208 | tf_op jit(solution)/shard_map/all_gather | solution.py:338
  25.6 428.0 %all-gather.9.cloned.1.call-start = ((), (), s32[]{:S(2)}) async-start(), calls=%async_computation.13 | async-start | bytes 7962624 | tf_op jit(solution)/shard_map/all_gather | solution.py:337
  53.0 471.5 %all-gather.13.cloned.1.call-start = ((), (), s32[]{:S(2)}) async-start(), calls=%async_computation.15 | async-start | bytes 5308416 | tf_op jit(solution)/shard_map/all_gather | solution.py:339
  70.1 461.4 %all-gather.15.cloned.1.call-start = ((), (), s32[]{:S(2)}) async-start(), calls=%async_computation.16 | async-start | bytes 5308416 | tf_op jit(solution)/shard_map/all_gather | solution.py:340
  85.8 567.7 %all-gather.19.cloned.1.call-start = ((), (), s32[]{:S(2)}) async-start(), calls=%async_computation.18 | async-start | bytes 11796480 | tf_op jit(solution)/shard_map/all_gather | solution.py:348
  86.4 581.4 %all-gather.17.cloned.1.call-start = ((), (), s32[]{:S(2)}) async-start(), calls=%async_computation.17 | async-start | bytes 11796480 | tf_op jit(solution)/shard_map/all_gather | solution.py:347
  90.0 158.3 %copy-start.103 = (s32[1023]{0:T(1024)}, s32[1023]{0:T(1024)S(1)}, u32[]{:S(2)}) copy-start(s32[1023]{0:T(1024)S(1)} %select_add_fusion) | copy-start | bytes 12280
  247.1 237.6 %copy-start.92 = (f32[768]{0:T(1024)}, f32[768]{0:T(1024)S(1)}, u32[]{:S(2)}) copy-start(f32[768]{0:T(1024)S(1)} %get-tuple-element.231) | copy-start | bytes 9220
  247.2 277.4 %copy-start.64 = (f32[768]{0:T(1024)}, f32[768]{0:T(1024)S(1)}, u32[]{:S(2)}) copy-start(f32[768]{0:T(1024)S(1)} %get-tuple-element.230) | copy-start | bytes 9220
  247.4 237.3 %copy-start.97 = (f32[512]{0:T(512)}, f32[512]{0:T(512)S(1)}, u32[]{:S(2)}) copy-start(f32[512]{0:T(512)S(1)} %add_rsqrt_fusion.3) | copy-start | bytes 6148
  583.1 33.1 %all-to-all-start.2 = ((bf16[16,96,768]{2,1,0:T(8,128)(2,1)}), bf16[16,96,768]{2,1,0:T(8,128)(2,1)S(1)}, u32[]{:S(2)}, u32[]{:S(2)}) async-start(bf16[16,96,768]{2,1,0:T(8,128)(2,1)} %bitcast.253), calls=%async_computation.2 | async-start | bytes 4718592 | tf_op jit(solution)/shard_map/all_to_all | solution.py:292
  616.3 34.0 %all-to-all-start = ((bf16[16,96,768]{2,1,0:T(8,128)(2,1)}), bf16[16,96,768]{2,1,0:T(8,128)(2,1)}, u32[]{:S(2)}, u32[]{:S(2)}) async-start(bf16[16,96,768]{2,1,0:T(8,128)(2,1)} %bitcast.252), calls=%async_computation | async-start | bytes 4718592 | tf_op jit(solution)/shard_map/all_to_all | solution.py:251
  709.3 33.0 %all-to-all-start.3 = ((bf16[2,768,768]{2,0,1:T(2,128)(2,1)}), bf16[2,768,768]{2,0,1:T(2,128)(2,1)S(1)}, u32[]{:S(2)}, u32[]{:S(2)}) async-start(bf16[2,768,768]{2,0,1:T(2,128)(2,1)} %copy.365), calls=%async_computation.3 | async-start | bytes 4718592 | tf_op jit(solution)/shard_map/all_to_all | solution.py:308
  742.3 33.8 %all-to-all-start.1 = ((bf16[2,768,768]{2,0,1:T(2,128)(2,1)}), bf16[2,768,768]{2,0,1:T(2,128)(2,1)}, u32[]{:S(2)}, u32[]{:S(2)}) async-start(bf16[2,768,768]{2,0,1:T(2,128)(2,1)} %copy.361), calls=%async_computation.1 | async-start | bytes 4718592 | tf_op jit(solution)/shard_map/all_to_all | solution.py:263
  746.7 306.3 %all-reduce.13.cloned.1.call-start = ((), (), s32[]{:S(2)}) async-start(), calls=%async_computation.28 | async-start | bytes 18874368
  917.7 323.4 %reduce-scatter.32.cloned.1.call-start = ((), (), s32[]{:S(2)}) async-start(), calls=%async_computation.26 | async-start | bytes 5308416
  932.6 310.8 %reduce-scatter.20.cloned.1.call-start = ((), (), s32[]{:S(2)}) async-start(), calls=%async_computation.20 | async-start | bytes 5308416 | tf_op jit(solution)/shard_map/reduce_scatter | solution.py:463
  942.1 648.0 %reduce-scatter.34.cloned.1.call-start = ((), (), s32[]{:S(2)}) async-start(), calls=%async_computation.27 | async-start | bytes 245760
  969.1 622.5 %reduce-scatter.30.cloned.1.call-start = ((), (), s32[]{:S(2)}) async-start(), calls=%async_computation.25 | async-start | bytes 491520
  1113.0 496.6 %reduce-scatter.28.cloned.1.call-start = ((), (), s32[]{:S(2)}) async-start(), calls=%async_computation.24 | async-start | bytes 1228800
  1241.1 413.9 %reduce-scatter.18.cloned.1.call-start = ((), (), s32[]{:S(2)}) async-start(), calls=%async_computation.19 | async-start | bytes 737280 | tf_op jit(solution)/shard_map/reduce_scatter | solution.py:477
  1243.3 413.3 %reduce-scatter.22.cloned.1.call-start = ((), (), s32[]{:S(2)}) async-start(), calls=%async_computation.21 | async-start | bytes 737280 | tf_op jit(solution)/shard_map/reduce_scatter | solution.py:480
  1243.9 414.4 %reduce-scatter.24.cloned.1.call-start = ((), (), s32[]{:S(2)}) async-start(), calls=%async_computation.22 | async-start | bytes 11796480 | tf_op jit(solution)/shard_map/reduce_scatter | solution.py:444
  1257.6 404.9 %reduce-scatter.26.cloned.1.call-start = ((), (), s32[]{:S(2)}) async-start(), calls=%async_computation.23 | async-start | bytes 11796480 | tf_op jit(solution)/shard_map/reduce_scatter | solution.py:447
  (121 other events, 1458.3 us)
Sparse Core Ops, SparseCore 0:
  25.7 30.7 all-gather.10
  58.9 48.8 all-gather.8
  109.7 39.7 all-gather.12
  151.2 38.9 all-gather.14
  191.6 166.7 all-gather.18
  359.8 165.0 all-gather.16
  917.8 135.0 all-reduce.12
  1057.4 53.9 reduce-scatter.31
  1115.4 53.8 reduce-scatter.19
  1172.1 19.3 reduce-scatter.33
  1194.3 18.8 reduce-scatter.29
  1241.2 26.1 reduce-scatter.27
  1270.2 20.4 reduce-scatter.17
  1292.9 20.3 reduce-scatter.21
  1315.5 159.5 reduce-scatter.23
  1477.3 163.1 reduce-scatter.25
where the time goes:
time: 1690 us; the launch traced here: 1670 us
  local copies, waits for them, and re-layouts  998 us (59%)
  matrix products  230 us (14%)
  blocking collectives  161 us (10%)
  waiting for transfers between devices  150 us (9%)
  other arithmetic  99.5 us (6%)
  between operations  18.5 us (1%)
  starting transfers between devices  17.4 us (1%)
    unnamed x290, local copies, waits for them, and re-layouts  536 us
    reshape x2, local copies, waits for them, and re-layouts, diagonal_sums(): skewed = flat.reshape(heads_count, row_count, length + row_count + 1)  132 us
    reshape x2, local copies, waits for them, and re-layouts, block_bias(): tiled[:, :row_count * (width - 1)]  86.1 us
    unnamed x21, waiting for transfers between devices  85.6 us
    slice x2, local copies, waits for them, and re-layouts, block_bias(): tiled[:, :row_count * (width - 1)]  45.7 us
    psum x1, blocking collectives, per_device(): small_sums = lax.psum((gain_stack, table_stack), ('expert', 'shard'))  44 us
  transfers between devices with their start and end apart: 20, of which 5 were waited for; matrix products, arithmetic and copies ran while one was open for 67% of the time, Pallas kernels for 0%

commit v1 on v0

v1 whole, which is shorter than its diff:
```python
import jax
import jax.numpy as jnp
from jax import lax
from jax.experimental import pallas as pl
from jax.experimental.pallas import tpu as pltpu
from jax.sharding import PartitionSpec as P

PIECE = 256
norm_eps = 1e-06
far_below = -1e30
BF = jnp.bfloat16
F32 = jnp.float32
VMEM_BYTES = 56 * 1024 * 1024


def nn(a, b):
    return lax.dot_general(a, b, (((1,), (0,)), ((), ())), preferred_element_type=F32)


def nt(a, b):
    return lax.dot_general(a, b, (((1,), (1,)), ((), ())), preferred_element_type=F32)


def tn(a, b):
    return lax.dot_general(a, b, (((0,), (0,)), ((), ())), preferred_element_type=F32)


def inverse_rms(field):
    return lax.rsqrt(jnp.mean(field * field, axis=1, keepdims=True) + norm_eps)


def gelu_parts(u):
    cubic = 0.7978845608028654 * (u + 0.044715 * (u * u * u))
    bend = jnp.tanh(cubic)
    half = 0.5 * (1.0 + bend)
    slope = half + 0.5 * u * (1.0 - bend * bend) * (0.7978845608028654 * (1.0 + 0.134145 * (u * u)))
    return u * half, slope


def gelu_of(u):
    return 0.5 * u * (1.0 + jnp.tanh(0.7978845608028654 * (u + 0.044715 * (u * u * u))))


def fill_mask(piece_ref, mask_ref):
    length = mask_ref.shape[0]
    first = piece_ref[0]
    key_pos = lax.broadcasted_iota(jnp.int32, (length, length), 0)
    query_pos = lax.broadcasted_iota(jnp.int32, (length, length), 1)
    key_in = (key_pos >= first) & (key_pos < first + PIECE)
    query_in = (query_pos >= first) & (query_pos < first + PIECE)
    keep = (key_pos <= query_pos) | (key_in & query_in)
    mask_ref[...] = jnp.where(keep, 0.0, far_below)


def bias_strip(vector_row, strip_ref):
    wide = jnp.broadcast_to(vector_row, (128, vector_row.shape[1]))
    strip_ref[...] = pltpu.roll(wide, vector_row.shape[1] - 127, 1, stride=1, stride_axis=0)


def attend_kernel(
    piece_ref, x_ref, gain_ref, w_ref, wo_ref, vec_ref,
    out_ref, normed_ref, qkv_ref, mixed_ref, lse_ref,
    mask_ref, strip_ref, score_ref, prob_ref,
):
    length, width = x_ref.shape
    tiles = length // 128
    fill_mask(piece_ref, mask_ref)
    field = x_ref[...]
    normed_ref[...] = (field * inverse_rms(field) * gain_ref[...]).astype(BF)

    def project(c, _):
        cols = pl.ds(pl.multiple_of(c * 256, 256), 256)
        qkv_ref[:, cols] = nt(normed_ref[...], w_ref[cols, :]).astype(BF)
        return 0

    lax.fori_loop(0, 3 * width // 256, project, 0)
    lane_low = lax.broadcasted_iota(jnp.int32, (length, 128), 1) < 64
    row_low = lax.broadcasted_iota(jnp.int32, (128, length), 0) < 64

    def pair(hp, _):
        base = hp * 128
        q2 = qkv_ref[:, pl.ds(pl.multiple_of(base, 128), 128)] * jnp.asarray(0.125, BF)
        v2 = qkv_ref[:, pl.ds(pl.multiple_of(2 * width + base, 128), 128)]
        mixed = []
        for half in range(2):
            head = hp * 2 + half
            keep = lane_low if half == 0 else ~lane_low
            qm = jnp.where(keep, q2, jnp.zeros_like(q2))
            bias_strip(vec_ref[pl.ds(head, 1), :], strip_ref)
            peak = jnp.full((1, length), far_below, F32)
            for jt in range(tiles):
                rows = slice(jt * 128, jt * 128 + 128)
                k2 = qkv_ref[rows, pl.ds(pl.multiple_of(width + base, 128), 128)]
                at = 128 * (tiles - 1 - jt)
                s = nt(k2, qm) + strip_ref[:, at:at + length] + mask_ref[rows, :]
                score_ref[rows, :] = s
                peak = jnp.maximum(peak, jnp.max(s, axis=0, keepdims=True))
            total = jnp.zeros((1, length), F32)
            for jt in range(tiles):
                rows = slice(jt * 128, jt * 128 + 128)
                e = jnp.exp(score_ref[rows, :] - peak)
                total = total + jnp.sum(e, axis=0, keepdims=True)
                prob_ref[rows, :] = e.astype(BF)
            lse_ref[pl.ds(head, 1), :] = peak + jnp.log(total)
            mixed.append(tn(v2, prob_ref[...]) * (1.0 / total))
        both = jnp.where(row_low, mixed[0], mixed[1]).astype(BF)
        mixed_ref[:, pl.ds(pl.multiple_of(base, 128), 128)] = both.T
        return 0

    lax.fori_loop(0, width // 128, pair, 0)

    def back(c, _):
        cols = pl.ds(pl.multiple_of(c * 256, 256), 256)
        out_ref[:, cols] = x_ref[:, cols] + nt(mixed_ref[...], wo_ref[cols, :])
        return 0

    lax.fori_loop(0, width // 256, back, 0)


SMEM_SPEC = pl.BlockSpec(memory_space=pltpu.SMEM)
VMEM_SPEC = pl.BlockSpec(memory_space=pltpu.VMEM)


def attend(piece, x, gain, w, wo, vectors):
    length, width = x.shape
    heads = vectors.shape[0]
    span = vectors.shape[1]
    return pl.pallas_call(
        attend_kernel,
        out_shape=(
            jax.ShapeDtypeStruct((length, width), F32),
            jax.ShapeDtypeStruct((length, width), BF),
            jax.ShapeDtypeStruct((length, 3 * width), BF),
            jax.ShapeDtypeStruct((length, width), BF),
            jax.ShapeDtypeStruct((heads, length), F32),
        ),
        in_specs=[SMEM_SPEC] + [VMEM_SPEC] * 5,
        out_specs=[VMEM_SPEC] * 5,
        scratch_shapes=[
            pltpu.VMEM((length, length), F32),
            pltpu.VMEM((128, span), F32),
            pltpu.VMEM((length, length), F32),
            pltpu.VMEM((length, length), BF),
        ],
        compiler_params=pltpu.CompilerParams(vmem_limit_bytes=VMEM_BYTES),
        cost_estimate=pl.CostEstimate(
            flops=8 * length * width * width + 4 * length * length * width,
            bytes_accessed=20 * length * width + 8 * width * width,
            transcendentals=heads * length * length,
        ),
        name="attend",
    )(piece, x, gain, w, wo, vectors)


def attend_back_kernel(
    piece_ref, x_ref, gain_ref, w_ref, wo_ref, vec_ref, normed_ref, qkv_ref, mixed_ref, lse_ref, grad_ref,
    dx_ref, dw_ref, dwo_ref, dvec_ref, dgain_ref,
    mask_ref, strip_ref, sums_ref, prob_ref, ds_ref, low_ref, do_ref, dqkv_ref, delta_ref,
):
    length, width = x_ref.shape
    heads = vec_ref.shape[0]
    tiles = length // 128
    fill_mask(piece_ref, mask_ref)
    low_ref[...] = grad_ref[...].astype(BF)

    def out_back(c, _):
        cols = pl.ds(pl.multiple_of(c * 256, 256), 256)
        do_ref[:, cols] = nn(low_ref[...], wo_ref[:, cols]).astype(BF)
        dwo_ref[cols, :] = tn(low_ref[:, cols], mixed_ref[...]).astype(BF)
        return 0

    lax.fori_loop(0, width // 256, out_back, 0)
    pick = (
        lax.broadcasted_iota(jnp.int32, (delta_ref.shape[0], width), 1) // (width // heads)
        == lax.broadcasted_iota(jnp.int32, (delta_ref.shape[0], width), 0)
    ).astype(F32)
    delta_ref[...] = lax.dot_general(
        pick, do_ref[...].astype(F32) * mixed_ref[...].astype(F32), (((1,), (1,)), ((), ())),
        precision=lax.Precision.HIGHEST, preferred_element_type=F32,
    )
    lane_low = lax.broadcasted_iota(jnp.int32, (length, 128), 1) < 64
    lane_low_tile = lax.broadcasted_iota(jnp.int32, (128, 128), 1) < 64
    row_low = lax.broadcasted_iota(jnp.int32, (128, length), 0) < 64
    flip = (
        lax.broadcasted_iota(jnp.int32, (128, 128), 0) + lax.broadcasted_iota(jnp.int32, (128, 128), 1) == 127
    ).astype(F32)
    sums_ref[...] = jnp.zeros_like(sums_ref)

    def pair(hp, _):
        base = hp * 128
        q_cols = pl.ds(pl.multiple_of(base, 128), 128)
        k_cols = pl.ds(pl.multiple_of(width + base, 128), 128)
        v_cols = pl.ds(pl.multiple_of(2 * width + base, 128), 128)
        q2 = qkv_ref[:, q_cols] * jnp.asarray(0.125, BF)
        do2 = do_ref[:, q_cols]
        parts = []
        for half in range(2):
            head = hp * 2 + half
            keep = lane_low if half == 0 else ~lane_low
            qm = jnp.where(keep, q2, jnp.zeros_like(q2))
            dm = jnp.where(keep, do2, jnp.zeros_like(do2))
            bias_strip(vec_ref[pl.ds(head, 1), :], strip_ref)
            lse = lse_ref[pl.ds(head, 1), :]
            delta = delta_ref[pl.ds(head, 1), :]
            for jt in range(tiles):
                rows = slice(jt * 128, jt * 128 + 128)
                at = 128 * (tiles - 1 - jt)
                s = nt(qkv_ref[rows, k_cols], qm) + strip_ref[:, at:at + length] + mask_ref[rows, :]
                p = jnp.exp(s - lse)
                dp = nt(qkv_ref[rows, v_cols], dm)
                ds = (p * (dp - delta)).astype(BF)
                prob_ref[half, rows, :] = p.astype(BF)
                ds_ref[half, rows, :] = ds
                if jt == 0:
                    sums_ref[:, at:at + length] = ds.astype(F32)
                    sums_ref[:, 0:at] = jnp.zeros((128, at), F32)
                else:
                    sums_ref[:, at:at + length] += ds.astype(F32)
            turned = lax.dot_general(
                flip, sums_ref[...], (((1,), (0,)), ((), ())),
                precision=lax.Precision.HIGHEST, preferred_element_type=F32,
            )
            turned = pltpu.roll(turned, 0, 1, stride=1, stride_axis=0)
            dvec_ref[pl.ds(head, 1), :] = jnp.sum(turned, axis=0, keepdims=True)
            parts.append(tn(qkv_ref[:, k_cols], ds_ref[half]) * 0.125)
        both = jnp.where(row_low, parts[0], parts[1]).astype(BF)
        dqkv_ref[:, q_cols] = both.T
        for jt in range(tiles):
            rows = slice(jt * 128, jt * 128 + 128)
            dk = jnp.where(lane_low_tile, nn(ds_ref[0, rows, :], q2), nn(ds_ref[1, rows, :], q2))
            dqkv_ref[rows, k_cols] = dk.astype(BF)
            dv = jnp.where(lane_low_tile, nn(prob_ref[0, rows, :], do2), nn(prob_ref[1, rows, :], do2))
            dqkv_ref[rows, v_cols] = dv.astype(BF)
        return 0

    lax.fori_loop(0, width // 128, pair, 0)

    def weights_back(c, _):
        cols = pl.ds(pl.multiple_of(c * 256, 256), 256)
        dw_ref[cols, :] = tn(dqkv_ref[:, cols], normed_ref[...]).astype(BF)
        return 0

    lax.fori_loop(0, 3 * width // 256, weights_back, 0)

    def rows_back(c, _):
        cols = pl.ds(pl.multiple_of(c * 256, 256), 256)
        dx_ref[:, cols] = nn(dqkv_ref[...], w_ref[:, cols])
        return 0

    lax.fori_loop(0, width // 256, rows_back, 0)
    norm_back(x_ref, gain_ref, dx_ref, grad_ref, dx_ref, dgain_ref)


def norm_back(x_ref, gain_ref, upper_ref, base_ref, dx_ref, dgain_ref):
    field = x_ref[...]
    inverse = inverse_rms(field)
    unit = field * inverse
    upper = upper_ref[...]
    scaled = upper * gain_ref[...]
    dgain_ref[...] = jnp.sum(upper * unit, axis=0, keepdims=True)
    dx_ref[...] = base_ref[...] + inverse * (scaled - unit * jnp.mean(scaled * unit, axis=1, keepdims=True))


def attend_back(piece, x, gain, w, wo, vectors, normed, qkv, mixed, lse, grad):
    length, width = x.shape
    heads, span = vectors.shape
    return pl.pallas_call(
        attend_back_kernel,
        out_shape=(
            jax.ShapeDtypeStruct((length, width), F32),
            jax.ShapeDtypeStruct((3 * width, width), BF),
            jax.ShapeDtypeStruct((width, width), BF),
            jax.ShapeDtypeStruct((heads, span), F32),
            jax.ShapeDtypeStruct((1, width), F32),
        ),
        in_specs=[SMEM_SPEC] + [VMEM_SPEC] * 10,
        out_specs=[VMEM_SPEC] * 5,
        scratch_shapes=[
            pltpu.VMEM((length, length), F32),
            pltpu.VMEM((128, span), F32),
            pltpu.VMEM((128, span), F32),
            pltpu.VMEM((2, length, length), BF),
            pltpu.VMEM((2, length, length), BF),
            pltpu.VMEM((length, width), BF),
            pltpu.VMEM((length, width), BF),
            pltpu.VMEM((length, 3 * width), BF),
            pltpu.VMEM((16, length), F32),
        ],
        compiler_params=pltpu.CompilerParams(vmem_limit_bytes=VMEM_BYTES),
        cost_estimate=pl.CostEstimate(
            flops=16 * length * width * width + 10 * length * length * width,
            bytes_accessed=40 * length * width + 16 * width * width,
            transcendentals=heads * length * length,
        ),
        name="attend_back",
    )(piece, x, gain, w, wo, vectors, normed, qkv, mixed, lse, grad)


def mlp_kernel(x_ref, gain_ref, up_ref, down_ref, out_ref, normed_ref):
    field = x_ref[...]
    normed_ref[...] = (field * inverse_rms(field) * gain_ref[...]).astype(BF)
    out_ref[...] = field

    def chunk(c, _):
        at = pl.ds(pl.multiple_of(c * 512, 512), 512)
        hidden = gelu_of(nt(normed_ref[...], up_ref[at, :])).astype(BF)
        out_ref[...] += nt(hidden, down_ref[:, at])
        return 0

    lax.fori_loop(0, up_ref.shape[0] // 512, chunk, 0)


def mlp(x, gain, up, down):
    length, width = x.shape
    hidden = up.shape[0]
    return pl.pallas_call(
        mlp_kernel,
        out_shape=(jax.ShapeDtypeStruct((length, width), F32), jax.ShapeDtypeStruct((length, width), BF)),
        in_specs=[VMEM_SPEC] * 4,
        out_specs=[VMEM_SPEC] * 2,
        compiler_params=pltpu.CompilerParams(vmem_limit_bytes=VMEM_BYTES),
        cost_estimate=pl.CostEstimate(
            flops=4 * length * width * hidden, bytes_accessed=10 * length * width + 4 * width * hidden,
            transcendentals=length * hidden,
        ),
        name="mlp",
    )(x, gain, up, down)


def mlp_back_kernel(x_ref, gain_ref, up_ref, down_ref, normed_ref, grad_ref,
                    dx_ref, dup_ref, ddown_ref, dgain_ref, low_ref, acc_ref):
    low_ref[...] = grad_ref[...].astype(BF)
    acc_ref[...] = jnp.zeros_like(acc_ref)

    def chunk(c, _):
        at = pl.ds(pl.multiple_of(c * 512, 512), 512)
        hidden, slope = gelu_parts(nt(normed_ref[...], up_ref[at, :]))
        pre_grad = (nn(low_ref[...], down_ref[:, at]) * slope).astype(BF)
        ddown_ref[:, at] = tn(low_ref[...], hidden.astype(BF)).astype(BF)
        dup_ref[at, :] = tn(pre_grad, normed_ref[...]).astype(BF)
        acc_ref[...] += nn(pre_grad, up_ref[at, :])
        return 0

    lax.fori_loop(0, up_ref.shape[0] // 512, chunk, 0)
    norm_back(x_ref, gain_ref, acc_ref, grad_ref, dx_ref, dgain_ref)


def mlp_back(x, gain, up, down, normed, grad):
    length, width = x.shape
    hidden = up.shape[0]
    return pl.pallas_call(
        mlp_back_kernel,
        out_shape=(
            jax.ShapeDtypeStruct((length, width), F32),
            jax.ShapeDtypeStruct((hidden, width), BF),
            jax.ShapeDtypeStruct((width, hidden), BF),
            jax.ShapeDtypeStruct((1, width), F32),
        ),
        in_specs=[VMEM_SPEC] * 6,
        out_specs=[VMEM_SPEC] * 4,
        scratch_shapes=[pltpu.VMEM((length, width), BF), pltpu.VMEM((length, width), F32)],
        compiler_params=pltpu.CompilerParams(vmem_limit_bytes=VMEM_BYTES),
        cost_estimate=pl.CostEstimate(
            flops=10 * length * width * hidden, bytes_accessed=16 * length * width + 8 * width * hidden,
            transcendentals=length * hidden,
        ),
        name="mlp_back",
    )(x, gain, up, down, normed, grad)


def experts_kernel(
    x_ref, c_ref, gate_ref, up_ref, down_ref,
    y_ref, dx_ref, dgate_ref, own_up_ref, own_down_ref, peer_up_ref, peer_down_ref,
    y_sum, dx_sum, dgate_sum, up_sum, down_sum,
):
    part = pl.program_id(1)
    sources, _, span, width = x_ref.shape
    group = max(1, 384 // span)
    rows = group * span
    up_sum[...] = jnp.zeros_like(up_sum)
    down_sum[...] = jnp.zeros_like(down_sum)

    @pl.when(part == 0)
    def _():
        y_sum[...] = jnp.zeros_like(y_sum)
        dx_sum[...] = jnp.zeros_like(dx_sum)
        dgate_sum[...] = jnp.zeros_like(dgate_sum)

    def tile(i, _):
        at = pl.ds(i * group, group)
        x = x_ref[at, 0].reshape(rows, width)
        c = c_ref[at, 0].reshape(rows, width)
        gate = gate_ref[at, 0].reshape(rows, 1)
        hidden, slope = gelu_parts(nn(x, up_ref[...]))
        hidden = hidden.astype(BF)
        back = nt(c, down_ref[...])
        pre_grad = (gate * back * slope).astype(BF)
        dgate_sum[at] += jnp.sum(hidden.astype(F32) * back, axis=1, keepdims=True).reshape(group, span, 1)
        y_sum[at] += nn(hidden, down_ref[...]).reshape(group, span, width)
        dx_sum[at] += nt(pre_grad, up_ref[...]).reshape(group, span, width)
        up_sum[...] += tn(x, pre_grad)
        down_sum[...] += tn(hidden, (gate * c.astype(F32)).astype(BF))
        return 0

    lax.fori_loop(0, sources // group, tile, 0)

    @pl.when(part == 0)
    def _():
        own_up_ref[...] = up_sum[...]
        own_down_ref[...] = down_sum[...]

    @pl.when(part == 1)
    def _():
        peer_up_ref[...] = up_sum[...].astype(BF)
        peer_down_ref[...] = down_sum[...].astype(BF)
        y_ref[:, 0] = (gate_ref[:, 0] * y_sum[...]).astype(BF)
        dx_ref[:, 0] = dx_sum[...].astype(BF)
        dgate_ref[:, 0] = dgate_sum[...]


def run_experts(x, c, gate, up, down):
    sources, local, span, width = x.shape
    hidden = up.shape[3]
    lean = sources * span > 2048
    once = dict(pipeline_mode=pl.Buffered(1)) if lean else {}
    row_spec = pl.BlockSpec((sources, 1, span, width), lambda e, j: (0, e, 0, 0), **once)
    row_out_spec = pl.BlockSpec((sources, 1, span, width), lambda e, j: (0, e, 0, 0), pipeline_mode=pl.Buffered(1))
    gate_spec = pl.BlockSpec((sources, 1, span, 1), lambda e, j: (0, e, 0, 0), **once)
    sq = pl.Squeezed()
    up_spec = pl.BlockSpec((sq, sq, width, hidden), lambda e, j: (j, e, 0, 0))
    down_spec = pl.BlockSpec((sq, sq, hidden, width), lambda e, j: (j, e, 0, 0))
    gup_spec = pl.BlockSpec((sq, width, hidden), lambda e, j: (e, 0, 0))
    gdown_spec = pl.BlockSpec((sq, hidden, width), lambda e, j: (e, 0, 0))
    rows = local * sources * span
    return pl.pallas_call(
        experts_kernel,
        grid=(local, 2),
        out_shape=(
            jax.ShapeDtypeStruct(x.shape, BF),
            jax.ShapeDtypeStruct(x.shape, BF),
            jax.ShapeDtypeStruct(gate.shape, F32),
            jax.ShapeDtypeStruct((local, width, hidden), F32),
            jax.ShapeDtypeStruct((local, hidden, width), F32),
            jax.ShapeDtypeStruct((local, width, hidden), BF),
            jax.ShapeDtypeStruct((local, hidden, width), BF),
        ),
        in_specs=[row_spec, row_spec, gate_spec, up_spec, down_spec],
        out_specs=[row_out_spec, row_out_spec, gate_spec, gup_spec, gdown_spec, gup_spec, gdown_spec],
        scratch_shapes=[
            pltpu.VMEM((sources, span, width), F32),
            pltpu.VMEM((sources, span, width), F32),
            pltpu.VMEM((sources, span, 1), F32),
            pltpu.VMEM((width, hidden), F32),
            pltpu.VMEM((hidden, width), F32),
        ],
        compiler_params=pltpu.CompilerParams(vmem_limit_bytes=VMEM_BYTES),
        cost_estimate=pl.CostEstimate(
            flops=24 * rows * width * hidden, bytes_accessed=16 * rows * width, transcendentals=2 * rows * hidden,
        ),
        name="experts",
    )(x, c, gate, up, down)


def spread_kernel(slot_ref, rows_ref, out_ref):
    experts, zones, capacity, width = out_ref.shape
    length = rows_ref.shape[1]
    take = max(1, 384 // capacity)

    def chunk(i, _):
        for zone in range(zones):
            place = lax.broadcasted_iota(jnp.int32, (take * capacity, length), 0) + i * (take * capacity)
            hit = (place == slot_ref[zone, 0:1, :]) | (place == slot_ref[zone, 1:2, :])
            picked = nn(jnp.where(hit, 1.0, 0.0).astype(BF), rows_ref[zone])
            out_ref[pl.ds(i * take, take), zone] = picked.reshape(take, capacity, width).astype(BF)
        return 0

    lax.fori_loop(0, experts // take, chunk, 0)


def spread(slot_rows, rows, experts, capacity):
    zones, length, width = rows.shape
    return pl.pallas_call(
        spread_kernel,
        out_shape=jax.ShapeDtypeStruct((experts, zones, capacity, width), BF),
        in_specs=[VMEM_SPEC] * 2,
        out_specs=VMEM_SPEC,
        compiler_params=pltpu.CompilerParams(vmem_limit_bytes=VMEM_BYTES),
        cost_estimate=pl.CostEstimate(
            flops=2 * zones * experts * capacity * length * width,
            bytes_accessed=2 * zones * (experts * capacity + length) * width, transcendentals=0,
        ),
        name="spread",
    )(slot_rows, rows)


def collect_kernel(slot_ref, rows_ref, out_ref):
    experts, zones, capacity, width = rows_ref.shape
    length = out_ref.shape[1]
    take = max(1, 384 // capacity)
    out_ref[...] = jnp.zeros_like(out_ref)

    def chunk(i, _):
        for zone in range(zones):
            place = lax.broadcasted_iota(jnp.int32, (length, take * capacity), 1) + i * (take * capacity)
            hit = (place == slot_ref[:, 2 * zone:2 * zone + 1]) | (place == slot_ref[:, 2 * zone + 1:2 * zone + 2])
            rows = rows_ref[pl.ds(i * take, take), zone].reshape(take * capacity, width)
            out_ref[zone] += nn(jnp.where(hit, 1.0, 0.0).astype(BF), rows)
        return 0

    lax.fori_loop(0, experts // take, chunk, 0)


def collect(slot_columns, rows):
    experts, zones, capacity, width = rows.shape
    length = slot_columns.shape[0]
    return pl.pallas_call(
        collect_kernel,
        out_shape=jax.ShapeDtypeStruct((zones, length, width), F32),
        in_specs=[VMEM_SPEC] * 2,
        out_specs=VMEM_SPEC,
        compiler_params=pltpu.CompilerParams(vmem_limit_bytes=VMEM_BYTES),
        cost_estimate=pl.CostEstimate(
            flops=2 * zones * experts * capacity * length * width,
            bytes_accessed=2 * zones * (experts * capacity + 2 * length) * width, transcendentals=0,
        ),
        name="collect",
    )(slot_columns, rows)


bucket_edges = (1, 2, 3, 4, 6, 8, 12, 16, 24, 32, 48, 64, 96, 128, 192, 256, 384, 512, 768, 1024, 1536)


def bucket_onehot(length, buckets):
    distance = (length - 1) - jnp.arange(2 * length, dtype=jnp.int32)
    edge_list = jnp.array(bucket_edges, dtype=jnp.int32)
    magnitude = jnp.sum(
        (jnp.abs(distance)[:, None] >= edge_list[None, :]).astype(jnp.int32), axis=1, dtype=jnp.int32
    )
    bucket = magnitude + buckets // 2 * (distance > 0).astype(jnp.int32)
    real = jnp.arange(2 * length)[:, None] < 2 * length - 1
    hit = (bucket[:, None] == jnp.arange(buckets, dtype=jnp.int32)[None, :]) & real
    return hit.astype(F32)


def expert_slots(routes, experts_all, capacity):
    pairs = routes.reshape(-1)
    onehot = pairs[:, None] == jnp.arange(experts_all, dtype=jnp.int32)[None, :]
    count = pairs.shape[0]
    before = jnp.arange(count)[:, None] > jnp.arange(count)[None, :]
    ranks = jnp.dot(before.astype(BF), onehot.astype(BF), preferred_element_type=F32)
    own = jnp.sum(jnp.where(onehot, ranks, 0.0), axis=1).astype(jnp.int32)
    return (pairs * capacity + own).reshape(routes.shape)


def shift_from(value, distance):
    size = lax.axis_size("shard")
    return lax.ppermute(value, "shard", [((z + distance) % size, z) for z in range(size)])


def shift_to(value, distance):
    size = lax.axis_size("shard")
    return lax.ppermute(value, "shard", [(z, (z + distance) % size) for z in range(size)])


def swap_pair(value):
    return lax.ppermute(value, "shard", [(z, z ^ 1) for z in range(lax.axis_size("shard"))])


def total_over_mesh(value):
    for name in ("shard", "expert"):
        size = lax.axis_size(name)
        step = 1
        while step < size:
            value = value + lax.ppermute(value, name, [(i, i ^ step) for i in range(size)])
            step *= 2
    return value


def exchange(value):
    return lax.all_to_all(value, "expert", split_axis=0, concat_axis=0, tiled=True)


def gather_rows(value, name):
    return lax.all_gather(value, name, axis=0, tiled=True)


def scatter_rows(value, name):
    return lax.psum_scatter(value, name, scatter_dimension=0, tiled=True)


def per_device(
    tokens, piece_start, routes, norm_gains, bias_tables, qkv_weight, out_weight, mlp_up, mlp_down, router,
    expert_up, expert_down, cotangent,
):
    length, width = tokens.shape
    owners = lax.axis_size("expert")
    zones = lax.axis_size("shard") // 2
    local = expert_up.shape[0]
    experts_all = local * owners
    capacity = 3 * routes.shape[1] * length // (2 * experts_all)
    qkv_cols, out_cols = qkv_weight.shape[2], out_weight.shape[2]
    router_pad = 16

    def router_block(part):
        return jnp.pad(part, ((0, 0), (0, router_pad - part.shape[1])))

    first = gather_rows(jnp.concatenate([qkv_weight[0], out_weight[0]], axis=1), "shard").T
    middle = gather_rows(mlp_up, "shard").T
    lower = gather_rows(mlp_down, "shard").T
    last = gather_rows(
        jnp.concatenate([qkv_weight[1], out_weight[1], router_block(router)], axis=1), "shard"
    ).T
    first = gather_rows(first, "expert").reshape(owners, qkv_cols + out_cols, width)
    up_full = gather_rows(middle, "expert")
    down_full = gather_rows(lower, "expert")
    last = gather_rows(last, "expert").reshape(owners, qkv_cols + out_cols + router_pad, width)

    def qkv_of(block):
        return block[:, :qkv_cols].reshape(-1, width)

    def out_of(block):
        return block[:, qkv_cols:qkv_cols + out_cols].reshape(-1, width)

    router_full = last[:, qkv_cols + out_cols:qkv_cols + out_cols + router.shape[1]].reshape(experts_all, width)

    up_pair = jnp.stack([expert_up, swap_pair(expert_up)])
    down_pair = jnp.stack([expert_down, swap_pair(expert_down)])

    slots = expert_slots(routes, experts_all, capacity)
    zone_slots = [slots] + [shift_from(slots, 2 * d) for d in range(1, zones)]
    slot_columns = jnp.concatenate(zone_slots, axis=1)
    slot_rows = slot_columns.T.reshape(zones, routes.shape[1], length)

    def dispatch(rows):
        own = [rows] + [shift_from(rows, 2 * d) for d in range(1, zones)]
        packed = spread(slot_rows, jnp.stack(own), experts_all, capacity)
        return exchange(packed.reshape(owners, local, zones * capacity, width))

    def undo(rows):
        back = exchange(rows).reshape(experts_all, zones, capacity, width)
        return collect(slot_columns, back)

    cotangent_rows = dispatch(cotangent)

    onehot = bucket_onehot(length, bias_tables.shape[2])
    vectors = lax.dot_general(
        bias_tables, onehot, (((2,), (1,)), ((), ())), precision=lax.Precision.HIGHEST
    )
    gains = [norm_gains[i:i + 1] for i in range(4)]
    x0 = tokens.astype(F32)
    x1, ah0, qkv0, o0, lse0 = attend(piece_start, x0, gains[0], qkv_of(first), out_of(first), vectors[0])
    x2, mh = mlp(x1, gains[1], up_full, down_full)
    x3, ah1, qkv1, o1, lse1 = attend(piece_start, x2, gains[2], qkv_of(last), out_of(last), vectors[1])

    unit3 = x3 * inverse_rms(x3)
    eh = (unit3 * gains[3]).astype(BF)
    logits = nt(eh, router_full)
    expert_ids = jnp.arange(experts_all, dtype=jnp.int32)
    chosen = routes[:, :, None] == expert_ids[None, None, :]
    gates = jax.nn.softmax(jnp.sum(jnp.where(chosen, logits[:, None, :], 0.0), axis=2), axis=1)

    eh_rows = dispatch(eh)
    slot_ids = jnp.arange(experts_all * capacity, dtype=jnp.int32)

    def gate_slots(zone):
        zone_gates = gates if zone == 0 else shift_from(gates, 2 * zone)
        hit = zone_slots[zone][:, :, None] == slot_ids[None, None, :]
        return jnp.sum(jnp.where(hit, zone_gates[:, :, None], 0.0), axis=(0, 1)).reshape(experts_all, capacity)

    gate_rows = exchange(
        jnp.stack([gate_slots(d) for d in range(zones)], axis=1).reshape(owners, local, zones * capacity)
    )
    y_rows, dx_rows, dgate_rows, own_up, own_down, peer_up, peer_down = run_experts(
        eh_rows, cotangent_rows, gate_rows[..., None], up_pair, down_pair
    )
    grad_up = own_up + swap_pair(peer_up).astype(F32)
    grad_down = own_down + swap_pair(peer_down).astype(F32)

    dx_back = undo(dx_rows)
    dgate_back = exchange(dgate_rows[..., 0]).reshape(experts_all, zones, capacity)
    token_grad = dx_back[0]
    gate_grad = 0.0
    for d in range(zones):
        hit = zone_slots[d][:, :, None] == slot_ids[None, None, :]
        part = jnp.sum(jnp.where(hit, dgate_back[:, d].reshape(-1)[None, None, :], 0.0), axis=2)
        gate_grad = gate_grad + (part if d == 0 else shift_to(part, 2 * d))
    for d in range(1, zones):
        token_grad = token_grad + shift_to(dx_back[d].astype(BF), 2 * d).astype(F32)
    y_back = undo(y_rows)
    final = x3 + y_back[0]
    for d in range(1, zones):
        final = final + shift_to(y_back[d].astype(BF), 2 * d).astype(F32)
    output = final.astype(BF)

    c = cotangent.astype(F32)
    dchoice = gates * (gate_grad - jnp.sum(gates * gate_grad, axis=1, keepdims=True))
    dlogits = jnp.sum(jnp.where(chosen, dchoice[:, :, None], 0.0), axis=1).astype(BF)
    grad_router = tn(dlogits, eh)
    deh = token_grad + nn(dlogits, router_full)
    scaled = deh * gains[3]
    dx3 = c + inverse_rms(x3) * (scaled - unit3 * jnp.mean(scaled * unit3, axis=1, keepdims=True))
    dgain3 = jnp.sum(deh * unit3, axis=0)[None]

    dx2, dqkv1, dout1, dvec1, dgain2 = attend_back(
        piece_start, x2, gains[2], qkv_of(last), out_of(last), vectors[1], ah1, qkv1, o1, lse1, dx3
    )
    dx1, dup, ddown, dgain1 = mlp_back(x1, gains[1], up_full, down_full, mh, dx2)
    dx0, dqkv0, dout0, dvec0, dgain0 = attend_back(
        piece_start, x0, gains[0], qkv_of(first), out_of(first), vectors[0], ah0, qkv0, o0, lse0, dx1
    )

    def reduce_block(parts):
        block = jnp.concatenate([p.reshape(owners, -1, p.shape[-1]) for p in parts], axis=1)
        rows = block.shape[1]
        mine = scatter_rows(block.reshape(owners * rows, block.shape[2]), "expert")
        return scatter_rows(mine.T, "shard").astype(F32)

    router_rows = jnp.pad(
        grad_router.astype(BF).reshape(owners, local, width), ((0, 0), (0, router_pad - local), (0, 0))
    )
    last_grad = reduce_block([dqkv1, dout1, router_rows])
    grad_mlp_up = reduce_block([dup])
    grad_mlp_down = reduce_block([ddown])
    first_grad = reduce_block([dqkv0, dout0])
    grad_qkv = jnp.stack([first_grad[:, :qkv_cols], last_grad[:, :qkv_cols]])
    grad_out = jnp.stack([first_grad[:, qkv_cols:], last_grad[:, qkv_cols:qkv_cols + out_cols]])
    grad_router_out = last_grad[:, qkv_cols + out_cols:qkv_cols + out_cols + local]

    dtables = lax.dot_general(
        jnp.stack([dvec0, dvec1]), onehot, (((2,), (0,)), ((), ())), precision=lax.Precision.HIGHEST
    )
    dgains = jnp.concatenate([dgain0, dgain1, dgain2, dgain3])
    small = total_over_mesh(jnp.concatenate([dgains.reshape(-1), dtables.reshape(-1)]))
    return (
        output,
        dx0,
        small[:dgains.size].reshape(dgains.shape),
        small[dgains.size:].reshape(dtables.shape),
        grad_qkv,
        grad_out,
        grad_mlp_up,
        grad_mlp_down,
        grad_router_out,
        grad_up,
        grad_down,
    )


def solution(mesh):
    both = P(("expert", "shard"), None)
    split3, split2 = P(None, "shard", "expert"), P("shard", "expert")
    up_spec, down_spec = P("expert", None, "shard"), P("expert", "shard", None)
    in_specs = (
        both, P(("expert", "shard")), both, P(), P(), split3, split3, split2, split2, split2, up_spec, down_spec, both
    )
    out_specs = (both, both, P(), P(), split3, split3, split2, split2, split2, up_spec, down_spec)
    return jax.shard_map(per_device, mesh=mesh, in_specs=in_specs, out_specs=out_specs, check_vma=False)
```

time: 1690 us -> 1060 us (0.63)
  local copies, waits for them, and re-layouts: 998 us -> 50.9 us
  waiting for transfers between devices: 150 us -> 516 us
  Pallas kernels: 0 us -> 242 us
  matrix products: 230 us -> 3.39 us
  other arithmetic: 99.5 us -> 43.7 us
  starting transfers between devices: 17.4 us -> 46.8 us
  blocking collectives: 161 us -> 140 us
    unnamed x290 -> x57, local copies, waits for them, and re-layouts: 536 us -> 13.6 us
    pallas_call x0 -> x11, Pallas kernels: none -> 242 us  [the longest x1 72 us: run_experts(): pl.pallas_call(experts_kernel, grid=(local, 2), out_shape=(jax.ShapeDtype...]
    dot_general x43 -> x6, matrix products: 230 us -> 3.39 us  [the longest x1 1.94 us: nn(): lax.dot_general(a, b, (((1,), (0,)), ((), ())), preferred_element_type=F32)]
    reshape x5 -> x10, local copies, waits for them, and re-layouts: 223 us -> 8.88 us  [the longest x1 6.63 us: per_device(): gather_rows(first, 'expert').reshape(owners, qkv_cols + out_cols, width)]
    reduce_scatter x5, waiting for transfers between devices: 0.02 us -> 200 us  [scatter_rows(): return lax.psum_scatter(value, name, scatter_dimension=0, tiled=True)]
    ppermute x0 -> x16, waiting for transfers between devices: none -> 195 us  [the longest x4 97.9 us: swap_pair(): lax.ppermute(value, 'shard', [(z, z ^ 1) for z in range(lax.axis_size('sh...]
    slice x8 -> x10, local copies, waits for them, and re-layouts: 96.1 us -> 14.9 us  [the longest x2 8.01 us: qkv_of(): return block[:, :qkv_cols].reshape(-1, width)]
    all_to_all x0 -> x2, blocking collectives: none -> 67.6 us  [exchange(): lax.all_to_all(value, 'expert', split_axis=0, concat_axis=0, tiled=True)]
  transfers between devices with their start and end apart: 20 -> 32, of which waited for: 5 -> 19; matrix products, arithmetic and copies ran while one was open for 67% -> 8% of each run, Pallas kernels for 0% -> 11%
where the time goes in v1:
time: 1060 us
  waiting for transfers between devices  516 us (49%)
  Pallas kernels  242 us (23%)
  blocking collectives  140 us (13%)
  local copies, waits for them, and re-layouts  50.9 us (5%)
  starting transfers between devices  46.8 us (4%)
  other arithmetic  43.7 us (4%)
  between operations  15.7 us (1%)
    reduce_scatter x5, waiting for transfers between devices, scatter_rows(): return lax.psum_scatter(value, name, scatter_dimension=0, tiled=True)  200 us
    ppermute x4, waiting for transfers between devices, swap_pair(): lax.ppermute(value, 'shard', [(z, z ^ 1) for z in range(lax.axis_size('sh...  97.9 us
    all_gather x4, blocking collectives, gather_rows(): return lax.all_gather(value, name, axis=0, tiled=True)  72.9 us
    pallas_call x1, Pallas kernels, run_experts(): pl.pallas_call(experts_kernel, grid=(local, 2), out_shape=(jax.ShapeDtype...  72 us
    all_to_all x2, blocking collectives, exchange(): lax.all_to_all(value, 'expert', split_axis=0, concat_axis=0, tiled=True)  67.6 us
    pallas_call x2, Pallas kernels, attend_back(): pl.pallas_call(attend_back_kernel, out_shape=(jax.ShapeDtypeStruct((lengt...  65.6 us
    ppermute x4, waiting for transfers between devices, shift_from(): lax.ppermute(value, 'shard', [((z + distance) % size, z) for z in range(s...  59.7 us
    unnamed x15, waiting for transfers between devices  43.8 us
  transfers between devices with their start and end apart: 32, of which 19 were waited for; matrix products, arithmetic and copies ran while one was open for 8% of the time, Pallas kernels for 11%

profile of v1, /device:TPU:0, one launch (start us, length us, event | category | flops | bytes accessed | tf_op | source)
XLA Modules:
  0.0 1058.8 jit_solution(4814758510199514514)
XLA Ops:
  9.2 18.4 %all_gather.24 = bf16[768,384]{1,0:T(8,128)(2,1)} all-gather(bf16[192,384]{1,0:T(8,128)(2,1)S(1)} %pad_maximum_fusion.7), channel_id=1, replica_groups=mesh['expert'=8,'shard'=4] {'shard'}, dimensions={0}, use_global_device_ids=true | all-gather | bytes 737280 | tf_op jit(solution)/shard_map/all_gather | solution.py:584
  27.7 17.0 %all_gather.26 = bf16[768,384]{1,0:T(8,128)(2,1)S(1)} all-gather(bf16[192,384]{1,0:T(8,128)(2,1)} %param.21), channel_id=1, replica_groups=mesh['expert'=8,'shard'=4] {'shard'}, dimensions={0}, use_global_device_ids=true | all-gather | bytes 737280 | tf_op jit(solution)/shard_map/all_gather | solution.py:584
  45.8 17.9 %all_gather.28 = bf16[3072,96]{0,1:T(8,128)(2,1)} all-gather(bf16[768,96]{0,1:T(8,128)(2,1)S(1)} %copy-done.10), channel_id=1, replica_groups=mesh['expert'=8,'shard'=4] {'shard'}, dimensions={0}, use_global_device_ids=true | all-gather | bytes 737280 | tf_op jit(solution)/shard_map/all_gather | solution.py:584
  64.2 19.6 %all_gather.30 = bf16[768,400]{1,0:T(8,128)(2,1)S(1)} all-gather(bf16[192,400]{1,0:T(8,128)(2,1)S(1)} %fusion.13), channel_id=1, replica_groups=mesh['expert'=8,'shard'=4] {'shard'}, dimensions={0}, use_global_device_ids=true | all-gather | bytes 768000 | tf_op jit(solution)/shard_map/all_gather | solution.py:584
  95.4 27.6 %collective-permute-done = s32[512,2]{1,0:T(8,128)S(1)} collective-permute-done((s32[512,2]{1,0:T(8,128)S(1)}, s32[512,2]{1,0:T(8,128)S(1)}, u32[]{:S(2)}, u32[]{:S(2)}) %collective-permute-start) | collective-permute-done | bytes 4128 | tf_op jit(solution)/shard_map/ppermute | solution.py:557
  153.0 18.3 %attend.2 = (f32[512,768]{1,0:T(8,128)}, bf16[512,768]{1,0:T(8,128)(2,1)}, bf16[512,2304]{1,0:T(8,128)(2,1)}, bf16[512,768]{1,0:T(8,128)(2,1)}, f32[12,512]{1,0:T(8,128)}) custom-call(s32[1]{0:T(128)S(6)} %copy.153.piece_ref, f32[512,768]{1,0:T(8,128)} %convert_element_type.70.x_ref, f32[1,768]{1,0:T(1,128)} %get-tuple-element.159.gain_ref, ...), custom_call_target="tpu_custom_call" | custom-call | flops 3221225472 | bytes 12582912 | tf_op jit(solution)/shard_map/attend/pallas_call | solution.py:128
  184.1 40.8 %all-gather.11.cloned.1.call-done = bf16[3200,768]{1,0:T(8,128)(2,1)} async-done(((bf16[400,768]{1,0:T(8,128)(2,1)}), bf16[3200,768]{1,0:T(8,128)(2,1)}) %all-gather.11.cloned.1.call-update) | async-done | bytes 4915216 | tf_op jit(solution)/shard_map/all_gather | solution.py:584
  232.2 18.2 %attend.3 = (f32[512,768]{1,0:T(8,128)}, bf16[512,768]{1,0:T(8,128)(2,1)}, bf16[512,2304]{1,0:T(8,128)(2,1)}, bf16[512,768]{1,0:T(8,128)(2,1)}, f32[12,512]{1,0:T(8,128)}) custom-call(s32[1]{0:T(128)S(6)} %copy.153.piece_ref, f32[512,768]{1,0:T(8,128)} %get-tuple-element.45.x_ref, f32[1,768]{1,0:T(1,128)} %get-tuple-element.160.gain_ref, ...), custom_call_target="tpu_custom_call" | custom-call | flops 3221225472 | bytes 12582912 | tf_op jit(solution)/shard_map/attend/pallas_call | solution.py:128
  259.3 32.2 %collective-permute-done.3 = f32[512,2]{0,1:T(2,128)S(1)} collective-permute-done((f32[512,2]{0,1:T(2,128)S(1)}, f32[512,2]{0,1:T(2,128)S(1)}, u32[]{:S(2)}, u32[]{:S(2)}) %collective-permute-start.3) | collective-permute-done | bytes 4128 | tf_op jit(solution)/shard_map/ppermute | solution.py:557
  312.9 52.2 %collective-permute-done.4 = bf16[2,768,768]{2,1,0:T(8,128)(2,1)S(1)} collective-permute-done((bf16[2,768,768]{2,1,0:T(8,128)(2,1)}, bf16[2,768,768]{2,1,0:T(8,128)(2,1)S(1)}, u32[]{:S(2)}, u32[]{:S(2)}) %collective-permute-start.4) | collective-permute-done | bytes 2359328 | tf_op jit(solution)/shard_map/ppermute | solution.py:566
  369.6 45.7 %collective-permute-done.5 = bf16[2,768,768]{2,1,0:T(8,128)(2,1)S(1)} collective-permute-done((bf16[2,768,768]{2,1,0:T(8,128)(2,1)}, bf16[2,768,768]{2,1,0:T(8,128)(2,1)S(1)}, u32[]{:S(2)}, u32[]{:S(2)}) %collective-permute-start.5) | collective-permute-done | bytes 2359328 | tf_op jit(solution)/shard_map/ppermute | solution.py:566
  419.6 72.0 %experts.1 = (bf16[8,2,192,768]{3,2,1,0:T(8,128)(2,1)}, bf16[8,2,192,768]{3,2,1,0:T(8,128)(2,1)}, f32[8,2,192,1]{3,2,1,0:T(8,128)}, f32[2,768,768]{2,1,0:T(8,128...) custom-call(bf16[8,2,192,768]{3,2,1,0:T(8,128)(2,1)} %all-to-all-done.x_ref, ...), custom_call_target="tpu_custom_call" | custom-call | flops 43486543872 | bytes 37748736 | tf_op jit(solution)/shard_map/experts/pallas_call | solution.py:435
  502.1 59.2 %all_to_all.31 = bf16[8,2,192,768]{3,2,1,0:T(8,128)(2,1)} all-to-all(bf16[8,2,192,768]{3,2,1,0:T(8,128)(2,1)} %get-tuple-element.57), channel_id=1, replica_groups=mesh['expert'=8,'shard'=4] {'expert'}, dimensions={0} | all-to-all | bytes 9437184 | tf_op jit(solution)/shard_map/all_to_all | solution.py:580
  585.4 35.2 %all-to-all-done.3 = bf16[8,2,192,768]{3,2,1,0:T(8,128)(2,1)} async-done(((bf16[8,2,192,768]{3,2,1,0:T(8,128)(2,1)}), bf16[8,2,192,768]{3,2,1,0:T(8,128)(2,1)}, u32[]{:S(2)}, u32[]{:S(2)}) %all-to-all-start.3) | async-done | bytes 4718624 | tf_op jit(solution)/shard_map/all_to_all | solution.py:580
  635.2 29.9 %collective-permute-done.6 = bf16[512,768]{1,0:T(8,128)(2,1)S(1)} collective-permute-done((bf16[512,768]{1,0:T(8,128)(2,1)S(1)}, bf16[512,768]{1,0:T(8,128)(2,1)S(1)}, u32[]{:S(2)}, u32[]{:S(2)}) %collective-permute-start.6) | collective-permute-done | bytes 786464 | tf_op jit(solution)/shard_map/ppermute | solution.py:562
  667.1 32.8 %attend_back.2 = (f32[512,768]{1,0:T(8,128)}, bf16[2304,768]{1,0:T(8,128)(2,1)}, bf16[768,768]{1,0:T(8,128)(2,1)}, f32[12,1024]{1,0:T(8,128)}, f32[1,768]{1,0:T(1,128)}) custom-call(s32[1]{0:T(128)S(6)} %copy.153.piece_ref, f32[512,768]{1,0:T(8,128)} %get-tuple-element.45.x_ref, f32[1,768]{1,0:T(1,128)} %get-tuple-element.160.gain_ref, ...), custom_call_target="tpu_custom_call" | custom-call | flops 6845104128 | bytes 25165824 | tf_op jit(solution)/shard_map/attend_back/pallas_call | solution.py:267
  699.9 23.9 %mlp_back.1 = (f32[512,768]{1,0:T(8,128)}, bf16[3072,768]{1,0:T(8,128)(2,1)}, bf16[768,3072]{1,0:T(8,128)(2,1)}, f32[1,768]{1,0:T(1,128)}) custom-call(f32[512,768]{1,0:T(8,128)} %get-tuple-element.44.x_ref, f32[1,768]{1,0:T(1,128)} %get-tuple-element.158.gain_ref, bf16[3072,768]{1,0:T(8,128)(2,1)} %all-gather.7.cloned.1.call-done.up_ref, ...), custom_call_target="tpu_custom_call" | custom-call | flops 12079595520 | bytes 25165824 | tf_op jit(solution)/shard_map/mlp_back/pallas_call | solution.py:351
  723.9 32.8 %attend_back.3 = (f32[512,768]{1,0:T(8,128)}, bf16[2304,768]{1,0:T(8,128)(2,1)}, bf16[768,768]{1,0:T(8,128)(2,1)}, f32[12,1024]{1,0:T(8,128)}, f32[1,768]{1,0:T(1,128)}) custom-call(s32[1]{0:T(128)S(6)} %copy.153.piece_ref, f32[512,768]{1,0:T(8,128)} %convert_element_type.70.x_ref, f32[1,768]{1,0:T(1,128)} %get-tuple-element.159.gain_ref, ...), custom_call_target="tpu_custom_call" | custom-call | flops 6845104128 | bytes 25165824 | tf_op jit(solution)/shard_map/attend_back/pallas_call | solution.py:267
  782.0 55.4 %reduce-scatter.15.cloned.1.call-done = bf16[384,768]{1,0:T(8,128)(2,1)} async-done(((bf16[3072,768]{1,0:T(8,128)(2,1)}), bf16[384,768]{1,0:T(8,128)(2,1)}) %reduce-scatter.15.cloned.1.call-update) | async-done | bytes 589840 | tf_op jit(solution)/shard_map/reduce_scatter | solution.py:588
  841.7 53.7 %reduce-scatter.21.cloned.1.call-done = bf16[96,3072]{1,0:T(8,128)(2,1)} async-done(((bf16[768,3072]{1,0:T(8,128)(2,1)}), bf16[96,3072]{1,0:T(8,128)(2,1)}) %reduce-scatter.21.cloned.1.call-update) | async-done | bytes 589840 | tf_op jit(solution)/shard_map/reduce_scatter | solution.py:588
  896.0 58.2 %reduce-scatter.17.cloned.1.call-done = bf16[400,768]{1,0:T(8,128)(2,1)} async-done(((bf16[3200,768]{1,0:T(8,128)(2,1)}), bf16[400,768]{1,0:T(8,128)(2,1)}) %reduce-scatter.17.cloned.1.call-update) | async-done | bytes 614416 | tf_op jit(solution)/shard_map/reduce_scatter | solution.py:588
  980.8 20.7 %reduce-scatter.25.cloned.1.call-done = bf16[192,384]{1,0:T(8,128)(2,1)} async-done(((bf16[768,384]{1,0:T(8,128)(2,1)}), bf16[192,384]{1,0:T(8,128)(2,1)}) %reduce-scatter.25.cloned.1.call-update) | async-done | bytes 147472
  1002.6 21.5 %reduce-scatter.23.cloned.1.call-done = bf16[768,96]{0,1:T(8,128)(2,1)} async-done(((bf16[3072,96]{0,1:T(8,128)(2,1)}), bf16[768,96]{0,1:T(8,128)(2,1)}) %reduce-scatter.23.cloned.1.call-update) | async-done | bytes 147472 | tf_op jit(solution)/shard_map/reduce_scatter | solution.py:588
  1025.8 22.2 %reduce-scatter.27.cloned.1.call-done = bf16[192,400]{1,0:T(8,128)(2,1)} async-done(((bf16[768,400]{1,0:T(8,128)(2,1)}), bf16[192,400]{1,0:T(8,128)(2,1)}) %reduce-scatter.27.cloned.1.call-update) | async-done | bytes 153616
  (225 shorter events, 217.9 us)
Async XLA Ops:
  7.2 132.8 %all-gather.5.cloned.1.call-start = ((), (), s32[]{:S(2)}) async-start(), calls=%async_computation.14 | async-start | bytes 5308416 | tf_op jit(solution)/shard_map/all_gather | solution.py:584
  27.7 143.6 %all-gather.7.cloned.1.call-start = ((), (), s32[]{:S(2)}) async-start(), calls=%async_computation.15 | async-start | bytes 5308416 | tf_op jit(solution)/shard_map/all_gather | solution.py:584
  45.8 125.5 %all-gather.9.cloned.1.call-start = ((), (), s32[]{:S(2)}) async-start(), calls=%async_computation.16 | async-start | bytes 5308416 | tf_op jit(solution)/shard_map/all_gather | solution.py:584
  63.8 161.0 %all-gather.11.cloned.1.call-start = ((), (), s32[]{:S(2)}) async-start(), calls=%async_computation.17 | async-start | bytes 5529600 | tf_op jit(solution)/shard_map/all_gather | solution.py:584
  84.8 39.1 %collective-permute-start.2 = (bf16[512,768]{1,0:T(8,128)(2,1)S(1)}, bf16[512,768]{1,0:T(8,128)(2,1)S(1)}, u32[]{:S(2)}, u32[]{:S(2)}) collective-permute-start(bf16[512,768]{1,0:T(8,128)(2,1)S(1)} %copy-done.3), channel_id=1, source_target_pairs={{2,0},{3,1},{0,2},{1,3},{6,4},{7,5},{4,6},{5,7},{10,8},{11,9},{8,1... | collective-permute-start | bytes 2359304 | tf_op jit(solution)/shard_map/ppermute | solution.py:557
  131.9 164.0 %all-to-all-start.1 = ((bf16[8,2,192,768]{3,2,1,0:T(8,128)(2,1)}), bf16[8,2,192,768]{3,2,1,0:T(8,128)(2,1)}, u32[]{:S(2)}, u32[]{:S(2)}) async-start(bf16[8,2,192,768]{3,2,1,0:T(8,128)(2,1)} %bitcast.95), calls=%async_computation.1 | async-start | bytes 9437184 | tf_op jit(solution)/shard_map/all_to_all | solution.py:580
  253.7 39.5 %collective-permute-start.1 = (bf16[512,768]{1,0:T(8,128)(2,1)S(1)}, bf16[512,768]{1,0:T(8,128)(2,1)}, u32[]{:S(2)}, u32[]{:S(2)}) collective-permute-start(bf16[512,768]{1,0:T(8,128)(2,1)S(1)} %multiply_convert_fusion), channel_id=1, source_target_pairs={{2,0},{3,1},{0,2},{1,3},{6,4},{7,5},{4,6},{5,7},{10,8},{11,9},{8,1... | collective-permute-start | bytes 2359304 | tf_op jit(solution)/shard_map/ppermute | solution.py:557
  257.7 33.8 %collective-permute-start.3 = (f32[512,2]{0,1:T(2,128)S(1)}, f32[512,2]{0,1:T(2,128)S(1)}, u32[]{:S(2)}, u32[]{:S(2)}) collective-permute-start(f32[512,2]{0,1:T(2,128)S(1)} %fusion.35), channel_id=1, source_target_pairs={{2,0},{3,1},{0,2},{1,3},{6,4},{7,5},{4,6},{5,7},{10,8},{11,9},{8,1... | collective-permute-start | bytes 12296 | tf_op jit(solution)/shard_map/ppermute | solution.py:557
  306.0 113.6 %all-to-all-start = ((bf16[8,2,192,768]{3,2,1,0:T(8,128)(2,1)}), bf16[8,2,192,768]{3,2,1,0:T(8,128)(2,1)}, u32[]{:S(2)}, u32[]{:S(2)}) async-start(bf16[8,2,192,768]{3,2,1,0:T(8,128)(2,1)} %bitcast.97), calls=%async_computation | async-start | bytes 9437184 | tf_op jit(solution)/shard_map/all_to_all | solution.py:580
  310.8 54.3 %collective-permute-start.4 = (bf16[2,768,768]{2,1,0:T(8,128)(2,1)}, bf16[2,768,768]{2,1,0:T(8,128)(2,1)S(1)}, u32[]{:S(2)}, u32[]{:S(2)}) collective-permute-start(bf16[2,768,768]{2,1,0:T(8,128)(2,1)} %param.24), channel_id=1, source_target_pairs={{0,1},{1,0},{2,3},{3,2},{4,5},{5,4},{6,7},{7,6},{8,9},{9,8},{10,11... | collective-permute-start | bytes 7077896 | tf_op jit(solution)/shard_map/ppermute | solution.py:566
  311.4 103.9 %collective-permute-start.5 = (bf16[2,768,768]{2,1,0:T(8,128)(2,1)}, bf16[2,768,768]{2,1,0:T(8,128)(2,1)S(1)}, u32[]{:S(2)}, u32[]{:S(2)}) collective-permute-start(bf16[2,768,768]{2,1,0:T(8,128)(2,1)} %param.25), channel_id=1, source_target_pairs={{0,1},{1,0},{2,3},{3,2},{4,5},{5,4},{6,7},{7,6},{8,9},{9,8},{10,11... | collective-permute-start | bytes 7077896 | tf_op jit(solution)/shard_map/ppermute | solution.py:566
  561.2 59.4 %all-to-all-start.3 = ((bf16[8,2,192,768]{3,2,1,0:T(8,128)(2,1)}), bf16[8,2,192,768]{3,2,1,0:T(8,128)(2,1)}, u32[]{:S(2)}, u32[]{:S(2)}) async-start(bf16[8,2,192,768]{3,2,1,0:T(8,128)(2,1)} %get-tuple-element.47), calls=%async_computation.3 | async-start | bytes 9437184 | tf_op jit(solution)/shard_map/all_to_all | solution.py:580
  565.9 213.9 %reduce-scatter.19.cloned.1.call-start = ((), (), s32[]{:S(2)}) async-start(), calls=%async_computation.20 | async-start | bytes 5308416 | tf_op jit(solution)/shard_map/reduce_scatter | solution.py:588
  583.3 49.9 %collective-permute-start.7 = (bf16[512,768]{1,0:T(8,128)(2,1)}, bf16[512,768]{1,0:T(8,128)(2,1)}, u32[]{:S(2)}, u32[]{:S(2)}) collective-permute-start(bf16[512,768]{1,0:T(8,128)(2,1)} %fusion.11), channel_id=1, source_target_pairs={{0,2},{1,3},{2,0},{3,1},{4,6},{5,7},{6,4},{7,5},{8,10},{9,11},{10,... | collective-permute-start | bytes 2359304 | tf_op jit(solution)/shard_map/ppermute | solution.py:562
  631.0 34.1 %collective-permute-start.6 = (bf16[512,768]{1,0:T(8,128)(2,1)S(1)}, bf16[512,768]{1,0:T(8,128)(2,1)S(1)}, u32[]{:S(2)}, u32[]{:S(2)}) collective-permute-start(bf16[512,768]{1,0:T(8,128)(2,1)S(1)} %fusion.10), channel_id=1, source_target_pairs={{0,2},{1,3},{2,0},{3,1},{4,6},{5,7},{6,4},{7,5},{8,10},{9,11},{10,... | collective-permute-start | bytes 2359304 | tf_op jit(solution)/shard_map/ppermute | solution.py:562
  723.8 113.6 %reduce-scatter.15.cloned.1.call-start = ((), (), s32[]{:S(2)}) async-start(), calls=%async_computation.18 | async-start | bytes 5308416 | tf_op jit(solution)/shard_map/reduce_scatter | solution.py:588
  761.6 133.8 %reduce-scatter.21.cloned.1.call-start = ((), (), s32[]{:S(2)}) async-start(), calls=%async_computation.21 | async-start | bytes 5308416 | tf_op jit(solution)/shard_map/reduce_scatter | solution.py:588
  762.3 191.8 %reduce-scatter.17.cloned.1.call-start = ((), (), s32[]{:S(2)}) async-start(), calls=%async_computation.19 | async-start | bytes 5529600 | tf_op jit(solution)/shard_map/reduce_scatter | solution.py:588
  768.0 210.9 %reduce-scatter.29.cloned.1.call-start = ((), (), s32[]{:S(2)}) async-start(), calls=%async_computation.25 | async-start | bytes 737280
  782.0 219.6 %reduce-scatter.25.cloned.1.call-start = ((), (), s32[]{:S(2)}) async-start(), calls=%async_computation.23 | async-start | bytes 737280
  839.5 184.6 %reduce-scatter.23.cloned.1.call-start = ((), (), s32[]{:S(2)}) async-start(), calls=%async_computation.22 | async-start | bytes 737280 | tf_op jit(solution)/shard_map/reduce_scatter | solution.py:588
  839.6 128.2 %collective-permute-start.14 = (bf16[2,768,768]{2,1,0:T(8,128)(2,1)}, bf16[2,768,768]{2,1,0:T(8,128)(2,1)}, u32[]{:S(2)}, u32[]{:S(2)}) collective-permute-start(bf16[2,768,768]{2,1,0:T(8,128)(2,1)} %get-tuple-element.74), channel_id=1, source_target_pairs={{0,1},{1,0},{2,3},{3,2},{4,5},{5,4},{6,7},{7,6},{8,9},{9,8},{10,11... | collective-permute-start | bytes 7077896 | tf_op jit(solution)/shard_map/ppermute | solution.py:566
  841.2 133.1 %collective-permute-start.15 = (bf16[2,768,768]{2,1,0:T(8,128)(2,1)}, bf16[2,768,768]{2,1,0:T(8,128)(2,1)S(1)}, u32[]{:S(2)}, u32[]{:S(2)}) collective-permute-start(bf16[2,768,768]{2,1,0:T(8,128)(2,1)} %get-tuple-element.76), channel_id=1, source_target_pairs={{0,1},{1,0},{2,3},{3,2},{4,5},{5,4},{6,7},{7,6},{8,9},{9,8},{10,11... | collective-permute-start | bytes 7077896 | tf_op jit(solution)/shard_map/ppermute | solution.py:566
  895.4 152.6 %reduce-scatter.27.cloned.1.call-start = ((), (), s32[]{:S(2)}) async-start(), calls=%async_computation.24 | async-start | bytes 983040
  (30 other events, 1261.4 us)
Sparse Core Ops, SparseCore 0:
  27.8 41.5 all-gather.4
  71.9 38.9 all-gather.6
  112.7 48.8 all-gather.8
  163.9 60.8 all-gather.10
  723.9 55.8 reduce-scatter.18
  783.5 53.8 reduce-scatter.14
  841.4 53.8 reduce-scatter.20
  899.3 54.8 reduce-scatter.16
  956.4 22.0 reduce-scatter.28
  981.2 20.3 reduce-scatter.24
  1003.8 20.2 reduce-scatter.22
  1026.3 21.6 reduce-scatter.26

commit v2 on v1

--- a/solution.py
+++ b/solution.py
@@ -57,12 +57,42 @@
     strip_ref[...] = pltpu.roll(wide, vector_row.shape[1] - 127, 1, stride=1, stride_axis=0)
 
 
+def flatten(blocks_ref, flat_ref):
+    rows = blocks_ref.shape[1]
+    for i in range(blocks_ref.shape[0]):
+        flat_ref[i * rows:i * rows + rows, :] = blocks_ref[i]
+
+
+def unflatten(flat_ref, blocks_ref, start):
+    count = blocks_ref.shape[0]
+    rows = flat_ref.shape[0] // count
+    for i in range(count):
+        blocks_ref[i, start:start + rows, :] = flat_ref[i * rows:i * rows + rows, :]
+
+
+def weight_specs(weights):
+    packed, qkv_rows, out_rows = weights
+    if isinstance(packed, tuple):
+        return list(packed), [VMEM_SPEC, VMEM_SPEC]
+    return [packed], [VMEM_SPEC]
+
+
+def weight_views(weights, refs):
+    packed, qkv_rows, out_rows = weights
+    if isinstance(packed, tuple):
+        return refs[0], refs[1], refs[2:]
+    return refs[0].at[:, 0:qkv_rows, :], refs[0].at[:, qkv_rows:qkv_rows + out_rows, :], refs[1:]
+
+
 def attend_kernel(
-    piece_ref, x_ref, gain_ref, w_ref, wo_ref, vec_ref,
-    out_ref, normed_ref, qkv_ref, mixed_ref, lse_ref,
-    mask_ref, strip_ref, score_ref, prob_ref,
+    weights, piece_ref, x_ref, gain_ref, *refs
 ):
+    w_ref, wo_ref, refs = weight_views(weights, refs)
+    (vec_ref, out_ref, normed_ref, qkv_ref, mixed_ref, lse_ref,
+     mask_ref, strip_ref, score_ref, prob_ref, flat_ref, flat_out_ref) = refs
     length, width = x_ref.shape
+    flatten(w_ref, flat_ref)
+    flatten(wo_ref, flat_out_ref)
     tiles = length // 128
     fill_mask(piece_ref, mask_ref)
     field = x_ref[...]
@@ -70,7 +100,7 @@
 
     def project(c, _):
         cols = pl.ds(pl.multiple_of(c * 256, 256), 256)
-        qkv_ref[:, cols] = nt(normed_ref[...], w_ref[cols, :]).astype(BF)
+        qkv_ref[:, cols] = nt(normed_ref[...], flat_ref[cols, :]).astype(BF)
         return 0
 
     lax.fori_loop(0, 3 * width // 256, project, 0)
@@ -111,7 +141,7 @@
 
     def back(c, _):
         cols = pl.ds(pl.multiple_of(c * 256, 256), 256)
-        out_ref[:, cols] = x_ref[:, cols] + nt(mixed_ref[...], wo_ref[cols, :])
+        out_ref[:, cols] = x_ref[:, cols] + nt(mixed_ref[...], flat_out_ref[cols, :])
         return 0
 
     lax.fori_loop(0, width // 256, back, 0)
@@ -121,12 +151,13 @@
 VMEM_SPEC = pl.BlockSpec(memory_space=pltpu.VMEM)
 
 
-def attend(piece, x, gain, w, wo, vectors):
+def attend(piece, x, gain, weights, vectors):
     length, width = x.shape
+    w_args, w_specs = weight_specs(weights)
     heads = vectors.shape[0]
     span = vectors.shape[1]
     return pl.pallas_call(
-        attend_kernel,
+        lambda *refs: attend_kernel(weights, *refs),
         out_shape=(
             jax.ShapeDtypeStruct((length, width), F32),
             jax.ShapeDtypeStruct((length, width), BF),
@@ -134,13 +165,15 @@
             jax.ShapeDtypeStruct((length, width), BF),
             jax.ShapeDtypeStruct((heads, length), F32),
         ),
-        in_specs=[SMEM_SPEC] + [VMEM_SPEC] * 5,
+        in_specs=[SMEM_SPEC] + [VMEM_SPEC] * 2 + w_specs + [VMEM_SPEC],
         out_specs=[VMEM_SPEC] * 5,
         scratch_shapes=[
             pltpu.VMEM((length, length), F32),
             pltpu.VMEM((128, span), F32),
             pltpu.VMEM((length, length), F32),
             pltpu.VMEM((length, length), BF),
+            pltpu.VMEM((3 * width, width), BF),
+            pltpu.VMEM((width, width), BF),
         ],
         compiler_params=pltpu.CompilerParams(vmem_limit_bytes=VMEM_BYTES),
         cost_estimate=pl.CostEstimate(
@@ -149,14 +182,21 @@
             transcendentals=heads * length * length,
         ),
         name="attend",
-    )(piece, x, gain, w, wo, vectors)
+    )(piece, x, gain, *w_args, vectors)
 
 
 def attend_back_kernel(
-    piece_ref, x_ref, gain_ref, w_ref, wo_ref, vec_ref, normed_ref, qkv_ref, mixed_ref, lse_ref, grad_ref,
-    dx_ref, dw_ref, dwo_ref, dvec_ref, dgain_ref,
-    mask_ref, strip_ref, sums_ref, prob_ref, ds_ref, low_ref, do_ref, dqkv_ref, delta_ref,
+    tail, weights, piece_ref, x_ref, gain_ref, *refs
 ):
+    w_ref, wo_ref, refs = weight_views(weights, refs)
+    (vec_ref, normed_ref, qkv_ref, mixed_ref, lse_ref, grad_ref), refs = refs[:6], refs[6:]
+    tail_ref, refs = (refs[0], refs[1:]) if tail else (None, refs)
+    grad_refs, refs = (refs[1:len(refs) - 14], refs[:1] + refs[len(refs) - 14:])
+    (dx_ref, dvec_ref, dgain_ref,
+     mask_ref, strip_ref, sums_ref, prob_ref, ds_ref, low_ref, do_ref, dqkv_ref, delta_ref,
+     flat_ref, flat_out_ref, dw_ref) = refs
+    flatten(w_ref, flat_ref)
+    flatten(wo_ref, flat_out_ref)
     length, width = x_ref.shape
     heads = vec_ref.shape[0]
     tiles = length // 128
@@ -165,11 +205,17 @@
 
     def out_back(c, _):
         cols = pl.ds(pl.multiple_of(c * 256, 256), 256)
-        do_ref[:, cols] = nn(low_ref[...], wo_ref[:, cols]).astype(BF)
-        dwo_ref[cols, :] = tn(low_ref[:, cols], mixed_ref[...]).astype(BF)
+        do_ref[:, cols] = nn(low_ref[...], flat_out_ref[:, cols]).astype(BF)
         return 0
 
     lax.fori_loop(0, width // 256, out_back, 0)
+
+    def out_weights_back(c, _):
+        cols = pl.ds(pl.multiple_of(c * 256, 256), 256)
+        flat_out_ref[cols, :] = tn(low_ref[:, cols], mixed_ref[...]).astype(BF)
+        return 0
+
+    lax.fori_loop(0, width // 256, out_weights_back, 0)
     pick = (
         lax.broadcasted_iota(jnp.int32, (delta_ref.shape[0], width), 1) // (width // heads)
         == lax.broadcasted_iota(jnp.int32, (delta_ref.shape[0], width), 0)
@@ -244,10 +290,17 @@
 
     def rows_back(c, _):
         cols = pl.ds(pl.multiple_of(c * 256, 256), 256)
-        dx_ref[:, cols] = nn(dqkv_ref[...], w_ref[:, cols])
+        dx_ref[:, cols] = nn(dqkv_ref[...], flat_ref[:, cols])
         return 0
 
     lax.fori_loop(0, width // 256, rows_back, 0)
+    qkv_rows = w_ref.shape[1]
+    unflatten(dw_ref, grad_refs[0], 0)
+    unflatten(flat_out_ref, grad_refs[-1], qkv_rows if len(grad_refs) == 1 else 0)
+    if tail:
+        start = qkv_rows + wo_ref.shape[1]
+        for i in range(tail_ref.shape[0]):
+            grad_refs[0][i, start:, :] = tail_ref[i]
     norm_back(x_ref, gain_ref, dx_ref, grad_ref, dx_ref, dgain_ref)
 
 
@@ -261,20 +314,23 @@
     dx_ref[...] = base_ref[...] + inverse * (scaled - unit * jnp.mean(scaled * unit, axis=1, keepdims=True))
 
 
-def attend_back(piece, x, gain, w, wo, vectors, normed, qkv, mixed, lse, grad):
+def attend_back(piece, x, gain, weights, vectors, normed, qkv, mixed, lse, grad, tail=None):
     length, width = x.shape
     heads, span = vectors.shape
+    w_args, w_specs = weight_specs(weights)
+    packed = weights[0]
+    grad_shapes = packed if isinstance(packed, tuple) else (packed,)
+    tails = () if tail is None else (tail,)
     return pl.pallas_call(
-        attend_back_kernel,
-        out_shape=(
-            jax.ShapeDtypeStruct((length, width), F32),
-            jax.ShapeDtypeStruct((3 * width, width), BF),
-            jax.ShapeDtypeStruct((width, width), BF),
+        lambda *refs: attend_back_kernel(bool(tails), weights, *refs),
+        out_shape=(jax.ShapeDtypeStruct((length, width), F32),)
+        + tuple(jax.ShapeDtypeStruct(g.shape, BF) for g in grad_shapes)
+        + (
             jax.ShapeDtypeStruct((heads, span), F32),
             jax.ShapeDtypeStruct((1, width), F32),
         ),
-        in_specs=[SMEM_SPEC] + [VMEM_SPEC] * 10,
-        out_specs=[VMEM_SPEC] * 5,
+        in_specs=[SMEM_SPEC] + [VMEM_SPEC] * 2 + w_specs + [VMEM_SPEC] * (6 + len(tails)),
+        out_specs=[VMEM_SPEC] * (3 + len(grad_shapes)),
         scratch_shapes=[
             pltpu.VMEM((length, length), F32),
             pltpu.VMEM((128, span), F32),
@@ -285,6 +341,9 @@
             pltpu.VMEM((length, width), BF),
             pltpu.VMEM((length, 3 * width), BF),
             pltpu.VMEM((16, length), F32),
+            pltpu.VMEM((3 * width, width), BF),
+            pltpu.VMEM((width, width), BF),
+            pltpu.VMEM((3 * width, width), BF),
         ],
         compiler_params=pltpu.CompilerParams(vmem_limit_bytes=VMEM_BYTES),
         cost_estimate=pl.CostEstimate(
@@ -293,28 +352,39 @@
             transcendentals=heads * length * length,
         ),
         name="attend_back",
-    )(piece, x, gain, w, wo, vectors, normed, qkv, mixed, lse, grad)
-
-
-def mlp_kernel(x_ref, gain_ref, up_ref, down_ref, out_ref, normed_ref):
+    )(piece, x, gain, *w_args, vectors, normed, qkv, mixed, lse, grad, *tails)
+
+
+def mlp_chunk(c, parts, zones, up_ref, down_ref):
+    hidden, width = up_ref.shape
+    piece = hidden // (parts * zones)
+    rows = [
+        up_ref[pl.ds(pl.multiple_of(z * parts * piece + c * piece, 16), piece), :] for z in range(zones)
+    ]
+    span = down_ref.shape[1] // parts
+    down = down_ref[:, pl.ds(pl.multiple_of(c * span, 16), span), :].reshape(-1, down_ref.shape[2])
+    return jnp.concatenate(rows, axis=0), down
+
+
+def mlp_kernel(parts, zones, x_ref, gain_ref, up_ref, down_ref, out_ref, normed_ref):
     field = x_ref[...]
     normed_ref[...] = (field * inverse_rms(field) * gain_ref[...]).astype(BF)
     out_ref[...] = field
 
     def chunk(c, _):
-        at = pl.ds(pl.multiple_of(c * 512, 512), 512)
-        hidden = gelu_of(nt(normed_ref[...], up_ref[at, :])).astype(BF)
-        out_ref[...] += nt(hidden, down_ref[:, at])
-        return 0
-
-    lax.fori_loop(0, up_ref.shape[0] // 512, chunk, 0)
-
-
-def mlp(x, gain, up, down):
+        up, down = mlp_chunk(c, parts, zones, up_ref, down_ref)
+        hidden = gelu_of(nt(normed_ref[...], up)).astype(BF)
+        out_ref[...] += nt(hidden, down)
+        return 0
+
+    lax.fori_loop(0, parts, chunk, 0)
+
+
+def mlp(x, gain, up, down, parts, zones):
     length, width = x.shape
     hidden = up.shape[0]
     return pl.pallas_call(
-        mlp_kernel,
+        lambda *refs: mlp_kernel(parts, zones, *refs),
         out_shape=(jax.ShapeDtypeStruct((length, width), F32), jax.ShapeDtypeStruct((length, width), BF)),
         in_specs=[VMEM_SPEC] * 4,
         out_specs=[VMEM_SPEC] * 2,
@@ -327,33 +397,40 @@
     )(x, gain, up, down)
 
 
-def mlp_back_kernel(x_ref, gain_ref, up_ref, down_ref, normed_ref, grad_ref,
+def mlp_back_kernel(parts, zones, x_ref, gain_ref, up_ref, down_ref, normed_ref, grad_ref,
                     dx_ref, dup_ref, ddown_ref, dgain_ref, low_ref, acc_ref):
     low_ref[...] = grad_ref[...].astype(BF)
     acc_ref[...] = jnp.zeros_like(acc_ref)
 
+    piece = up_ref.shape[0] // (parts * zones)
+    span = down_ref.shape[1] // parts
+
     def chunk(c, _):
-        at = pl.ds(pl.multiple_of(c * 512, 512), 512)
-        hidden, slope = gelu_parts(nt(normed_ref[...], up_ref[at, :]))
-        pre_grad = (nn(low_ref[...], down_ref[:, at]) * slope).astype(BF)
-        ddown_ref[:, at] = tn(low_ref[...], hidden.astype(BF)).astype(BF)
-        dup_ref[at, :] = tn(pre_grad, normed_ref[...]).astype(BF)
-        acc_ref[...] += nn(pre_grad, up_ref[at, :])
-        return 0
-
-    lax.fori_loop(0, up_ref.shape[0] // 512, chunk, 0)
+        up, down = mlp_chunk(c, parts, zones, up_ref, down_ref)
+        hidden, slope = gelu_parts(nt(normed_ref[...], up))
+        pre_grad = (nn(low_ref[...], down) * slope).astype(BF)
+        ddown = tn(low_ref[...], hidden.astype(BF)).astype(BF)
+        ddown_ref[:, pl.ds(pl.multiple_of(c * span, 16), span), :] = ddown.reshape(-1, span, ddown.shape[1])
+        dup = tn(pre_grad, normed_ref[...]).astype(BF)
+        for z in range(zones):
+            at = pl.ds(pl.multiple_of(z * parts * piece + c * piece, 16), piece)
+            dup_ref[at, :] = dup[z * piece:z * piece + piece, :]
+        acc_ref[...] += nn(pre_grad, up)
+        return 0
+
+    lax.fori_loop(0, parts, chunk, 0)
     norm_back(x_ref, gain_ref, acc_ref, grad_ref, dx_ref, dgain_ref)
 
 
-def mlp_back(x, gain, up, down, normed, grad):
+def mlp_back(x, gain, up, down, normed, grad, parts, zones):
     length, width = x.shape
     hidden = up.shape[0]
     return pl.pallas_call(
-        mlp_back_kernel,
+        lambda *refs: mlp_back_kernel(parts, zones, *refs),
         out_shape=(
             jax.ShapeDtypeStruct((length, width), F32),
             jax.ShapeDtypeStruct((hidden, width), BF),
-            jax.ShapeDtypeStruct((width, hidden), BF),
+            jax.ShapeDtypeStruct(down.shape, BF),
             jax.ShapeDtypeStruct((1, width), F32),
         ),
         in_specs=[VMEM_SPEC] * 6,
@@ -527,6 +604,332 @@
     )(slot_columns, rows)
 
 
+MESH = pl.DeviceIdType.MESH
+
+
+def flip(index, mask):
+    bit = 1
+    while bit <= mask:
+        if mask & bit:
+            index = index + bit - 2 * bit * ((index // bit) % 2)
+        bit *= 2
+    return index
+
+
+def masks_of(bits):
+    found = [0]
+    for bit in bits:
+        found = found + [m | bit for m in found]
+    return found
+
+
+def bits_below(size):
+    found, bit = [], 1
+    while bit < size:
+        found.append(bit)
+        bit *= 2
+    return found
+
+
+def halves_of(rows):
+    cut = rows // 2 // 16 * 16
+    return ((0, cut), (cut, rows - cut))
+
+
+def routes_of(chips):
+    bits = bits_below(chips)
+    cut = len(bits) // 2
+    return (bits, bits[cut:] + bits[:cut])
+
+
+def greet(owner, zone, owners, zones):
+    barrier = pltpu.get_barrier_semaphore()
+    peers = [(flip(owner, bit), zone) for bit in bits_below(owners)]
+    peers += [(owner, flip(zone, d)) for d in range(1, zones)]
+    for peer in peers:
+        pl.semaphore_signal(barrier, inc=1, device_id=peer, device_id_type=MESH)
+    pl.semaphore_wait(barrier, len(peers))
+
+
+def sender(send_sem, recv_sem):
+    used = [0]
+
+    def send(source, target, device):
+        at = used[0]
+        used[0] += 1
+        copy = pltpu.make_async_remote_copy(
+            source, target, send_sem.at[at], recv_sem.at[at], device_id=device, device_id_type=MESH
+        )
+        copy.start()
+        return copy
+
+    return send
+
+
+def gather_copies(owners, zones):
+    chips = owners // 2
+    return zones - 1 + 2 * (chips - 1) + 2 * chips
+
+
+def gather_kernel(owners, zones, used_rows, *refs):
+    count = len(used_rows)
+    blocks, outs = refs[:count], refs[count:2 * count]
+    slabs, turned = refs[2 * count:3 * count], refs[3 * count:4 * count]
+    send_sem, recv_sem, local_sem = refs[4 * count:]
+    owner, zone = lax.axis_index("expert"), lax.axis_index("shard")
+    greet(owner, zone, owners, zones)
+    send = sender(send_sem, recv_sem)
+    chips = owners // 2
+    pending, finals = [], []
+
+    def across(g):
+        slabs[g][zone] = blocks[g][...]
+        return [send(blocks[g], slabs[g].at[zone], (owner, flip(zone, d))) for d in range(1, zones)]
+
+    def place(g, index, half):
+        start, size = halves_of(used_rows[g])[half]
+        return outs[g].at[index, pl.ds(start, size), :]
+
+    def onward(g, half, index):
+        finals.append(send(place(g, index, half), place(g, index, half), (flip(owner, 1), zone)))
+
+    def start_rows(g, copies):
+        for copy in copies:
+            copy.wait_recv()
+        pending.extend(copies)
+        slab = slabs[g]
+        turned[g][...] = slab[...].reshape(slab.shape[0] * slab.shape[1], slab.shape[2]).T
+        local = pltpu.make_async_copy(
+            turned[g].at[pl.ds(0, used_rows[g]), :], outs[g].at[owner], local_sem.at[g]
+        )
+        local.start()
+        firsts = []
+        for half, order in enumerate(routes_of(chips)):
+            start, size = halves_of(used_rows[g])[half]
+            source = turned[g].at[pl.ds(start, size), :]
+            firsts.append([send(source, place(g, owner, half), (flip(owner, 2 * order[0]), zone))])
+            finals.append(send(source, place(g, owner, half), (flip(owner, 1), zone)))
+        return firsts, local
+
+    def finish_rows(g, state, step):
+        firsts, local = state
+        if step == 0:
+            local.wait()
+        for half, order in enumerate(routes_of(chips)):
+            for copy in firsts[half]:
+                copy.wait_recv()
+            pending.extend(firsts[half])
+            done = masks_of(order[:step])
+            arrived = [m | order[step] for m in done]
+            if step + 1 < len(order):
+                device = (flip(owner, 2 * order[step + 1]), zone)
+                firsts[half] = [
+                    send(place(g, flip(owner, 2 * m), half), place(g, flip(owner, 2 * m), half), device)
+                    for m in done + arrived
+                ]
+            for m in arrived:
+                onward(g, half, flip(owner, 2 * m))
+        return firsts, local
+
+    steps = len(routes_of(chips)[0])
+    moving = {0: across(0)}
+    states = {}
+    for g in range(count):
+        states[g] = start_rows(g, moving[g])
+        if g + 1 < count:
+            moving[g + 1] = across(g + 1)
+        if g > 0:
+            for step in range(1, steps):
+                states[g - 1] = finish_rows(g - 1, states[g - 1], step)
+        states[g] = finish_rows(g, states[g], 0)
+    for step in range(1, steps):
+        states[count - 1] = finish_rows(count - 1, states[count - 1], step)
+    for copy in finals:
+        copy.wait_recv()
+    for copy in pending + finals:
+        copy.wait_send()
+
+
+def gather_weights(blocks, used_rows, owners, zones):
+    count = len(blocks)
+    depth = zones * blocks[0].shape[0]
+    copies = count * gather_copies(owners, zones)
+    return pl.pallas_call(
+        lambda *refs: gather_kernel(owners, zones, used_rows, *refs),
+        out_shape=tuple(jax.ShapeDtypeStruct((owners, used, depth), BF) for used in used_rows),
+        in_specs=[VMEM_SPEC] * count,
+        out_specs=tuple([pl.BlockSpec(memory_space=pl.ANY)] * count),
+        scratch_shapes=[pltpu.VMEM((zones,) + b.shape, BF) for b in blocks]
+        + [pltpu.VMEM((b.shape[1], depth), BF) for b in blocks]
+        + [pltpu.SemaphoreType.DMA((copies,)), pltpu.SemaphoreType.DMA((copies,)), pltpu.SemaphoreType.DMA((count,))],
+        compiler_params=pltpu.CompilerParams(
+            vmem_limit_bytes=24 * 1024 * 1024, collective_id=1, has_side_effects=True
+        ),
+        name="gather_weights",
+    )(*blocks)
+
+
+def reduce_copies(owners, zones):
+    return 1 + 2 * (owners // 2 - 1) + zones - 1
+
+
+def add_rows(into, other):
+    return (into.astype(F32) + other.astype(F32)).astype(BF)
+
+
+def reduce_kernel(owners, zones, used_rows, *refs):
+    count = len(used_rows)
+    parts, small = refs[:count], refs[count]
+    outs, small_out = refs[count + 1:2 * count + 1], refs[2 * count + 1]
+    scratch = refs[2 * count + 2:]
+    keep, near, far = scratch[:count], scratch[count:2 * count], scratch[2 * count:3 * count]
+    slabs, incoming = scratch[3 * count:4 * count], scratch[4 * count:5 * count]
+    small_mine, small_other, send_sem, recv_sem, local_sem = scratch[5 * count:]
+    owner, zone = lax.axis_index("expert"), lax.axis_index("shard")
+    chip, core = owner // 2, owner % 2
+    greet(owner, zone, owners, zones)
+    send = sender(send_sem, recv_sem)
+    chips = owners // 2
+    orders = routes_of(chips)
+    steps = len(orders[0])
+    sent = []
+    small_peers = [(flip(owner, bit), zone) for bit in bits_below(owners)]
+    small_peers += [(owner, flip(zone, bit)) for bit in bits_below(zones)]
+    small_mine[0] = small[...]
+
+    def small_start(i):
+        return send(small_mine.at[i], small_other.at[i], small_peers[i])
+
+    def small_finish(i, copy):
+        copy.wait_recv()
+        sent.append(copy)
+        small_mine[i + 1] = small_mine[i] + small_other[i]
+
+    def begin(g):
+        local = pltpu.make_async_copy(parts[g].at[:, core], keep[g], local_sem.at[g])
+        local.start()
+        return send(parts[g].at[:, 1 - core], near[g], (flip(owner, 1), zone)), local
+
+    def window(g, half):
+        start, size = halves_of(used_rows[g])[half]
+        return pl.ds(start, size)
+
+    def push(g, step):
+        copies = []
+        for half, order in enumerate(orders):
+            bit, rest = order[step], masks_of(order[step + 1:])
+            device = (flip(owner, 2 * bit), zone)
+            for i, m in enumerate(rest):
+                slot = chips - 2 * len(rest) + i
+                copies.append(send(
+                    keep[g].at[flip(chip, bit | m), window(g, half), :], far[g].at[slot, window(g, half), :], device
+                ))
+        return copies
+
+    def absorb(g, step, copies):
+        for copy in copies:
+            copy.wait_recv()
+        sent.extend(copies)
+        for half, order in enumerate(orders):
+            rest = masks_of(order[step + 1:])
+            for i, m in enumerate(rest):
+                slot = chips - 2 * len(rest) + i
+                index = flip(chip, m)
+                keep[g][index, window(g, half), :] = add_rows(
+                    keep[g][index, window(g, half), :], far[g][slot, window(g, half), :]
+                )
+
+    def stage_near(g, state):
+        copy, local = state
+        local.wait()
+        copy.wait_recv()
+        sent.append(copy)
+
+        def one(h, _):
+            keep[g][h] = add_rows(keep[g][h], near[g][h])
+            return 0
+
+        lax.fori_loop(0, chips, one, 0)
+        return push(g, 0)
+
+    def stage_zone(g):
+        slab = slabs[g]
+        spare = slab.shape[2] - used_rows[g]
+        own = keep[g][chip]
+        if spare:
+            own = jnp.concatenate([own, jnp.zeros((spare, own.shape[1]), BF)], axis=0)
+        slab[...] = own.T.reshape(slab.shape)
+        return [
+            send(slab.at[flip(zone, d)], incoming[g].at[d - 1], (owner, flip(zone, d))) for d in range(1, zones)
+        ]
+
+    def stage_end(g, copies):
+        total = slabs[g][zone].astype(F32)
+        for d in range(1, zones):
+            copies[d - 1].wait_recv()
+            total = total + incoming[g][d - 1].astype(F32)
+        sent.extend(copies)
+        outs[g][...] = total
+
+    begun = [begin(g) for g in range(count)]
+    small_copy = small_start(0)
+    state = {}
+    stages = steps + 2
+    turn = 0
+    for t in range(count + stages - 1):
+        for g in reversed(range(count)):
+            at = t - g
+            if at == 0:
+                state[g] = stage_near(g, begun[g])
+            elif 1 <= at <= steps:
+                absorb(g, at - 1, state[g])
+                state[g] = push(g, at) if at < steps else stage_zone(g)
+            elif at == steps + 1:
+                stage_end(g, state[g])
+        if turn < len(small_peers):
+            small_finish(turn, small_copy)
+            turn += 1
+            if turn < len(small_peers):
+                small_copy = small_start(turn)
+    while turn < len(small_peers):
+        small_finish(turn, small_copy)
+        turn += 1
+        if turn < len(small_peers):
+            small_copy = small_start(turn)
+    small_out[...] = small_mine[len(small_peers)]
+    for copy in sent:
+        copy.wait_send()
+
+
+def reduce_grads(parts, small, owners, zones):
+    count = len(parts)
+    used_rows = tuple(p.shape[1] for p in parts)
+    depth = parts[0].shape[2]
+    chips = owners // 2
+    parts = [p.reshape(chips, 2, p.shape[1], depth) for p in parts]
+    wide = [-(-used // 128) * 128 for used in used_rows]
+    rounds = len(bits_below(owners)) + len(bits_below(zones))
+    copies = count * reduce_copies(owners, zones) + rounds
+    return pl.pallas_call(
+        lambda *refs: reduce_kernel(owners, zones, used_rows, *refs),
+        out_shape=tuple(jax.ShapeDtypeStruct((depth // zones, w), F32) for w in wide)
+        + (jax.ShapeDtypeStruct(small.shape, F32),),
+        in_specs=[pl.BlockSpec(memory_space=pl.ANY)] * count + [VMEM_SPEC],
+        out_specs=tuple([VMEM_SPEC] * (count + 1)),
+        scratch_shapes=[pltpu.VMEM((chips, used, depth), BF) for used in used_rows]
+        + [pltpu.VMEM((chips, used, depth), BF) for used in used_rows]
+        + [pltpu.VMEM((chips - 1, used, depth), BF) for used in used_rows]
+        + [pltpu.VMEM((zones, depth // zones, w), BF) for w in wide]
+        + [pltpu.VMEM((zones - 1, depth // zones, w), BF) for w in wide]
+        + [pltpu.VMEM((rounds + 1,) + small.shape, F32), pltpu.VMEM((rounds,) + small.shape, F32)]
+        + [pltpu.SemaphoreType.DMA((copies,)), pltpu.SemaphoreType.DMA((copies,)), pltpu.SemaphoreType.DMA((count,))],
+        compiler_params=pltpu.CompilerParams(
+            vmem_limit_bytes=VMEM_BYTES, collective_id=2, has_side_effects=True
+        ),
+        name="reduce_grads",
+    )(*parts, small)
+
+
 bucket_edges = (1, 2, 3, 4, 6, 8, 12, 16, 24, 32, 48, 64, 96, 128, 192, 256, 384, 512, 768, 1024, 1536)
 
 
@@ -566,26 +969,8 @@
     return lax.ppermute(value, "shard", [(z, z ^ 1) for z in range(lax.axis_size("shard"))])
 
 
-def total_over_mesh(value):
-    for name in ("shard", "expert"):
-        size = lax.axis_size(name)
-        step = 1
-        while step < size:
-            value = value + lax.ppermute(value, name, [(i, i ^ step) for i in range(size)])
-            step *= 2
-    return value
-
-
 def exchange(value):
     return lax.all_to_all(value, "expert", split_axis=0, concat_axis=0, tiled=True)
-
-
-def gather_rows(value, name):
-    return lax.all_gather(value, name, axis=0, tiled=True)
-
-
-def scatter_rows(value, name):
-    return lax.psum_scatter(value, name, scatter_dimension=0, tiled=True)
 
 
 def per_device(
@@ -599,32 +984,41 @@
     experts_all = local * owners
     capacity = 3 * routes.shape[1] * length // (2 * experts_all)
     qkv_cols, out_cols = qkv_weight.shape[2], out_weight.shape[2]
+    zones_all = 2 * zones
     router_pad = 16
-
-    def router_block(part):
-        return jnp.pad(part, ((0, 0), (0, router_pad - part.shape[1])))
-
-    first = gather_rows(jnp.concatenate([qkv_weight[0], out_weight[0]], axis=1), "shard").T
-    middle = gather_rows(mlp_up, "shard").T
-    lower = gather_rows(mlp_down, "shard").T
-    last = gather_rows(
-        jnp.concatenate([qkv_weight[1], out_weight[1], router_block(router)], axis=1), "shard"
-    ).T
-    first = gather_rows(first, "expert").reshape(owners, qkv_cols + out_cols, width)
-    up_full = gather_rows(middle, "expert")
-    down_full = gather_rows(lower, "expert")
-    last = gather_rows(last, "expert").reshape(owners, qkv_cols + out_cols + router_pad, width)
-
-    def qkv_of(block):
-        return block[:, :qkv_cols].reshape(-1, width)
-
-    def out_of(block):
-        return block[:, qkv_cols:qkv_cols + out_cols].reshape(-1, width)
-
+    parts = mlp_down.shape[0] // qkv_weight.shape[1]
+    aligned = qkv_cols % 16 == 0 and out_cols % 16 == 0 and qkv_cols % out_cols == 0
+
+    def padded(block):
+        return jnp.pad(block, ((0, 0), (0, -block.shape[1] % 128)))
+
+    down_block = mlp_down.reshape(parts, -1, mlp_down.shape[1]).transpose(1, 0, 2).reshape(qkv_weight.shape[1], -1)
+    router_block = jnp.pad(router, ((0, 0), (0, router_pad - router.shape[1])))
+    first, up_full, down_full, last = gather_weights(
+        [
+            padded(jnp.concatenate([qkv_weight[0], out_weight[0]], axis=1)),
+            padded(mlp_up),
+            padded(down_block),
+            padded(jnp.concatenate([qkv_weight[1], out_weight[1], router_block], axis=1)),
+        ],
+        (qkv_cols + out_cols, mlp_up.shape[1], parts * mlp_down.shape[1], qkv_cols + out_cols + router_pad),
+        owners, zones_all,
+    )
+
+    def layer_weights(block):
+        if aligned:
+            return (block, qkv_cols, out_cols)
+        flat = (block[:, :qkv_cols].reshape(1, -1, width), block[:, qkv_cols:qkv_cols + out_cols].reshape(1, -1, width))
+        return (flat, 3 * width, width)
+
+    up_full = up_full.reshape(-1, width)
+    if mlp_down.shape[1] % 16:
+        down_full = down_full.reshape(owners, parts, -1, width).transpose(1, 0, 2, 3).reshape(1, -1, width)
     router_full = last[:, qkv_cols + out_cols:qkv_cols + out_cols + router.shape[1]].reshape(experts_all, width)
 
-    up_pair = jnp.stack([expert_up, swap_pair(expert_up)])
-    down_pair = jnp.stack([expert_down, swap_pair(expert_down)])
+    first, cotangent_late, down_late = lax.optimization_barrier((first, cotangent, expert_down))
+    weights0, weights1 = layer_weights(first), layer_weights(last)
+    up_other, down_other = swap_pair(expert_up), swap_pair(down_late)
 
     slots = expert_slots(routes, experts_all, capacity)
     zone_slots = [slots] + [shift_from(slots, 2 * d) for d in range(1, zones)]
@@ -640,7 +1034,7 @@
         back = exchange(rows).reshape(experts_all, zones, capacity, width)
         return collect(slot_columns, back)
 
-    cotangent_rows = dispatch(cotangent)
+    cotangent_rows = dispatch(cotangent_late)
 
     onehot = bucket_onehot(length, bias_tables.shape[2])
     vectors = lax.dot_general(
@@ -648,10 +1042,14 @@
     )
     gains = [norm_gains[i:i + 1] for i in range(4)]
     x0 = tokens.astype(F32)
-    x1, ah0, qkv0, o0, lse0 = attend(piece_start, x0, gains[0], qkv_of(first), out_of(first), vectors[0])
-    x2, mh = mlp(x1, gains[1], up_full, down_full)
-    x3, ah1, qkv1, o1, lse1 = attend(piece_start, x2, gains[2], qkv_of(last), out_of(last), vectors[1])
-
+    x1, ah0, qkv0, o0, lse0 = attend(piece_start, x0, gains[0], weights0, vectors[0])
+    x1, up_other = lax.optimization_barrier((x1, up_other))
+    x2, mh = mlp(x1, gains[1], up_full, down_full, parts, zones_all)
+    x3, ah1, qkv1, o1, lse1 = attend(piece_start, x2, gains[2], weights1, vectors[1])
+
+    x3, down_other, cotangent_rows = lax.optimization_barrier((x3, down_other, cotangent_rows))
+    up_pair = jnp.stack([expert_up, up_other])
+    down_pair = jnp.stack([expert_down, down_other])
     unit3 = x3 * inverse_rms(x3)
     eh = (unit3 * gains[3]).astype(BF)
     logits = nt(eh, router_full)
@@ -673,8 +1071,7 @@
     y_rows, dx_rows, dgate_rows, own_up, own_down, peer_up, peer_down = run_experts(
         eh_rows, cotangent_rows, gate_rows[..., None], up_pair, down_pair
     )
-    grad_up = own_up + swap_pair(peer_up).astype(F32)
-    grad_down = own_down + swap_pair(peer_down).astype(F32)
+    peer_up, peer_down = swap_pair(peer_up), swap_pair(peer_down)
 
     dx_back = undo(dx_rows)
     dgate_back = exchange(dgate_rows[..., 0]).reshape(experts_all, zones, capacity)
@@ -686,12 +1083,6 @@
         gate_grad = gate_grad + (part if d == 0 else shift_to(part, 2 * d))
     for d in range(1, zones):
         token_grad = token_grad + shift_to(dx_back[d].astype(BF), 2 * d).astype(F32)
-    y_back = undo(y_rows)
-    final = x3 + y_back[0]
-    for d in range(1, zones):
-        final = final + shift_to(y_back[d].astype(BF), 2 * d).astype(F32)
-    output = final.astype(BF)
-
     c = cotangent.astype(F32)
     dchoice = gates * (gate_grad - jnp.sum(gates * gate_grad, axis=1, keepdims=True))
     dlogits = jnp.sum(jnp.where(chosen, dchoice[:, :, None], 0.0), axis=1).astype(BF)
@@ -701,41 +1092,65 @@
     dx3 = c + inverse_rms(x3) * (scaled - unit3 * jnp.mean(scaled * unit3, axis=1, keepdims=True))
     dgain3 = jnp.sum(deh * unit3, axis=0)[None]
 
-    dx2, dqkv1, dout1, dvec1, dgain2 = attend_back(
-        piece_start, x2, gains[2], qkv_of(last), out_of(last), vectors[1], ah1, qkv1, o1, lse1, dx3
-    )
-    dx1, dup, ddown, dgain1 = mlp_back(x1, gains[1], up_full, down_full, mh, dx2)
-    dx0, dqkv0, dout0, dvec0, dgain0 = attend_back(
-        piece_start, x0, gains[0], qkv_of(first), out_of(first), vectors[0], ah0, qkv0, o0, lse0, dx1
-    )
-
-    def reduce_block(parts):
-        block = jnp.concatenate([p.reshape(owners, -1, p.shape[-1]) for p in parts], axis=1)
-        rows = block.shape[1]
-        mine = scatter_rows(block.reshape(owners * rows, block.shape[2]), "expert")
-        return scatter_rows(mine.T, "shard").astype(F32)
-
     router_rows = jnp.pad(
         grad_router.astype(BF).reshape(owners, local, width), ((0, 0), (0, router_pad - local), (0, 0))
     )
-    last_grad = reduce_block([dqkv1, dout1, router_rows])
-    grad_mlp_up = reduce_block([dup])
-    grad_mlp_down = reduce_block([ddown])
-    first_grad = reduce_block([dqkv0, dout0])
-    grad_qkv = jnp.stack([first_grad[:, :qkv_cols], last_grad[:, :qkv_cols]])
-    grad_out = jnp.stack([first_grad[:, qkv_cols:], last_grad[:, qkv_cols:qkv_cols + out_cols]])
-    grad_router_out = last_grad[:, qkv_cols + out_cols:qkv_cols + out_cols + local]
-
+
+    def layer_grads(results, tail=None):
+        grads = results[1:-2]
+        if not aligned:
+            pieces = [g.reshape(owners, -1, width) for g in grads] + ([] if tail is None else [tail])
+            grads = [jnp.concatenate(pieces, axis=1)]
+        return results[0], grads[0], results[-2], results[-1]
+
+    dx2, last_part, dvec1, dgain2 = layer_grads(
+        attend_back(
+            piece_start, x2, gains[2], weights1, vectors[1], ah1, qkv1, o1, lse1, dx3, router_rows if aligned else None
+        ),
+        router_rows,
+    )
+    dx2, y_rows = lax.optimization_barrier((dx2, y_rows))
+    y_back = undo(y_rows)
+    final = x3 + y_back[0]
+    for d in range(1, zones):
+        final = final + shift_to(y_back[d].astype(BF), 2 * d).astype(F32)
+    output = final.astype(BF)
+    dx1, up_part, down_part, dgain1 = mlp_back(x1, gains[1], up_full, down_full, mh, dx2, parts, zones_all)
+    dx0, first_part, dvec0, dgain0 = layer_grads(
+        attend_back(piece_start, x0, gains[0], weights0, vectors[0], ah0, qkv0, o0, lse0, dx1)
+    )
+    dx0, output, peer_up, peer_down = lax.optimization_barrier((dx0, output, peer_up, peer_down))
+    grad_up = own_up + peer_up.astype(F32)
+    grad_down = own_down + peer_down.astype(F32)
+    if mlp_down.shape[1] % 16:
+        down_part = down_part.reshape(parts, owners, -1, width).transpose(1, 0, 2, 3)
     dtables = lax.dot_general(
         jnp.stack([dvec0, dvec1]), onehot, (((2,), (0,)), ((), ())), precision=lax.Precision.HIGHEST
     )
     dgains = jnp.concatenate([dgain0, dgain1, dgain2, dgain3])
-    small = total_over_mesh(jnp.concatenate([dgains.reshape(-1), dtables.reshape(-1)]))
+    small = jnp.concatenate([dgains.reshape(-1), dtables.reshape(-1)])
+    small = jnp.pad(small, (0, -small.size % 1024)).reshape(-1, 128)
+    last_grad, up_grad, down_grad, first_grad, small = reduce_grads(
+        [
+            last_part, up_part.reshape(owners, -1, width), down_part.reshape(owners, -1, width), first_part
+        ],
+        small, owners, zones_all,
+    )
+    small = small.reshape(-1)
+    grad_qkv = jnp.stack([first_grad[:, :qkv_cols], last_grad[:, :qkv_cols]])
+    grad_out = jnp.stack(
+        [first_grad[:, qkv_cols:qkv_cols + out_cols], last_grad[:, qkv_cols:qkv_cols + out_cols]]
+    )
+    grad_router_out = last_grad[:, qkv_cols + out_cols:qkv_cols + out_cols + local]
+    grad_mlp_up = up_grad[:, :mlp_up.shape[1]]
+    down_cols = mlp_down.shape[1]
+    grad_mlp_down = down_grad[:, :parts * down_cols].reshape(-1, parts, down_cols).transpose(1, 0, 2)
+    grad_mlp_down = grad_mlp_down.reshape(mlp_down.shape)
     return (
         output,
         dx0,
         small[:dgains.size].reshape(dgains.shape),
-        small[dgains.size:].reshape(dtables.shape),
+        small[dgains.size:dgains.size + dtables.size].reshape(dtables.shape),
         grad_qkv,
         grad_out,
         grad_mlp_up,

time: 1060 us -> 835 us (0.79)
  waiting for transfers between devices: 516 us -> 255 us
  Pallas kernels: 242 us -> 450 us
  blocking collectives: 140 us -> 7.12 us
  local copies, waits for them, and re-layouts: 50.9 us -> 36.9 us
  between operations: 15.7 us -> 2.17 us
    pallas_call x6 -> x8, Pallas kernels: 139 us -> 348 us  [the longest x1 107 us: reduce_grads(): pl.pallas_call(lambda *refs: reduce_kernel(owners, zones, used_rows, *ref...]
    reduce_scatter x5 -> x0, waiting for transfers between devices: 200 us -> none  [scatter_rows(): return lax.psum_scatter(value, name, scatter_dimension=0, tiled=True)]
    all_gather x4 -> x0, blocking collectives: 72.9 us -> none  [gather_rows(): return lax.all_gather(value, name, axis=0, tiled=True)]
    all_to_all x4 -> x5, waiting for transfers between devices: 35.2 us -> 96.3 us  [exchange(): lax.all_to_all(value, 'expert', split_axis=0, concat_axis=0, tiled=True)]
    all_to_all x2 -> x1, blocking collectives: 67.6 us -> 7.12 us  [exchange(): lax.all_to_all(value, 'expert', split_axis=0, concat_axis=0, tiled=True)]
    ppermute x4, waiting for transfers between devices: 97.9 us -> 48.8 us  [swap_pair(): lax.ppermute(value, 'shard', [(z, z ^ 1) for z in range(lax.axis_size('sh...]
    unnamed x15 -> x0, waiting for transfers between devices: 43.8 us -> none
    all_gather x4 -> x0, waiting for transfers between devices: 40.8 us -> none  [gather_rows(): return lax.all_gather(value, name, axis=0, tiled=True)]
  transfers between devices with their start and end apart: 32 -> 16, of which waited for: 19 -> 7; matrix products, arithmetic and copies ran while one was open for 8% -> 5% of each run, Pallas kernels for 11% -> 29%
where the time goes in v2:
time: 835 us; the launch traced here: 828 us
  Pallas kernels  450 us (54%)
  waiting for transfers between devices  255 us (31%)
  local copies, waits for them, and re-layouts  36.9 us (4%)
  starting transfers between devices  36.4 us (4%)
  other arithmetic  36.1 us (4%)
    pallas_call x1, Pallas kernels, reduce_grads(): pl.pallas_call(lambda *refs: reduce_kernel(owners, zones, used_rows, *ref...  107 us
    pallas_call x1, Pallas kernels, gather_weights(): pl.pallas_call(lambda *refs: gather_kernel(owners, zones, used_rows, *ref...  98.7 us
    all_to_all x5, waiting for transfers between devices, exchange(): lax.all_to_all(value, 'expert', split_axis=0, concat_axis=0, tiled=True)  96.3 us
    ppermute x4, waiting for transfers between devices, shift_from(): lax.ppermute(value, 'shard', [((z + distance) % size, z) for z in range(s...  77.5 us
    pallas_call x2, Pallas kernels, attend_back(): pl.pallas_call(lambda *refs: attend_back_kernel(bool(tails), weights, *re...  70.8 us
    pallas_call x1, Pallas kernels, run_experts(): pl.pallas_call(experts_kernel, grid=(local, 2), out_shape=(jax.ShapeDtype...  70.6 us
    ppermute x4, waiting for transfers between devices, swap_pair(): lax.ppermute(value, 'shard', [(z, z ^ 1) for z in range(lax.axis_size('sh...  48.8 us
    pallas_call x2, Pallas kernels, attend(): pl.pallas_call(lambda *refs: attend_kernel(weights, *refs), out_shape=(ja...  36.8 us
  transfers between devices with their start and end apart: 16, of which 7 were waited for; matrix products, arithmetic and copies ran while one was open for 5% of the time, Pallas kernels for 29%

profile of v2, /device:TPU:0, one launch (start us, length us, event | category | flops | bytes accessed | tf_op | source)
XLA Modules:
  0.0 827.9 jit_solution(16138901688976457797)
XLA Ops:
  5.2 98.7 %gather_weights.1 = (bf16[8,384,768]{2,1,0:T(8,128)(2,1)S(1)}, bf16[8,384,768]{2,1,0:T(8,128)(2,1)S(1)}, bf16[8,384,768]{2,1,0:T(8,128)(2,1)S(1)}, bf16[8,400,768]{2,1,0:T(8,128)(2,1)S(1)}) custom-call(bf16[192,384]{1,0:T(8,128)(2,1)S(1)} %pad_maximum_fusion.6.refs_0_, bf16[192,384]{1,0:T(8,128)(2,1)S(1)} %copy-done.2, ...), custom_call_target="tpu_custom_call" | custom-call | tf_op jit(solution)/shard_map/gather_weights/pallas_call | solution.py:757
  118.1 44.9 %collective-permute-done.2 = s32[512,2]{1,0:T(8,128)S(1)} collective-permute-done((s32[512,2]{1,0:T(8,128)S(1)}, s32[512,2]{1,0:T(8,128)S(1)}, u32[]{:S(2)}, u32[]{:S(2)}) %collective-permute-start.2) | collective-permute-done | bytes 4128 | tf_op jit(solution)/shard_map/ppermute | solution.py:960
  165.2 6.8 spread.2
  183.8 18.4 %attend.2 = (f32[512,768]{1,0:T(8,128)}, bf16[512,768]{1,0:T(8,128)(2,1)}, bf16[512,2304]{1,0:T(8,128)(2,1)}, bf16[512,768]{1,0:T(8,128)(2,1)}, f32[12,512]{1,0:T(8,128)}) custom-call(s32[1]{0:T(128)S(6)} %copy.121.refs_0_, f32[512,768]{1,0:T(8,128)} %convert_element_type.62.refs_1_, f32[1,768]{1,0:T(1,128)} %get-tuple-element.199.refs_2_, ...), custom_call_target="tpu_custom_call" | custom-call | flops 3221225472 | bytes 12582912 | tf_op jit(solution)/shard_map/attend/pallas_call | solution.py:159
  202.3 29.2 %collective-permute-done = bf16[2,768,768]{2,1,0:T(8,128)(2,1)} collective-permute-done((bf16[2,768,768]{2,1,0:T(8,128)(2,1)}, bf16[2,768,768]{2,1,0:T(8,128)(2,1)}, u32[]{:S(2)}, u32[]{:S(2)}) %collective-permute-start) | collective-permute-done | bytes 2359328 | tf_op jit(solution)/shard_map/ppermute | solution.py:969
  231.5 12.0 %mlp.1 = (f32[512,768]{1,0:T(8,128)}, bf16[512,768]{1,0:T(8,128)(2,1)}) custom-call(f32[512,768]{1,0:T(8,128)} %get-tuple-element.72.refs_0_, f32[1,768]{1,0:T(1,128)} %get-tuple-element.198.refs_1_, bf16[3072,768]{1,0:T(8,128)(2,1)} %bitcast.82, bf16[8,384,768]{2,1,0:T(8,128)(2,1)} %copy-done.6), custom_call_target="tpu_custom_call" | custom-call | flops 4831838208 | bytes 13369344 | tf_op jit(solution)/shard_map/mlp/pallas_call | solution.py:386
  243.5 18.4 %attend.3 = (f32[512,768]{1,0:T(8,128)}, bf16[512,768]{1,0:T(8,128)(2,1)}, bf16[512,2304]{1,0:T(8,128)(2,1)}, bf16[512,768]{1,0:T(8,128)(2,1)}, f32[12,512]{1,0:T(8,128)}) custom-call(s32[1]{0:T(128)S(6)} %copy.121.refs_0_, f32[512,768]{1,0:T(8,128)} %get-tuple-element.76.refs_1_, f32[1,768]{1,0:T(1,128)} %get-tuple-element.200.refs_2_, ...), custom_call_target="tpu_custom_call" | custom-call | flops 3221225472 | bytes 12582912 | tf_op jit(solution)/shard_map/attend/pallas_call | solution.py:159
  261.9 19.7 %collective-permute-done.1 = bf16[2,768,768]{2,1,0:T(8,128)(2,1)} collective-permute-done((bf16[2,768,768]{2,1,0:T(8,128)(2,1)}, bf16[2,768,768]{2,1,0:T(8,128)(2,1)}, u32[]{:S(2)}, u32[]{:S(2)}) %collective-permute-start.1) | collective-permute-done | bytes 2359328 | tf_op jit(solution)/shard_map/ppermute | solution.py:969
  288.1 32.6 %collective-permute-done.5 = f32[512,2]{0,1:T(2,128)S(1)} collective-permute-done((f32[512,2]{0,1:T(2,128)S(1)}, f32[512,2]{0,1:T(2,128)S(1)}, u32[]{:S(2)}, u32[]{:S(2)}) %collective-permute-start.5) | collective-permute-done | bytes 4128 | tf_op jit(solution)/shard_map/ppermute | solution.py:960
  328.5 6.7 spread.3
  335.2 5.1 all-to-all-start.1
  351.3 43.8 %all-to-all-done.1.x_ref = bf16[8,2,192,768]{3,2,1,0:T(8,128)(2,1)} async-done(((bf16[8,2,192,768]{3,2,1,0:T(8,128)(2,1)}), bf16[8,2,192,768]{3,2,1,0:T(8,128)(2,1)}, u32[]{:S(2)}, u32[]{:S(2)}) %all-to-all-start.1) | async-done | bytes 4718624 | tf_op jit(solution)/shard_map/all_to_all | solution.py:973
  395.0 70.6 %experts.1 = (bf16[8,2,192,768]{3,2,1,0:T(8,128)(2,1)}, bf16[8,2,192,768]{3,2,1,0:T(8,128)(2,1)}, f32[8,2,192,1]{3,2,1,0:T(8,128)}, f32[2,768,768]{2,1,0:T(8,128...) custom-call(bf16[8,2,192,768]{3,2,1,0:T(8,128)(2,1)} %all-to-all-done.1.x_ref, ...), custom_call_target="tpu_custom_call" | custom-call | flops 43486543872 | bytes 37748736 | tf_op jit(solution)/shard_map/experts/pallas_call | solution.py:512
  467.7 7.1 all_to_all.30
  481.8 52.5 %all-to-all-done.3 = bf16[8,2,192,768]{3,2,1,0:T(8,128)(2,1)} async-done(((bf16[8,2,192,768]{3,2,1,0:T(8,128)(2,1)}), bf16[8,2,192,768]{3,2,1,0:T(8,128)(2,1)}, u32[]{:S(2)}, u32[]{:S(2)}) %all-to-all-start.3) | async-done | bytes 4718624 | tf_op jit(solution)/shard_map/all_to_all | solution.py:973
  534.3 8.7 %collect.2 = f32[2,512,768]{2,1,0:T(8,128)} custom-call(s32[512,4]{1,0:T(8,128)} %copy-done.12, bf16[16,2,96,768]{3,2,1,0:T(8,128)(2,1)} %bitcast.22.rows_ref), custom_call_target="tpu_custom_call" | custom-call | flops 2415919104 | bytes 7864320 | tf_op jit(solution)/shard_map/collect/pallas_call | solution.py:593
  546.4 32.0 %collective-permute-done.6 = bf16[512,768]{1,0:T(8,128)(2,1)S(1)} collective-permute-done((bf16[512,768]{1,0:T(8,128)(2,1)}, bf16[512,768]{1,0:T(8,128)(2,1)S(1)}, u32[]{:S(2)}, u32[]{:S(2)}) %collective-permute-start.6) | collective-permute-done | bytes 786464 | tf_op jit(solution)/shard_map/ppermute | solution.py:965
  582.1 35.4 %attend_back.2 = (f32[512,768]{1,0:T(8,128)}, bf16[8,400,768]{2,1,0:T(8,128)(2,1)}, f32[12,1024]{1,0:T(8,128)}, f32[1,768]{1,0:T(1,128)}) custom-call(s32[1]{0:T(128)S(6)} %copy.121.refs_0_, f32[512,768]{1,0:T(8,128)} %get-tuple-element.76.refs_1_, f32[1,768]{1,0:T(1,128)} %get-tuple-element.200.refs_2_, bf16[8,400,768]{2,1,0:T(8,128)(2,1)} %copy-done.3, ...), custom_call_target="tpu_custom_call" | custom-call | flops 6845104128 | bytes 25165824 | tf_op jit(solution)/shard_map/attend_back/pallas_call | solution.py:324
  617.6 5.2 all-to-all-start.5
  624.9 23.0 %mlp_back.1 = (f32[512,768]{1,0:T(8,128)}, bf16[3072,768]{1,0:T(8,128)(2,1)}, bf16[8,384,768]{2,1,0:T(8,128)(2,1)}, f32[1,768]{1,0:T(1,128)}) custom-call(f32[512,768]{1,0:T(8,128)} %get-tuple-element.72.refs_0_, f32[1,768]{1,0:T(1,128)} %get-tuple-element.198.refs_1_, bf16[3072,768]{1,0:T(8,128)(2,1)} %bitcast.83, bf16[8,384,768]{2,1,0:T(8,128)(2,1)} %copy-done.6, ...), custom_call_target="tpu_custom_call" | custom-call | flops 12079595520 | bytes 25165824 | tf_op jit(solution)/shard_map/mlp_back/pallas_call | solution.py:428
  647.9 35.3 %attend_back.3 = (f32[512,768]{1,0:T(8,128)}, bf16[8,384,768]{2,1,0:T(8,128)(2,1)}, f32[12,1024]{1,0:T(8,128)}, f32[1,768]{1,0:T(1,128)}) custom-call(s32[1]{0:T(128)S(6)} %copy.121.refs_0_, f32[512,768]{1,0:T(8,128)} %convert_element_type.62.refs_1_, f32[1,768]{1,0:T(1,128)} %get-tuple-element.199.refs_2_, bf16[8,384,768]{2,1,0:T(8,128)(2,1)} %copy-done.4, ...), custom_call_target="tpu_custom_call" | custom-call | flops 6845104128 | bytes 25165824 | tf_op jit(solution)/shard_map/attend_back/pallas_call | solution.py:324
  685.1 8.9 %collect.3 = f32[2,512,768]{2,1,0:T(8,128)} custom-call(s32[512,4]{1,0:T(8,128)} %copy-done.12, bf16[16,2,96,768]{3,2,1,0:T(8,128)(2,1)} %bitcast.26.rows_ref), custom_call_target="tpu_custom_call" | custom-call | flops 2415919104 | bytes 7864320 | tf_op jit(solution)/shard_map/collect/pallas_call | solution.py:593
  698.1 107.2 %reduce_grads.1 = (f32[192,512]{1,0:T(8,128)}, f32[192,384]{1,0:T(8,128)}, f32[192,384]{1,0:T(8,128)}, f32[192,384]{1,0:T(8,128)}, f32[40,128]{1,0:T(8,128)}) custom-call(bf16[4,2,400,768]{3,2,1,0:T(8,128)(2,1)} %bitcast.84, bf16[4,2,384,768]{3,2,1,0:T(8,128)(2,1)} %bitcast.87, bf16[4,2,384,768]{3,2,1,0:T(8,128)(2,1)} %bitcast.88, ...), custom_call_target="tpu_custom_call" | custom-call | tf_op jit(solution)/shard_map/reduce_grads/pallas_call | solution.py:913
  817.1 9.8 %convert_add_fusion = (f32[2,768,768]{2,1,0:T(8,128)}, f32[2,768,768]{2,1,0:T(8,128)}) fusion(f32[2,768,768]{2,1,0:T(8,128)} %get-tuple-element.117, bf16[2,768,768]{2,1,0:T(8,128)(2,1)} %collective-permute-done.10, f32[2,768,768]{2,1,0:T(8,128)} %get-tuple-element.115, bf16[2,768,768]{2,1,0:T(8,128)(2,1)} %collective-permute-done.9), kind=kLoop, calls=%fused_computation.8 | loop fusion | flops 4718592 | bytes 23592960 | tf_op jit(solution)/shard_map/add | solution.py:1124
  (160 shorter events, 93.8 us)
Async XLA Ops:
  0.6 182.3 %copy-start = (f32[2,12,44]{2,0,1:T(2,128)S(1)}, f32[2,12,44]{2,0,1:T(2,128)}, u32[]{:S(2)}) copy-start(f32[2,12,44]{2,0,1:T(2,128)} %param.18) | copy-start | bytes 12676
  0.7 111.9 %copy-start.8 = (bf16[512,768]{1,0:T(8,128)(2,1)S(1)}, bf16[512,768]{1,0:T(8,128)(2,1)}, u32[]{:S(2)}) copy-start(bf16[512,768]{1,0:T(8,128)(2,1)} %param.26) | copy-start | bytes 2359300
  0.7 116.1 %copy-start.16 = (s32[512,2]{0,1:T(2,128)S(1)}, s32[512,2]{0,1:T(2,128)}, u32[]{:S(2)}) copy-start(s32[512,2]{0,1:T(2,128)} %param.16) | copy-start | bytes 12292
  112.6 51.3 %collective-permute-start.3 = (bf16[512,768]{1,0:T(8,128)(2,1)S(1)}, bf16[512,768]{1,0:T(8,128)(2,1)S(1)}, u32[]{:S(2)}, u32[]{:S(2)}) collective-permute-start(bf16[512,768]{1,0:T(8,128)(2,1)S(1)} %copy-done.8), channel_id=1, source_target_pairs={{2,0},{3,1},{0,2},{1,3},{6,4},{7,5},{4,6},{5,7},{10,8},{11,9},{8,1... | collective-permute-start | bytes 2359304 | tf_op jit(solution)/shard_map/ppermute | solution.py:960
  118.0 45.0 %collective-permute-start.2 = (s32[512,2]{1,0:T(8,128)S(1)}, s32[512,2]{1,0:T(8,128)S(1)}, u32[]{:S(2)}, u32[]{:S(2)}) collective-permute-start(s32[512,2]{1,0:T(8,128)S(1)} %add.55), channel_id=1, source_target_pairs={{2,0},{3,1},{0,2},{1,3},{6,4},{7,5},{4,6},{5,7},{10,8},{11,9},{8,1... | collective-permute-start | bytes 12296 | tf_op jit(solution)/shard_map/ppermute | solution.py:960
  172.0 109.6 %all-to-all-start = ((bf16[8,2,192,768]{3,2,1,0:T(8,128)(2,1)}), bf16[8,2,192,768]{3,2,1,0:T(8,128)(2,1)}, u32[]{:S(2)}, u32[]{:S(2)}) async-start(bf16[8,2,192,768]{3,2,1,0:T(8,128)(2,1)} %bitcast.85), calls=%async_computation | async-start | bytes 9437184 | tf_op jit(solution)/shard_map/all_to_all | solution.py:973
  177.1 54.4 %collective-permute-start = (bf16[2,768,768]{2,1,0:T(8,128)(2,1)}, bf16[2,768,768]{2,1,0:T(8,128)(2,1)}, u32[]{:S(2)}, u32[]{:S(2)}) collective-permute-start(bf16[2,768,768]{2,1,0:T(8,128)(2,1)} %param.24), channel_id=1, source_target_pairs={{0,1},{1,0},{2,3},{3,2},{4,5},{5,4},{6,7},{7,6},{8,9},{9,8},{10,11... | collective-permute-start | bytes 7077896 | tf_op jit(solution)/shard_map/ppermute | solution.py:969
  177.1 104.5 %collective-permute-start.1 = (bf16[2,768,768]{2,1,0:T(8,128)(2,1)}, bf16[2,768,768]{2,1,0:T(8,128)(2,1)}, u32[]{:S(2)}, u32[]{:S(2)}) collective-permute-start(bf16[2,768,768]{2,1,0:T(8,128)(2,1)} %param.25), channel_id=1, source_target_pairs={{0,1},{1,0},{2,3},{3,2},{4,5},{5,4},{6,7},{7,6},{8,9},{9,8},{10,11... | collective-permute-start | bytes 7077896 | tf_op jit(solution)/shard_map/ppermute | solution.py:969
  261.9 21.3 %copy-start.7 = (f32[512,768]{1,0:T(8,128)S(1)}, f32[512,768]{1,0:T(8,128)}, u32[]{:S(2)}) copy-start(f32[512,768]{1,0:T(8,128)} %get-tuple-element.85) | copy-start | bytes 4718596
  283.6 42.5 %collective-permute-start.4 = (bf16[512,768]{1,0:T(8,128)(2,1)S(1)}, bf16[512,768]{1,0:T(8,128)(2,1)}, u32[]{:S(2)}, u32[]{:S(2)}) collective-permute-start(bf16[512,768]{1,0:T(8,128)(2,1)S(1)} %multiply_convert_fusion), channel_id=1, source_target_pairs={{2,0},{3,1},{0,2},{1,3},{6,4},{7,5},{4,6},{5,7},{10,8},{11,9},{8,1... | collective-permute-start | bytes 2359304 | tf_op jit(solution)/shard_map/ppermute | solution.py:960
  284.3 36.4 %collective-permute-start.5 = (f32[512,2]{0,1:T(2,128)S(1)}, f32[512,2]{0,1:T(2,128)S(1)}, u32[]{:S(2)}, u32[]{:S(2)}) collective-permute-start(f32[512,2]{0,1:T(2,128)S(1)} %fusion.34), channel_id=1, source_target_pairs={{2,0},{3,1},{0,2},{1,3},{6,4},{7,5},{4,6},{5,7},{10,8},{11,9},{8,1... | collective-permute-start | bytes 12296 | tf_op jit(solution)/shard_map/ppermute | solution.py:960
  322.4 12.7 %all-to-all-start.2 = ((f32[8,2,192]{2,1,0:T(2,128)}), f32[8,2,192]{2,1,0:T(2,128)S(1)}, u32[]{:S(2)}, u32[]{:S(2)}) async-start(f32[8,2,192]{2,1,0:T(2,128)} %reshape.187), calls=%async_computation.2 | async-start | bytes 32768 | tf_op jit(solution)/shard_map/all_to_all | solution.py:973
  335.2 59.9 %all-to-all-start.1 = ((bf16[8,2,192,768]{3,2,1,0:T(8,128)(2,1)}), bf16[8,2,192,768]{3,2,1,0:T(8,128)(2,1)}, u32[]{:S(2)}, u32[]{:S(2)}) async-start(bf16[8,2,192,768]{3,2,1,0:T(8,128)(2,1)} %bitcast.86), calls=%async_computation.1 | async-start | bytes 9437184 | tf_op jit(solution)/shard_map/all_to_all | solution.py:973
  474.8 59.5 %all-to-all-start.3 = ((bf16[8,2,192,768]{3,2,1,0:T(8,128)(2,1)}), bf16[8,2,192,768]{3,2,1,0:T(8,128)(2,1)}, u32[]{:S(2)}, u32[]{:S(2)}) async-start(bf16[8,2,192,768]{3,2,1,0:T(8,128)(2,1)} %get-tuple-element.89), calls=%async_computation.3 | async-start | bytes 9437184 | tf_op jit(solution)/shard_map/all_to_all | solution.py:973
  480.8 64.6 %collective-permute-start.7 = (f32[512,2]{0,1:T(2,128)S(1)}, f32[512,2]{0,1:T(2,128)S(1)}, u32[]{:S(2)}, u32[]{:S(2)}) collective-permute-start(f32[512,2]{0,1:T(2,128)S(1)} %select_reduce_fusion), channel_id=1, source_target_pairs={{0,2},{1,3},{2,0},{3,1},{4,6},{5,7},{6,4},{7,5},{8,10},{9,11},{10,... | collective-permute-start | bytes 12296 | tf_op jit(solution)/shard_map/ppermute | solution.py:965
  545.4 33.0 %collective-permute-start.6 = (bf16[512,768]{1,0:T(8,128)(2,1)}, bf16[512,768]{1,0:T(8,128)(2,1)S(1)}, u32[]{:S(2)}, u32[]{:S(2)}) collective-permute-start(bf16[512,768]{1,0:T(8,128)(2,1)} %fusion.8), channel_id=1, source_target_pairs={{0,2},{1,3},{2,0},{3,1},{4,6},{5,7},{6,4},{7,5},{8,10},{9,11},{10,... | collective-permute-start | bytes 2359304 | tf_op jit(solution)/shard_map/ppermute | solution.py:965
  546.4 34.1 %copy-start.9 = (bf16[512,768]{1,0:T(8,128)(2,1)S(1)}, bf16[512,768]{1,0:T(8,128)(2,1)}, u32[]{:S(2)}) copy-start(bf16[512,768]{1,0:T(8,128)(2,1)} %param.26) | copy-start | bytes 2359300
  617.6 67.6 %all-to-all-start.5 = ((bf16[8,2,192,768]{3,2,1,0:T(8,128)(2,1)}), bf16[8,2,192,768]{3,2,1,0:T(8,128)(2,1)}, u32[]{:S(2)}, u32[]{:S(2)}) async-start(bf16[8,2,192,768]{3,2,1,0:T(8,128)(2,1)} %get-tuple-element.96), calls=%async_computation.5 | async-start | bytes 9437184 | tf_op jit(solution)/shard_map/all_to_all | solution.py:973
  622.8 194.3 %collective-permute-start.9 = (bf16[2,768,768]{2,1,0:T(8,128)(2,1)}, bf16[2,768,768]{2,1,0:T(8,128)(2,1)}, u32[]{:S(2)}, u32[]{:S(2)}) collective-permute-start(bf16[2,768,768]{2,1,0:T(8,128)(2,1)} %get-tuple-element.97), channel_id=1, source_target_pairs={{0,1},{1,0},{2,3},{3,2},{4,5},{5,4},{6,7},{7,6},{8,9},{9,8},{10,11... | collective-permute-start | bytes 7077896 | tf_op jit(solution)/shard_map/ppermute | solution.py:969
  622.9 194.2 %collective-permute-start.10 = (bf16[2,768,768]{2,1,0:T(8,128)(2,1)}, bf16[2,768,768]{2,1,0:T(8,128)(2,1)}, u32[]{:S(2)}, u32[]{:S(2)}) collective-permute-start(bf16[2,768,768]{2,1,0:T(8,128)(2,1)} %get-tuple-element.98), channel_id=1, source_target_pairs={{0,1},{1,0},{2,3},{3,2},{4,5},{5,4},{6,7},{7,6},{8,9},{9,8},{10,11... | collective-permute-start | bytes 7077896 | tf_op jit(solution)/shard_map/ppermute | solution.py:969
  647.9 35.4 %copy-start.21 = (f32[12,1024]{1,0:T(8,128)S(1)}, f32[12,1024]{1,0:T(8,128)}, u32[]{:S(2)}) copy-start(f32[12,1024]{1,0:T(8,128)} %get-tuple-element.109) | copy-start | bytes 147460
  647.9 36.5 %copy-start.18 = (f32[1,768]{1,0:T(1,128)S(1)}, f32[1,768]{1,0:T(1,128)}, u32[]{:S(2)}) copy-start(f32[1,768]{1,0:T(1,128)} %get-tuple-element.107) | copy-start | bytes 9220
  647.9 36.5 %copy-start.19 = (f32[1,768]{1,0:T(1,128)S(1)}, f32[1,768]{1,0:T(1,128)}, u32[]{:S(2)}) copy-start(f32[1,768]{1,0:T(1,128)} %get-tuple-element.106) | copy-start | bytes 9220
  696.4 119.4 %collective-permute-start.8 = (bf16[512,768]{1,0:T(8,128)(2,1)}, bf16[512,768]{1,0:T(8,128)(2,1)S(1)}, u32[]{:S(2)}, u32[]{:S(2)}) collective-permute-start(bf16[512,768]{1,0:T(8,128)(2,1)} %fusion.9), channel_id=1, source_target_pairs={{0,2},{1,3},{2,0},{3,1},{4,6},{5,7},{6,4},{7,5},{8,10},{9,11},{10,... | collective-permute-start | bytes 2359304 | tf_op jit(solution)/shard_map/ppermute | solution.py:965
  (14 other events, 76.3 us)

commit v3 on v2

--- a/solution.py
+++ b/solution.py
@@ -445,165 +445,6 @@
     )(x, gain, up, down, normed, grad)
 
 
-def experts_kernel(
-    x_ref, c_ref, gate_ref, up_ref, down_ref,
-    y_ref, dx_ref, dgate_ref, own_up_ref, own_down_ref, peer_up_ref, peer_down_ref,
-    y_sum, dx_sum, dgate_sum, up_sum, down_sum,
-):
-    part = pl.program_id(1)
-    sources, _, span, width = x_ref.shape
-    group = max(1, 384 // span)
-    rows = group * span
-    up_sum[...] = jnp.zeros_like(up_sum)
-    down_sum[...] = jnp.zeros_like(down_sum)
-
-    @pl.when(part == 0)
-    def _():
-        y_sum[...] = jnp.zeros_like(y_sum)
-        dx_sum[...] = jnp.zeros_like(dx_sum)
-        dgate_sum[...] = jnp.zeros_like(dgate_sum)
-
-    def tile(i, _):
-        at = pl.ds(i * group, group)
-        x = x_ref[at, 0].reshape(rows, width)
-        c = c_ref[at, 0].reshape(rows, width)
-        gate = gate_ref[at, 0].reshape(rows, 1)
-        hidden, slope = gelu_parts(nn(x, up_ref[...]))
-        hidden = hidden.astype(BF)
-        back = nt(c, down_ref[...])
-        pre_grad = (gate * back * slope).astype(BF)
-        dgate_sum[at] += jnp.sum(hidden.astype(F32) * back, axis=1, keepdims=True).reshape(group, span, 1)
-        y_sum[at] += nn(hidden, down_ref[...]).reshape(group, span, width)
-        dx_sum[at] += nt(pre_grad, up_ref[...]).reshape(group, span, width)
-        up_sum[...] += tn(x, pre_grad)
-        down_sum[...] += tn(hidden, (gate * c.astype(F32)).astype(BF))
-        return 0
-
-    lax.fori_loop(0, sources // group, tile, 0)
-
-    @pl.when(part == 0)
-    def _():
-        own_up_ref[...] = up_sum[...]
-        own_down_ref[...] = down_sum[...]
-
-    @pl.when(part == 1)
-    def _():
-        peer_up_ref[...] = up_sum[...].astype(BF)
-        peer_down_ref[...] = down_sum[...].astype(BF)
-        y_ref[:, 0] = (gate_ref[:, 0] * y_sum[...]).astype(BF)
-        dx_ref[:, 0] = dx_sum[...].astype(BF)
-        dgate_ref[:, 0] = dgate_sum[...]
-
-
-def run_experts(x, c, gate, up, down):
-    sources, local, span, width = x.shape
-    hidden = up.shape[3]
-    lean = sources * span > 2048
-    once = dict(pipeline_mode=pl.Buffered(1)) if lean else {}
-    row_spec = pl.BlockSpec((sources, 1, span, width), lambda e, j: (0, e, 0, 0), **once)
-    row_out_spec = pl.BlockSpec((sources, 1, span, width), lambda e, j: (0, e, 0, 0), pipeline_mode=pl.Buffered(1))
-    gate_spec = pl.BlockSpec((sources, 1, span, 1), lambda e, j: (0, e, 0, 0), **once)
-    sq = pl.Squeezed()
-    up_spec = pl.BlockSpec((sq, sq, width, hidden), lambda e, j: (j, e, 0, 0))
-    down_spec = pl.BlockSpec((sq, sq, hidden, width), lambda e, j: (j, e, 0, 0))
-    gup_spec = pl.BlockSpec((sq, width, hidden), lambda e, j: (e, 0, 0))
-    gdown_spec = pl.BlockSpec((sq, hidden, width), lambda e, j: (e, 0, 0))
-    rows = local * sources * span
-    return pl.pallas_call(
-        experts_kernel,
-        grid=(local, 2),
-        out_shape=(
-            jax.ShapeDtypeStruct(x.shape, BF),
-            jax.ShapeDtypeStruct(x.shape, BF),
-            jax.ShapeDtypeStruct(gate.shape, F32),
-            jax.ShapeDtypeStruct((local, width, hidden), F32),
-            jax.ShapeDtypeStruct((local, hidden, width), F32),
-            jax.ShapeDtypeStruct((local, width, hidden), BF),
-            jax.ShapeDtypeStruct((local, hidden, width), BF),
-        ),
-        in_specs=[row_spec, row_spec, gate_spec, up_spec, down_spec],
-        out_specs=[row_out_spec, row_out_spec, gate_spec, gup_spec, gdown_spec, gup_spec, gdown_spec],
-        scratch_shapes=[
-            pltpu.VMEM((sources, span, width), F32),
-            pltpu.VMEM((sources, span, width), F32),
-            pltpu.VMEM((sources, span, 1), F32),
-            pltpu.VMEM((width, hidden), F32),
-            pltpu.VMEM((hidden, width), F32),
-        ],
-        compiler_params=pltpu.CompilerParams(vmem_limit_bytes=VMEM_BYTES),
-        cost_estimate=pl.CostEstimate(
-            flops=24 * rows * width * hidden, bytes_accessed=16 * rows * width, transcendentals=2 * rows * hidden,
-        ),
-        name="experts",
-    )(x, c, gate, up, down)
-
-
-def spread_kernel(slot_ref, rows_ref, out_ref):
-    experts, zones, capacity, width = out_ref.shape
-    length = rows_ref.shape[1]
-    take = max(1, 384 // capacity)
-
-    def chunk(i, _):
-        for zone in range(zones):
-            place = lax.broadcasted_iota(jnp.int32, (take * capacity, length), 0) + i * (take * capacity)
-            hit = (place == slot_ref[zone, 0:1, :]) | (place == slot_ref[zone, 1:2, :])
-            picked = nn(jnp.where(hit, 1.0, 0.0).astype(BF), rows_ref[zone])
-            out_ref[pl.ds(i * take, take), zone] = picked.reshape(take, capacity, width).astype(BF)
-        return 0
-
-    lax.fori_loop(0, experts // take, chunk, 0)
-
-
-def spread(slot_rows, rows, experts, capacity):
-    zones, length, width = rows.shape
-    return pl.pallas_call(
-        spread_kernel,
-        out_shape=jax.ShapeDtypeStruct((experts, zones, capacity, width), BF),
-        in_specs=[VMEM_SPEC] * 2,
-        out_specs=VMEM_SPEC,
-        compiler_params=pltpu.CompilerParams(vmem_limit_bytes=VMEM_BYTES),
-        cost_estimate=pl.CostEstimate(
-            flops=2 * zones * experts * capacity * length * width,
-            bytes_accessed=2 * zones * (experts * capacity + length) * width, transcendentals=0,
-        ),
-        name="spread",
-    )(slot_rows, rows)
-
-
-def collect_kernel(slot_ref, rows_ref, out_ref):
-    experts, zones, capacity, width = rows_ref.shape
-    length = out_ref.shape[1]
-    take = max(1, 384 // capacity)
-    out_ref[...] = jnp.zeros_like(out_ref)
-
-    def chunk(i, _):
-        for zone in range(zones):
-            place = lax.broadcasted_iota(jnp.int32, (length, take * capacity), 1) + i * (take * capacity)
-            hit = (place == slot_ref[:, 2 * zone:2 * zone + 1]) | (place == slot_ref[:, 2 * zone + 1:2 * zone + 2])
-            rows = rows_ref[pl.ds(i * take, take), zone].reshape(take * capacity, width)
-            out_ref[zone] += nn(jnp.where(hit, 1.0, 0.0).astype(BF), rows)
-        return 0
-
-    lax.fori_loop(0, experts // take, chunk, 0)
-
-
-def collect(slot_columns, rows):
-    experts, zones, capacity, width = rows.shape
-    length = slot_columns.shape[0]
-    return pl.pallas_call(
-        collect_kernel,
-        out_shape=jax.ShapeDtypeStruct((zones, length, width), F32),
-        in_specs=[VMEM_SPEC] * 2,
-        out_specs=VMEM_SPEC,
-        compiler_params=pltpu.CompilerParams(vmem_limit_bytes=VMEM_BYTES),
-        cost_estimate=pl.CostEstimate(
-            flops=2 * zones * experts * capacity * length * width,
-            bytes_accessed=2 * zones * (experts * capacity + 2 * length) * width, transcendentals=0,
-        ),
-        name="collect",
-    )(slot_columns, rows)
-
-
 MESH = pl.DeviceIdType.MESH
 
 
@@ -671,11 +512,12 @@
     return zones - 1 + 2 * (chips - 1) + 2 * chips
 
 
-def gather_kernel(owners, zones, used_rows, *refs):
+def gather_kernel(owners, zones, used_rows, experts, capacity, *refs):
     count = len(used_rows)
-    blocks, outs = refs[:count], refs[count:2 * count]
-    slabs, turned = refs[2 * count:3 * count], refs[3 * count:4 * count]
-    send_sem, recv_sem, local_sem = refs[4 * count:]
+    blocks, (late_ref, route_ref), refs = refs[:count], refs[count:count + 2], refs[count + 2:]
+    outs, (near_ref, slot_ref), refs = refs[:count], refs[count:count + 2], refs[count + 2:]
+    slabs, turned = refs[:count], refs[count:2 * count]
+    slot_in_ref, send_sem, recv_sem, local_sem = refs[2 * count:]
     owner, zone = lax.axis_index("expert"), lax.axis_index("shard")
     greet(owner, zone, owners, zones)
     send = sender(send_sem, recv_sem)
@@ -734,39 +576,59 @@
     steps = len(routes_of(chips)[0])
     moving = {0: across(0)}
     states = {}
+    slot_ref[0] = token_slots(route_ref[...], experts, capacity)
+    slot_copies = []
+    for d in range(1, zones // 2):
+        device = (owner, (zone + zones - 2 * d) % zones)
+        slot_copies.append(send(slot_ref.at[0], slot_in_ref.at[d - 1], device))
     for g in range(count):
         states[g] = start_rows(g, moving[g])
         if g + 1 < count:
             moving[g + 1] = across(g + 1)
+        else:
+            for d in range(1, zones // 2):
+                device = (owner, (zone + zones - 2 * d) % zones)
+                finals.append(send(late_ref, near_ref.at[d - 1], device))
         if g > 0:
             for step in range(1, steps):
                 states[g - 1] = finish_rows(g - 1, states[g - 1], step)
         states[g] = finish_rows(g, states[g], 0)
     for step in range(1, steps):
         states[count - 1] = finish_rows(count - 1, states[count - 1], step)
+    for d in range(1, zones // 2):
+        slot_copies[d - 1].wait_recv()
+        slot_ref[d] = slot_in_ref[d - 1]
     for copy in finals:
         copy.wait_recv()
-    for copy in pending + finals:
+    for copy in pending + finals + slot_copies:
         copy.wait_send()
 
 
-def gather_weights(blocks, used_rows, owners, zones):
+def gather_weights(blocks, used_rows, late, route_rows, owners, zones, experts, capacity):
     count = len(blocks)
     depth = zones * blocks[0].shape[0]
-    copies = count * gather_copies(owners, zones)
+    groups = zones // 2
+    copies = count * gather_copies(owners, zones) + 2 * (groups - 1)
+    length = route_rows.shape[1]
+    any_spec = pl.BlockSpec(memory_space=pltpu.HBM)
     return pl.pallas_call(
-        lambda *refs: gather_kernel(owners, zones, used_rows, *refs),
-        out_shape=tuple(jax.ShapeDtypeStruct((owners, used, depth), BF) for used in used_rows),
-        in_specs=[VMEM_SPEC] * count,
-        out_specs=tuple([pl.BlockSpec(memory_space=pl.ANY)] * count),
+        lambda *refs: gather_kernel(owners, zones, used_rows, experts, capacity, *refs),
+        out_shape=tuple(jax.ShapeDtypeStruct((owners, used, depth), BF) for used in used_rows)
+        + (
+            jax.ShapeDtypeStruct((groups - 1,) + late.shape, late.dtype),
+            jax.ShapeDtypeStruct((groups, 8, length), F32),
+        ),
+        in_specs=[VMEM_SPEC] * count + [any_spec, VMEM_SPEC],
+        out_specs=tuple([any_spec] * (count + 1)) + (VMEM_SPEC,),
         scratch_shapes=[pltpu.VMEM((zones,) + b.shape, BF) for b in blocks]
         + [pltpu.VMEM((b.shape[1], depth), BF) for b in blocks]
+        + [pltpu.VMEM((groups - 1, 8, length), F32)]
         + [pltpu.SemaphoreType.DMA((copies,)), pltpu.SemaphoreType.DMA((copies,)), pltpu.SemaphoreType.DMA((count,))],
         compiler_params=pltpu.CompilerParams(
             vmem_limit_bytes=24 * 1024 * 1024, collective_id=1, has_side_effects=True
         ),
         name="gather_weights",
-    )(*blocks)
+    )(*blocks, late, route_rows)
 
 
 def reduce_copies(owners, zones):
@@ -914,7 +776,7 @@
         lambda *refs: reduce_kernel(owners, zones, used_rows, *refs),
         out_shape=tuple(jax.ShapeDtypeStruct((depth // zones, w), F32) for w in wide)
         + (jax.ShapeDtypeStruct(small.shape, F32),),
-        in_specs=[pl.BlockSpec(memory_space=pl.ANY)] * count + [VMEM_SPEC],
+        in_specs=[pl.BlockSpec(memory_space=pltpu.HBM)] * count + [VMEM_SPEC],
         out_specs=tuple([VMEM_SPEC] * (count + 1)),
         scratch_shapes=[pltpu.VMEM((chips, used, depth), BF) for used in used_rows]
         + [pltpu.VMEM((chips, used, depth), BF) for used in used_rows]
@@ -930,6 +792,500 @@
     )(*parts, small)
 
 
+def three_pieces(row):
+    top = row.astype(BF)
+    rest = row - top.astype(F32)
+    middle = rest.astype(BF)
+    low = (rest - middle.astype(F32)).astype(BF)
+    return jnp.concatenate([top, middle, low, jnp.zeros((5, row.shape[1]), BF)], axis=0)
+
+
+def sum_pieces(rows):
+    return rows[0:1] + rows[1:2] + rows[2:3]
+
+
+def token_slots(route_rows, experts, capacity):
+    length = route_rows.shape[1]
+    ids = lax.broadcasted_iota(jnp.int32, (experts, length), 0)
+    first, second = route_rows[0:1] == ids, route_rows[1:2] == ids
+    named = jnp.where(first | second, 1.0, 0.0).astype(BF)
+    earlier = (
+        lax.broadcasted_iota(jnp.int32, (length, length), 0) < lax.broadcasted_iota(jnp.int32, (length, length), 1)
+    )
+    place = nn(named, jnp.where(earlier, 1.0, 0.0).astype(BF)) + (ids * capacity).astype(F32)
+    rows = [jnp.sum(jnp.where(hit, place, 0.0), axis=0, keepdims=True) for hit in (first, second)]
+    return jnp.concatenate(rows + [jnp.zeros((6, length), F32)], axis=0)
+
+
+def slot_hits(slots, start, count):
+    place = lax.broadcasted_iota(jnp.int32, (count, slots.shape[1]), 0).astype(F32) + start.astype(F32)
+    one, zero = jnp.asarray(1.0, F32), jnp.asarray(0.0, F32)
+    return [jnp.where(place == slots[k:k + 1], one, zero).astype(BF) for k in range(2)]
+
+
+def greet_plane(owner, zone, owners, zones):
+    barrier = pltpu.get_barrier_semaphore()
+    peers = [(flip(owner, mask), zone) for mask in range(1, owners)]
+    peers += [(owner, (zone + d) % zones) for d in range(2, zones, 2)] + [(owner, flip(zone, 1))]
+    for peer in peers:
+        pl.semaphore_signal(barrier, inc=1, device_id=peer, device_id_type=MESH)
+    pl.semaphore_wait(barrier, len(peers))
+
+
+def peer_order(owners):
+    return list(range(2, owners)) + [1, 0]
+
+
+def softmax_pair(logits, route_rows):
+    ids = lax.broadcasted_iota(jnp.int32, logits.shape, 0)
+    a, b = [jnp.sum(jnp.where(route_rows[k:k + 1] == ids, logits, 0.0), axis=0, keepdims=True) for k in range(2)]
+    peak = jnp.maximum(a, b)
+    ea, eb = jnp.exp(a - peak), jnp.exp(b - peak)
+    return ea / (ea + eb), eb / (ea + eb)
+
+
+def send_rows_kernel(
+    owners, zones, capacity, x_ref, gain_ref, router_ref, route_ref, slot_ref, slices_ref,
+    normed_ref, gates_ref, rows_ref, gate_ref, other_ref,
+    near_ref, near_gates_ref, packed_ref, tags_ref, tags_in_ref, send_sem, recv_sem, local_sem,
+):
+    owner, zone = lax.axis_index("expert"), lax.axis_index("shard")
+    tags_ref[...] = jnp.zeros_like(tags_ref)
+    greet_plane(owner, zone, owners, zones)
+    send = sender(send_sem, recv_sem)
+    groups = zones // 2
+    local = rows_ref.shape[1]
+    span = local * capacity
+    field = x_ref[...]
+    normed_ref[...] = (field * inverse_rms(field) * gain_ref[...]).astype(BF)
+    cut = normed_ref.shape[1] // 2
+    lanes = [pl.ds(0, cut), pl.ds(cut, cut)]
+    copies = {}
+    for half in range(2):
+        for d in range(1, groups):
+            device = (owner, (zone + zones - 2 * d) % zones)
+            copies[d, half] = send(normed_ref.at[:, lanes[half]], near_ref.at[d - 1, :, lanes[half]], device)
+    gates = softmax_pair(nt(router_ref[...], normed_ref[...]), route_ref[...])
+    gates_ref[...] = jnp.concatenate(list(gates) + [jnp.zeros((6, gates[0].shape[1]), F32)], axis=0)
+    for d in range(1, groups):
+        copies[d, 2] = send(gates_ref, near_gates_ref.at[d - 1], (owner, (zone + zones - 2 * d) % zones))
+    arrivals, stays = [], []
+    for part in range(local):
+        arrivals.append(send(slices_ref.at[part], other_ref.at[part], (owner, flip(zone, 1))))
+    def ship(d, mask, target, half):
+        columns = slice(None) if half is None else lanes[half]
+        for part in range(local):
+            source = packed_ref.at[d, mask, pl.ds(part * capacity, capacity), columns]
+            place = rows_ref.at[owner, part, pl.ds(d * capacity, capacity), columns]
+            if mask:
+                arrivals.append(send(source, place, (target, zone)))
+            else:
+                at = (2 * d + (half or 0)) * local + part
+                copy = pltpu.make_async_copy(source, place, local_sem.at[at])
+                copy.start()
+                stays.append(copy)
+
+    for d in range(groups):
+        for half in (None,) if d == 0 else (0, 1):
+            if d:
+                copies[d, half].wait_recv()
+                if half == 0:
+                    copies[d, 2].wait_recv()
+            rows = normed_ref if d == 0 else near_ref.at[d - 1]
+            weights = gates_ref[...] if d == 0 else near_gates_ref[d - 1]
+            pieces = [three_pieces(weights[k:k + 1]) for k in range(2)]
+            slots = slot_ref[d]
+            for mask in peer_order(owners):
+                target = flip(owner, mask)
+                hits = slot_hits(slots, target * span, span)
+                both = hits[0] + hits[1]
+                if half is None:
+                    packed_ref[d, mask] = nn(both, rows[...]).astype(BF)
+                else:
+                    packed_ref[d, mask, :, lanes[half]] = nn(both, rows[:, lanes[half]]).astype(BF)
+                ship(d, mask, target, half)
+                if half == 1:
+                    continue
+                tag = sum_pieces(nt(pieces[0], hits[0]) + nt(pieces[1], hits[1]))
+                tags_ref[d, mask, :, 0:span] = jnp.broadcast_to(tag, (8, span))
+                if mask:
+                    arrivals.append(send(tags_ref.at[d, mask], tags_in_ref.at[d, owner], (target, zone)))
+                else:
+                    tags_in_ref[d, owner] = tags_ref[d, mask]
+    for copy in arrivals:
+        copy.wait_recv()
+    for d in range(groups):
+        for source in range(owners):
+            column = tags_in_ref[d, source].T
+            for part in range(local):
+                gate_ref[source, part, d * capacity:(d + 1) * capacity, :] = column[
+                    part * capacity:(part + 1) * capacity, 0:1
+                ]
+    for copy in stays:
+        copy.wait()
+    for copy in list(copies.values()) + arrivals:
+        copy.wait_send()
+
+
+def send_rows(x, gain, router, route_rows, slot_rows, slices, owners, zones, local, capacity):
+    length, width = x.shape
+    groups = zones // 2
+    span = local * capacity
+    any_spec = pl.BlockSpec(memory_space=pltpu.HBM)
+    wide = -(-span // 128) * 128
+    copies = local + 3 * (groups - 1) + (owners - 1) * (local + 1 + (groups - 1) * (2 * local + 1))
+    return pl.pallas_call(
+        lambda *refs: send_rows_kernel(owners, zones, capacity, *refs),
+        out_shape=(
+            jax.ShapeDtypeStruct((length, width), BF),
+            jax.ShapeDtypeStruct((8, length), F32),
+            jax.ShapeDtypeStruct((owners, local, groups * capacity, width), BF),
+            jax.ShapeDtypeStruct((owners, local, groups * capacity, 1), F32),
+            jax.ShapeDtypeStruct(slices.shape, slices.dtype),
+        ),
+        in_specs=[VMEM_SPEC] * 5 + [any_spec],
+        out_specs=(VMEM_SPEC, VMEM_SPEC, any_spec, VMEM_SPEC, any_spec),
+        scratch_shapes=[
+            pltpu.VMEM((groups - 1, length, width), BF),
+            pltpu.VMEM((groups - 1, 8, length), F32),
+            pltpu.VMEM((groups, owners, span, width), BF),
+            pltpu.VMEM((groups, owners, 8, wide), F32),
+            pltpu.VMEM((groups, owners, 8, wide), F32),
+            pltpu.SemaphoreType.DMA((copies,)),
+            pltpu.SemaphoreType.DMA((copies,)),
+            pltpu.SemaphoreType.DMA((2 * groups * local,)),
+        ],
+        compiler_params=pltpu.CompilerParams(
+            vmem_limit_bytes=40 * 1024 * 1024, collective_id=3, has_side_effects=True
+        ),
+        name="send_rows",
+    )(x, gain, router, route_rows, slot_rows, slices)
+
+
+def return_rows_kernel(
+    owners, zones, capacity,
+    rows_ref, dgate_ref, slot_ref, gates_ref, route_ref, x_ref, gain_ref, router_ref, normed_ref, top_ref,
+    dx_ref, dgain_ref, drouter_ref,
+    back_ref, tags_ref, tags_in_ref, part_ref, part_in_ref, mark_ref, mark_in_ref, sum_ref, send_sem, recv_sem, local_sem,
+):
+    owner, zone = lax.axis_index("expert"), lax.axis_index("shard")
+    tags_ref[...] = jnp.zeros_like(tags_ref)
+    greet_plane(owner, zone, owners, zones)
+    send = sender(send_sem, recv_sem)
+    groups = zones // 2
+    local = rows_ref.shape[1]
+    span = local * capacity
+    chip = owner // 2
+    cut = back_ref.shape[3] // 2
+    lanes = [pl.ds(0, cut), pl.ds(cut, cut)]
+    arrivals, stays, sent = {}, {}, []
+
+    def ship(d, half):
+        window = pl.ds(d * capacity, capacity)
+        columns = slice(None) if half is None else lanes[half]
+        for mask in peer_order(owners):
+            target = flip(owner, mask)
+            for part in range(local):
+                source = rows_ref.at[target, part, window, columns]
+                place = back_ref.at[d, owner, pl.ds(part * capacity, capacity), columns]
+                if mask:
+                    arrivals.setdefault((d, half, mask), []).append(send(source, place, (target, zone)))
+                else:
+                    at = (2 * d + (half or 0)) * local + part
+                    copy = pltpu.make_async_copy(source, place, local_sem.at[at])
+                    copy.start()
+                    stays.setdefault((d, half), []).append(copy)
+
+    def ship_tags(d):
+        for mask in peer_order(owners):
+            target = flip(owner, mask)
+            columns = [dgate_ref[target, part, d * capacity:(d + 1) * capacity, :] for part in range(local)]
+            column = jnp.concatenate(columns, axis=0)
+            tags_ref[d, mask, :, 0:span] = jnp.broadcast_to(column, (span, 128)).T[0:8]
+            if mask:
+                arrivals.setdefault((d, "tags", mask), []).append(
+                    send(tags_ref.at[d, mask], tags_in_ref.at[d, owner], (target, zone))
+                )
+            else:
+                tags_in_ref[d, owner] = tags_ref[d, mask]
+
+    def collect_zone(d, half):
+        slots = slot_ref[d]
+        columns = slice(None) if half is None else lanes[half]
+        marks = [jnp.zeros((1, slots.shape[1]), F32) for _ in range(2)]
+        for turn, hop in enumerate(list(range(1, owners // 2)) + [0]):
+            for mask in (2 * hop, 2 * hop + 1):
+                waits = arrivals.get((d, half, mask), [])
+                if half != 1:
+                    waits = waits + arrivals.get((d, "tags", mask), [])
+                for copy in waits:
+                    copy.wait_recv()
+                if mask == 0:
+                    for copy in stays[d, half]:
+                        copy.wait()
+            peer = flip(chip, hop)
+            hits = slot_hits(slots, peer * (2 * span), 2 * span)
+            rows = back_ref[d, pl.ds(2 * peer, 2), :, columns]
+            added = tn(hits[0] + hits[1], rows.reshape(2 * span, rows.shape[2]))
+            if turn == 0:
+                sum_ref[:, columns] = added
+            else:
+                sum_ref[:, columns] += added
+            if half == 1:
+                continue
+            tag = tags_in_ref[d, pl.ds(2 * peer, 2)]
+            tag = jnp.concatenate([tag[0, 0:1, 0:span], tag[1, 0:1, 0:span]], axis=1)
+            pieces = three_pieces(tag)
+            for k in range(2):
+                marks[k] = marks[k] + sum_pieces(nn(pieces, hits[k]))
+        return marks
+
+    for d in range(1, groups):
+        ship(d, 0)
+        ship_tags(d)
+    incoming = {d: [] for d in range(1, groups)}
+    for half in range(2):
+        for d in range(1, groups):
+            for mask in peer_order(owners):
+                for copy in arrivals.get((d, half, mask), []):
+                    copy.wait_send()
+            if half == 0:
+                ship(d, 1)
+        if half == 1:
+            ship(0, None)
+            ship_tags(0)
+        for d in range(1, groups):
+            device = (owner, (zone + 2 * d) % zones)
+            marks = collect_zone(d, half)
+            part_ref[d - 1, :, lanes[half]] = sum_ref[:, lanes[half]].astype(BF)
+            incoming[d].append(
+                send(part_ref.at[d - 1, :, lanes[half]], part_in_ref.at[d - 1, :, lanes[half]], device)
+            )
+            if half == 0:
+                mark_ref[d - 1] = jnp.concatenate(marks + [jnp.zeros((6, marks[0].shape[1]), F32)], axis=0)
+                incoming[d].append(send(mark_ref.at[d - 1], mark_in_ref.at[d - 1], device))
+    marks = collect_zone(0, None)
+    for d in range(1, groups):
+        for copy in incoming[d]:
+            copy.wait_recv()
+            sent.append(copy)
+        sum_ref[...] += part_in_ref[d - 1].astype(F32)
+        marks = [marks[k] + mark_in_ref[d - 1, k:k + 1, :] for k in range(2)]
+    gates = [gates_ref[k:k + 1, :] for k in range(2)]
+    mean = gates[0] * marks[0] + gates[1] * marks[1]
+    ids = lax.broadcasted_iota(jnp.int32, (router_ref.shape[0], mean.shape[1]), 0)
+    dlogits = jnp.zeros(ids.shape, F32)
+    for k in range(2):
+        dlogits = dlogits + jnp.where(route_ref[k:k + 1, :] == ids, gates[k] * (marks[k] - mean), 0.0)
+    dlogits = dlogits.astype(BF)
+    drouter_ref[...] = nn(dlogits, normed_ref[...])
+    sum_ref[...] += tn(dlogits, router_ref[...])
+    field = x_ref[...]
+    inverse = inverse_rms(field)
+    unit = field * inverse
+    upper = sum_ref[...]
+    scaled = upper * gain_ref[...]
+    dgain_ref[...] = jnp.sum(upper * unit, axis=0, keepdims=True)
+    dx_ref[...] = top_ref[...].astype(F32) + inverse * (
+        scaled - unit * jnp.mean(scaled * unit, axis=1, keepdims=True)
+    )
+    for (d, half, _), copies in arrivals.items():
+        if d == 0 or half == "tags":
+            sent.extend(copies)
+    for copy in sent:
+        copy.wait_send()
+
+
+def return_rows(rows, dgate, slot_rows, gates, route_rows, x, gain, router, normed, top, zones, capacity):
+    length, width = x.shape
+    owners, local = rows.shape[:2]
+    groups = zones // 2
+    span = local * capacity
+    wide = -(-span // 128) * 128
+    copies = 3 * (groups - 1) + (owners - 1) * (local + 1 + (groups - 1) * (2 * local + 1))
+    return pl.pallas_call(
+        lambda *refs: return_rows_kernel(owners, zones, capacity, *refs),
+        out_shape=(
+            jax.ShapeDtypeStruct((length, width), F32),
+            jax.ShapeDtypeStruct((1, width), F32),
+            jax.ShapeDtypeStruct(router.shape, F32),
+        ),
+        in_specs=[pl.BlockSpec(memory_space=pltpu.HBM)] + [VMEM_SPEC] * 9,
+        out_specs=[VMEM_SPEC] * 3,
+        scratch_shapes=[
+            pltpu.VMEM((groups, owners, span, width), BF),
+            pltpu.VMEM((groups, owners, 8, wide), F32),
+            pltpu.VMEM((groups, owners, 8, wide), F32),
+            pltpu.VMEM((groups - 1, length, width), BF),
+            pltpu.VMEM((groups - 1, length, width), BF),
+            pltpu.VMEM((groups - 1, 8, length), F32),
+            pltpu.VMEM((groups - 1, 8, length), F32),
+            pltpu.VMEM((length, width), F32),
+            pltpu.SemaphoreType.DMA((copies,)),
+            pltpu.SemaphoreType.DMA((copies,)),
+            pltpu.SemaphoreType.DMA((2 * groups * local,)),
+        ],
+        compiler_params=pltpu.CompilerParams(
+            vmem_limit_bytes=40 * 1024 * 1024, collective_id=4, has_side_effects=True
+        ),
+        name="return_rows",
+    )(rows, dgate, slot_rows, gates, route_rows, x, gain, router, normed, top)
+
+
+def experts_kernel(
+    x_ref, c_ref, gate_ref, own_up_in, own_down_in, peer_up_in, peer_down_in,
+    y_ref, dx_ref, dgate_ref, own_up_ref, own_down_ref, peer_up_ref, peer_down_ref,
+    hidden_ref, pre_ref, dey_ref,
+):
+    sources, _, span, width = x_ref.shape
+    size = own_up_in.shape[1]
+    group = max(1, 384 // span)
+    rows = group * span
+
+    @pl.loop(0, sources // group)
+    def _(i):
+        at = pl.ds(i * group, group)
+        rows_at = pl.ds(pl.multiple_of(i * rows, 16), rows)
+        x = x_ref[at, 0].reshape(rows, width)
+        c = c_ref[at, 0].reshape(rows, width)
+        gate = gate_ref[at, 0].reshape(rows, 1)
+        dey_ref[rows_at, :] = (gate * c.astype(F32)).astype(BF)
+        dgate = jnp.zeros((rows, 1), F32)
+        for part, (up_ref, down_ref) in enumerate(((own_up_in, own_down_in), (peer_up_in, peer_down_in))):
+            cols = slice(part * size, part * size + size)
+            hidden, slope = gelu_parts(nn(x, up_ref[...]))
+            hidden = hidden.astype(BF)
+            hidden_ref[rows_at, cols] = hidden
+            back = nt(c, down_ref[...])
+            dgate = dgate + jnp.sum(hidden.astype(F32) * back, axis=1, keepdims=True)
+            pre_ref[rows_at, cols] = (gate * back * slope).astype(BF)
+        y = nn(hidden_ref[rows_at, 0:size], own_down_in[...]) + nn(hidden_ref[rows_at, size:], peer_down_in[...])
+        y_ref[at, 0] = (gate * y).astype(BF).reshape(group, span, width)
+        dx = nt(pre_ref[rows_at, 0:size], own_up_in[...]) + nt(pre_ref[rows_at, size:], peer_up_in[...])
+        dx_ref[at, 0] = dx.astype(BF).reshape(group, span, width)
+        dgate_ref[at, 0] = dgate.reshape(group, span, 1)
+
+    step = 256 if width % 256 == 0 else 128
+
+    @pl.loop(0, width // step)
+    def _(i):
+        at = pl.ds(pl.multiple_of(i * step, step), step)
+        x = x_ref[:, 0, :, at].reshape(sources * span, step)
+        own_up_ref[at, :] = tn(x, pre_ref[:, 0:size])
+        peer_up_ref[at, :] = tn(x, pre_ref[:, size:]).astype(BF)
+
+    step = 256 if size % 256 == 0 else 128
+
+    @pl.loop(0, size // step)
+    def _(i):
+        at = pl.ds(pl.multiple_of(i * step, step), step)
+        own_down_ref[at, :] = tn(hidden_ref[:, at], dey_ref[...])
+        peer_at = pl.ds(pl.multiple_of(i * step + size, step), step)
+        peer_down_ref[at, :] = tn(hidden_ref[:, peer_at], dey_ref[...]).astype(BF)
+
+
+def run_experts(x, c, gate, own_up, own_down, peer_up, peer_down):
+    sources, local, span, width = x.shape
+    hidden = own_up.shape[2]
+    lean = sources * span > 2048
+    once = dict(pipeline_mode=pl.Buffered(1)) if lean else {}
+    row_spec = pl.BlockSpec((sources, 1, span, width), lambda e: (0, e, 0, 0), **once)
+    gate_spec = pl.BlockSpec((sources, 1, span, 1), lambda e: (0, e, 0, 0), **once)
+    late_spec = pl.BlockSpec((sources, 1, span, width), lambda e: (0, e, 0, 0), pipeline_mode=pl.Buffered(1))
+    sq = pl.Squeezed()
+    gup_spec = pl.BlockSpec((sq, width, hidden), lambda e: (e, 0, 0))
+    gdown_spec = pl.BlockSpec((sq, hidden, width), lambda e: (e, 0, 0))
+    rows = local * sources * span
+    return pl.pallas_call(
+        experts_kernel,
+        grid=(local,),
+        out_shape=(
+            jax.ShapeDtypeStruct(x.shape, BF),
+            jax.ShapeDtypeStruct(x.shape, BF),
+            jax.ShapeDtypeStruct(gate.shape, F32),
+            jax.ShapeDtypeStruct((local, width, hidden), F32),
+            jax.ShapeDtypeStruct((local, hidden, width), F32),
+            jax.ShapeDtypeStruct((local, width, hidden), BF),
+            jax.ShapeDtypeStruct((local, hidden, width), BF),
+        ),
+        in_specs=[row_spec, late_spec, gate_spec, gup_spec, gdown_spec, gup_spec, gdown_spec],
+        out_specs=[late_spec, row_spec, gate_spec, gup_spec, gdown_spec, gup_spec, gdown_spec],
+        scratch_shapes=[
+            pltpu.VMEM((sources * span, 2 * hidden), BF),
+            pltpu.VMEM((sources * span, 2 * hidden), BF),
+            pltpu.VMEM((sources * span, width), BF),
+        ],
+        compiler_params=pltpu.CompilerParams(vmem_limit_bytes=60 * 1024 * 1024),
+        cost_estimate=pl.CostEstimate(
+            flops=24 * rows * width * hidden, bytes_accessed=16 * rows * width, transcendentals=2 * rows * hidden,
+        ),
+        name="experts",
+    )(x, c, gate, own_up, own_down, peer_up, peer_down)
+
+
+def spread_kernel(slot_ref, rows_ref, out_ref):
+    experts, zones, capacity, width = out_ref.shape
+    take = max(1, 384 // capacity)
+
+    def chunk(i, _):
+        for zone in range(zones):
+            hits = slot_hits(slot_ref[zone], i * (take * capacity), take * capacity)
+            picked = nn(hits[0] + hits[1], rows_ref[zone])
+            out_ref[pl.ds(i * take, take), zone] = picked.reshape(take, capacity, width).astype(BF)
+        return 0
+
+    lax.fori_loop(0, experts // take, chunk, 0)
+
+
+def spread(slot_rows, rows, experts, capacity):
+    zones, length, width = rows.shape
+    return pl.pallas_call(
+        spread_kernel,
+        out_shape=jax.ShapeDtypeStruct((experts, zones, capacity, width), BF),
+        in_specs=[VMEM_SPEC] * 2,
+        out_specs=VMEM_SPEC,
+        compiler_params=pltpu.CompilerParams(vmem_limit_bytes=VMEM_BYTES),
+        cost_estimate=pl.CostEstimate(
+            flops=2 * zones * experts * capacity * length * width,
+            bytes_accessed=2 * zones * (experts * capacity + length) * width, transcendentals=0,
+        ),
+        name="spread",
+    )(slot_rows, rows)
+
+
+def collect_kernel(slot_ref, rows_ref, out_ref):
+    experts, zones, capacity, width = rows_ref.shape
+    length = out_ref.shape[1]
+    take = max(1, 384 // capacity)
+    out_ref[...] = jnp.zeros_like(out_ref)
+
+    def chunk(i, _):
+        for zone in range(zones):
+            hits = slot_hits(slot_ref[zone], i * (take * capacity), take * capacity)
+            rows = rows_ref[pl.ds(i * take, take), zone].reshape(take * capacity, width)
+            out_ref[zone] += tn(hits[0] + hits[1], rows)
+        return 0
+
+    lax.fori_loop(0, experts // take, chunk, 0)
+
+
+def collect(slot_rows, rows):
+    experts, zones, capacity, width = rows.shape
+    length = slot_rows.shape[2]
+    return pl.pallas_call(
+        collect_kernel,
+        out_shape=jax.ShapeDtypeStruct((zones, length, width), F32),
+        in_specs=[VMEM_SPEC] * 2,
+        out_specs=VMEM_SPEC,
+        compiler_params=pltpu.CompilerParams(vmem_limit_bytes=VMEM_BYTES),
+        cost_estimate=pl.CostEstimate(
+            flops=2 * zones * experts * capacity * length * width,
+            bytes_accessed=2 * zones * (experts * capacity + 2 * length) * width, transcendentals=0,
+        ),
+        name="collect",
+    )(slot_rows, rows)
+
+
 bucket_edges = (1, 2, 3, 4, 6, 8, 12, 16, 24, 32, 48, 64, 96, 128, 192, 256, 384, 512, 768, 1024, 1536)
 
 
@@ -943,16 +1299,6 @@
     real = jnp.arange(2 * length)[:, None] < 2 * length - 1
     hit = (bucket[:, None] == jnp.arange(buckets, dtype=jnp.int32)[None, :]) & real
     return hit.astype(F32)
-
-
-def expert_slots(routes, experts_all, capacity):
-    pairs = routes.reshape(-1)
-    onehot = pairs[:, None] == jnp.arange(experts_all, dtype=jnp.int32)[None, :]
-    count = pairs.shape[0]
-    before = jnp.arange(count)[:, None] > jnp.arange(count)[None, :]
-    ranks = jnp.dot(before.astype(BF), onehot.astype(BF), preferred_element_type=F32)
-    own = jnp.sum(jnp.where(onehot, ranks, 0.0), axis=1).astype(jnp.int32)
-    return (pairs * capacity + own).reshape(routes.shape)
 
 
 def shift_from(value, distance):
@@ -994,7 +1340,8 @@
 
     down_block = mlp_down.reshape(parts, -1, mlp_down.shape[1]).transpose(1, 0, 2).reshape(qkv_weight.shape[1], -1)
     router_block = jnp.pad(router, ((0, 0), (0, router_pad - router.shape[1])))
-    first, up_full, down_full, last = gather_weights(
+    route_rows = routes.T
+    first, up_full, down_full, last, cotangent_near, slot_rows = gather_weights(
         [
             padded(jnp.concatenate([qkv_weight[0], out_weight[0]], axis=1)),
             padded(mlp_up),
@@ -1002,7 +1349,7 @@
             padded(jnp.concatenate([qkv_weight[1], out_weight[1], router_block], axis=1)),
         ],
         (qkv_cols + out_cols, mlp_up.shape[1], parts * mlp_down.shape[1], qkv_cols + out_cols + router_pad),
-        owners, zones_all,
+        cotangent, route_rows, owners, zones_all, experts_all, capacity,
     )
 
     def layer_weights(block):
@@ -1016,25 +1363,20 @@
         down_full = down_full.reshape(owners, parts, -1, width).transpose(1, 0, 2, 3).reshape(1, -1, width)
     router_full = last[:, qkv_cols + out_cols:qkv_cols + out_cols + router.shape[1]].reshape(experts_all, width)
 
-    first, cotangent_late, down_late = lax.optimization_barrier((first, cotangent, expert_down))
+    first, up_late = lax.optimization_barrier((first, expert_up))
     weights0, weights1 = layer_weights(first), layer_weights(last)
-    up_other, down_other = swap_pair(expert_up), swap_pair(down_late)
-
-    slots = expert_slots(routes, experts_all, capacity)
-    zone_slots = [slots] + [shift_from(slots, 2 * d) for d in range(1, zones)]
-    slot_columns = jnp.concatenate(zone_slots, axis=1)
-    slot_rows = slot_columns.T.reshape(zones, routes.shape[1], length)
+    up_other = swap_pair(up_late)
+    direct = capacity % 16 == 0
 
     def dispatch(rows):
-        own = [rows] + [shift_from(rows, 2 * d) for d in range(1, zones)]
-        packed = spread(slot_rows, jnp.stack(own), experts_all, capacity)
+        packed = spread(slot_rows, rows, experts_all, capacity)
         return exchange(packed.reshape(owners, local, zones * capacity, width))
 
     def undo(rows):
         back = exchange(rows).reshape(experts_all, zones, capacity, width)
-        return collect(slot_columns, back)
-
-    cotangent_rows = dispatch(cotangent_late)
+        return collect(slot_rows, back)
+
+    cotangent_rows = dispatch(jnp.concatenate([cotangent[None], cotangent_near]))
 
     onehot = bucket_onehot(length, bias_tables.shape[2])
     vectors = lax.dot_general(
@@ -1043,55 +1385,59 @@
     gains = [norm_gains[i:i + 1] for i in range(4)]
     x0 = tokens.astype(F32)
     x1, ah0, qkv0, o0, lse0 = attend(piece_start, x0, gains[0], weights0, vectors[0])
-    x1, up_other = lax.optimization_barrier((x1, up_other))
     x2, mh = mlp(x1, gains[1], up_full, down_full, parts, zones_all)
     x3, ah1, qkv1, o1, lse1 = attend(piece_start, x2, gains[2], weights1, vectors[1])
 
-    x3, down_other, cotangent_rows = lax.optimization_barrier((x3, down_other, cotangent_rows))
-    up_pair = jnp.stack([expert_up, up_other])
-    down_pair = jnp.stack([expert_down, down_other])
-    unit3 = x3 * inverse_rms(x3)
-    eh = (unit3 * gains[3]).astype(BF)
-    logits = nt(eh, router_full)
-    expert_ids = jnp.arange(experts_all, dtype=jnp.int32)
-    chosen = routes[:, :, None] == expert_ids[None, None, :]
-    gates = jax.nn.softmax(jnp.sum(jnp.where(chosen, logits[:, None, :], 0.0), axis=2), axis=1)
-
-    eh_rows = dispatch(eh)
-    slot_ids = jnp.arange(experts_all * capacity, dtype=jnp.int32)
-
-    def gate_slots(zone):
-        zone_gates = gates if zone == 0 else shift_from(gates, 2 * zone)
-        hit = zone_slots[zone][:, :, None] == slot_ids[None, None, :]
-        return jnp.sum(jnp.where(hit, zone_gates[:, :, None], 0.0), axis=(0, 1)).reshape(experts_all, capacity)
-
-    gate_rows = exchange(
-        jnp.stack([gate_slots(d) for d in range(zones)], axis=1).reshape(owners, local, zones * capacity)
-    )
+    x3, up_other, cotangent_rows = lax.optimization_barrier((x3, up_other, cotangent_rows))
+    if direct:
+        eh, gates, eh_rows, gate_rows, down_other = send_rows(
+            x3, gains[3], router_full, route_rows, slot_rows, expert_down, owners, zones_all, local, capacity
+        )
+    else:
+        down_other = swap_pair(expert_down)
+        eh = (x3 * inverse_rms(x3) * gains[3]).astype(BF)
+        gates = jnp.concatenate(softmax_pair(nt(router_full, eh), route_rows))
+        eh_rows = dispatch(jnp.stack([eh] + [shift_from(eh, 2 * d) for d in range(1, zones)]))
+        slot_ids = jnp.arange(experts_all * capacity, dtype=jnp.int32).astype(F32)
+        marks = [slot_rows[d, :2][None] == slot_ids[:, None, None] for d in range(zones)]
+
+        def gate_slots(d):
+            held = gates if d == 0 else shift_from(gates, 2 * d)
+            return jnp.sum(jnp.where(marks[d], held[None], 0.0), axis=(1, 2)).reshape(experts_all, capacity)
+
+        gate_rows = exchange(
+            jnp.stack([gate_slots(d) for d in range(zones)], axis=1).reshape(owners, local, zones * capacity)
+        )[..., None]
     y_rows, dx_rows, dgate_rows, own_up, own_down, peer_up, peer_down = run_experts(
-        eh_rows, cotangent_rows, gate_rows[..., None], up_pair, down_pair
+        eh_rows, cotangent_rows, gate_rows, expert_up, expert_down, up_other, down_other
     )
     peer_up, peer_down = swap_pair(peer_up), swap_pair(peer_down)
 
-    dx_back = undo(dx_rows)
-    dgate_back = exchange(dgate_rows[..., 0]).reshape(experts_all, zones, capacity)
-    token_grad = dx_back[0]
-    gate_grad = 0.0
-    for d in range(zones):
-        hit = zone_slots[d][:, :, None] == slot_ids[None, None, :]
-        part = jnp.sum(jnp.where(hit, dgate_back[:, d].reshape(-1)[None, None, :], 0.0), axis=2)
-        gate_grad = gate_grad + (part if d == 0 else shift_to(part, 2 * d))
-    for d in range(1, zones):
-        token_grad = token_grad + shift_to(dx_back[d].astype(BF), 2 * d).astype(F32)
-    c = cotangent.astype(F32)
-    dchoice = gates * (gate_grad - jnp.sum(gates * gate_grad, axis=1, keepdims=True))
-    dlogits = jnp.sum(jnp.where(chosen, dchoice[:, :, None], 0.0), axis=1).astype(BF)
-    grad_router = tn(dlogits, eh)
-    deh = token_grad + nn(dlogits, router_full)
-    scaled = deh * gains[3]
-    dx3 = c + inverse_rms(x3) * (scaled - unit3 * jnp.mean(scaled * unit3, axis=1, keepdims=True))
-    dgain3 = jnp.sum(deh * unit3, axis=0)[None]
-
+    if direct:
+        dx3, dgain3, grad_router = return_rows(
+            dx_rows, dgate_rows, slot_rows, gates, route_rows, x3, gains[3], router_full, eh, cotangent,
+            zones_all, capacity,
+        )
+    else:
+        dx_back = undo(dx_rows)
+        dgate_back = exchange(dgate_rows[..., 0]).reshape(experts_all, zones, capacity)
+        token_grad, gate_grad = dx_back[0], 0.0
+        for d in range(zones):
+            part = jnp.sum(jnp.where(marks[d], dgate_back[:, d].reshape(-1)[:, None, None], 0.0), axis=0)
+            gate_grad = gate_grad + (part if d == 0 else shift_to(part, 2 * d))
+        for d in range(1, zones):
+            token_grad = token_grad + shift_to(dx_back[d].astype(BF), 2 * d).astype(F32)
+        dchoice = gates * (gate_grad - jnp.sum(gates * gate_grad, axis=0, keepdims=True))
+        chosen = route_rows[:, None, :] == jnp.arange(experts_all, dtype=jnp.int32)[None, :, None]
+        dlogits = jnp.sum(jnp.where(chosen, dchoice[:, None, :], 0.0), axis=0).astype(BF)
+        grad_router = nn(dlogits, eh)
+        deh = token_grad + tn(dlogits, router_full)
+        unit3 = x3 * inverse_rms(x3)
+        scaled = deh * gains[3]
+        dx3 = cotangent.astype(F32) + inverse_rms(x3) * (
+            scaled - unit3 * jnp.mean(scaled * unit3, axis=1, keepdims=True)
+        )
+        dgain3 = jnp.sum(deh * unit3, axis=0)[None]
     router_rows = jnp.pad(
         grad_router.astype(BF).reshape(owners, local, width), ((0, 0), (0, router_pad - local), (0, 0))
     )

time: 835 us -> 657 us (0.79)
  waiting for transfers between devices: 255 us -> 0.02 us
  Pallas kernels: 450 us -> 569 us
  other arithmetic: 36.1 us -> 16.8 us
  starting transfers between devices: 36.4 us -> 21.6 us
    pallas_call x2 -> x4, Pallas kernels: 169 us -> 305 us  [the longest x1 102 us: gather_weights(): pl.pallas_call(lambda *refs: gather_kernel(owners, zones, used_rows, expe...]
    all_to_all x5 -> x2, waiting for transfers between devices: 96.3 us -> 0.01 us  [exchange(): lax.all_to_all(value, 'expert', split_axis=0, concat_axis=0, tiled=True)]
    ppermute x4 -> x0, waiting for transfers between devices: 77.5 us -> none  [shift_from(): lax.ppermute(value, 'shard', [((z + distance) % size, z) for z in range(s...]
    ppermute x4 -> x3, waiting for transfers between devices: 48.8 us -> 0.01 us  [swap_pair(): lax.ppermute(value, 'shard', [(z, z ^ 1) for z in range(lax.axis_size('sh...]
    ppermute x3 -> x1, waiting for transfers between devices: 32 us -> 0.01 us  [shift_to(): lax.ppermute(value, 'shard', [(z, (z + distance) % size) for z in range(s...]
    all_to_all x5 -> x2, starting transfers between devices: 23.8 us -> 9.78 us  [exchange(): lax.all_to_all(value, 'expert', split_axis=0, concat_axis=0, tiled=True)]
    another operation x6 -> x0, other arithmetic: 13.2 us -> none  [the longest x1 5.06 us: per_device(): up_pair = jnp.stack([expert_up, up_other])]
    unnamed x49 -> x62, local copies, waits for them, and re-layouts: 11.8 us -> 24.6 us
  transfers between devices with their start and end apart: 16 -> 6, of which waited for: 7 -> 0; matrix products, arithmetic and copies ran while one was open for 5% -> 3% of each run, Pallas kernels for 29% -> 34%
where the time goes in v3:
time: 657 us; the launch traced here: 652 us
  Pallas kernels  569 us (87%)
  local copies, waits for them, and re-layouts  40.9 us (6%)
  starting transfers between devices  21.6 us (3%)
  other arithmetic  16.8 us (3%)
    pallas_call x1, Pallas kernels, reduce_grads(): pl.pallas_call(lambda *refs: reduce_kernel(owners, zones, used_rows, *ref...  106 us
    pallas_call x1, Pallas kernels, gather_weights(): pl.pallas_call(lambda *refs: gather_kernel(owners, zones, used_rows, expe...  102 us
    pallas_call x1, Pallas kernels, send_rows(): pl.pallas_call(lambda *refs: send_rows_kernel(owners, zones, capacity, *r...  73.9 us
    pallas_call x2, Pallas kernels, attend_back(): pl.pallas_call(lambda *refs: attend_back_kernel(bool(tails), weights, *re...  70.6 us
    pallas_call x1, Pallas kernels, run_experts(): pl.pallas_call(experts_kernel, grid=(local,), out_shape=(jax.ShapeDtypeSt...  68.4 us
    pallas_call x1, Pallas kernels, return_rows(): pl.pallas_call(lambda *refs: return_rows_kernel(owners, zones, capacity,...  60.4 us
    pallas_call x2, Pallas kernels, attend(): pl.pallas_call(lambda *refs: attend_kernel(weights, *refs), out_shape=(ja...  37.1 us
    unnamed x62, local copies, waits for them, and re-layouts  24.6 us
  transfers between devices with their start and end apart: 6, of which 0 were waited for; matrix products, arithmetic and copies ran while one was open for 3% of the time, Pallas kernels for 34%

profile of v3, /device:TPU:0, one launch (start us, length us, event | category | flops | bytes accessed | tf_op | source)
XLA Modules:
  0.0 651.8 jit_solution(12539100378312102679)
XLA Ops:
  5.2 102.0 %gather_weights.1 = (bf16[8,384,768]{2,1,0:T(8,128)(2,1)S(1)}, bf16[8,384,768]{2,1,0:T(8,128)(2,1)S(1)}, bf16[8,384,768]{2,1,0:T(8,128)(2,1)S(1)}, bf16[8,400,76...) custom-call(bf16[192,384]{1,0:T(8,128)(2,1)S(1)} %pad_maximum_fusion.3.refs_0_, ...), custom_call_target="tpu_custom_call" | custom-call | tf_op jit(solution)/shard_map/gather_weights/pallas_call | solution.py:614
  107.2 2.2 copy-done.12
  109.4 2.2 copy-done.13
  111.6 2.2 copy-done.14
  113.8 2.2 copy-done.15
  117.3 6.7 %spread.1 = bf16[16,2,96,768]{3,2,1,0:T(8,128)(2,1)} custom-call(f32[2,8,512]{2,1,0:T(8,128)} %copy-done.9, bf16[2,512,768]{2,1,0:T(8,128)(2,1)} %pad_maximum_fusion.rows_ref), custom_call_target="tpu_custom_call" | custom-call | flops 2415919104 | bytes 6291456 | tf_op jit(solution)/shard_map/spread/pallas_call | solution.py:1242
  124.0 4.9 all-to-all-start
  128.9 8.1 %collective-permute-start = (bf16[2,768,768]{2,1,0:T(8,128)(2,1)}, bf16[2,768,768]{2,1,0:T(8,128)(2,1)}, u32[]{:S(2)}, u32[]{:S(2)}) collective-permute-start(bf16[2,768,768]{2,1,0:T(8,128)(2,1)} %own_up_in.1), channel_id=1, source_target_pairs={{0,1},{1,0},{2,3},{3,2},{4,5},{5,4},{6,7},{7,6},{8,9},{9,8},{10,11... | collective-permute-start | bytes 7077896 | tf_op jit(solution)/shard_map/ppermute | solution.py:1315
  141.6 18.5 %attend.2 = (f32[512,768]{1,0:T(8,128)}, bf16[512,768]{1,0:T(8,128)(2,1)}, bf16[512,2304]{1,0:T(8,128)(2,1)}, bf16[512,768]{1,0:T(8,128)(2,1)}, f32[12,512]{1,0:T(8,128)}) custom-call(s32[1]{0:T(128)S(6)} %copy.45.refs_0_, f32[512,768]{1,0:T(8,128)} %convert_element_type.35.refs_1_, f32[1,768]{1,0:T(1,128)} %get-tuple-element.174.refs_2_, ...), custom_call_target="tpu_custom_call" | custom-call | flops 3221225472 | bytes 12582912 | tf_op jit(solution)/shard_map/attend/pallas_call | solution.py:159
  160.1 12.0 %mlp.1 = (f32[512,768]{1,0:T(8,128)}, bf16[512,768]{1,0:T(8,128)(2,1)}) custom-call(f32[512,768]{1,0:T(8,128)} %get-tuple-element.78.refs_0_, f32[1,768]{1,0:T(1,128)} %get-tuple-element.173.refs_1_, bf16[3072,768]{1,0:T(8,128)(2,1)} %bitcast.60, bf16[8,384,768]{2,1,0:T(8,128)(2,1)} %copy-done.15), custom_call_target="tpu_custom_call" | custom-call | flops 4831838208 | bytes 13369344 | tf_op jit(solution)/shard_map/mlp/pallas_call | solution.py:386
  172.0 18.6 %attend.3 = (f32[512,768]{1,0:T(8,128)}, bf16[512,768]{1,0:T(8,128)(2,1)}, bf16[512,2304]{1,0:T(8,128)(2,1)}, bf16[512,768]{1,0:T(8,128)(2,1)}, f32[12,512]{1,0:T(8,128)}) custom-call(s32[1]{0:T(128)S(6)} %copy.45.refs_0_, f32[512,768]{1,0:T(8,128)} %get-tuple-element.82.refs_1_, f32[1,768]{1,0:T(1,128)} %get-tuple-element.175.refs_2_, ...), custom_call_target="tpu_custom_call" | custom-call | flops 3221225472 | bytes 12582912 | tf_op jit(solution)/shard_map/attend/pallas_call | solution.py:159
  193.7 73.9 %send_rows.1 = (bf16[512,768]{1,0:T(8,128)(2,1)S(1)}, f32[8,512]{1,0:T(8,128)S(1)}, bf16[8,2,192,768]{3,2,1,0:T(8,128)(2,1)S(1)}, f32[8,2,192,1]{3,2,1,0:T(8,128)S(1)}, bf16[2,768,768]{2,1,0:T(8,128)(2,1)S(1)}) custom-call(f32[512,768]{1,0:T(8,128)S(1)} %copy-done.2, f32[1,768]{1,0:T(1,128)S(1)} %get-tuple-element.172.refs_1_.refs_6_, ...), custom_call_target="tpu_custom_call" | custom-call | tf_op jit(solution)/shard_map/send_rows/pallas_call | solution.py:937
  267.7 2.2 copy-done.16
  272.5 68.4 %experts.1 = (bf16[8,2,192,768]{3,2,1,0:T(8,128)(2,1)}, bf16[8,2,192,768]{3,2,1,0:T(8,128)(2,1)}, f32[8,2,192,1]{3,2,1,0:T(8,128)}, f32[2,768,768]{2,1,0:T(8,128...) custom-call(bf16[8,2,192,768]{3,2,1,0:T(8,128)(2,1)} %copy-done.16, ...), custom_call_target="tpu_custom_call" | custom-call | flops 43486543872 | bytes 37748736 | tf_op jit(solution)/shard_map/experts/pallas_call | solution.py:1199
  340.9 2.3 copy-done.5
  344.7 60.4 %return_rows.1 = (f32[512,768]{1,0:T(8,128)S(1)}, f32[1,768]{1,0:T(1,128)S(1)}, f32[16,768]{1,0:T(8,128)S(1)}) custom-call(bf16[8,2,192,768]{3,2,1,0:T(8,128)(2,1)S(1)} %copy-done.5, f32[8,2,192,1]{3,2,1,0:T(8,128)S(1)} %copy-done.7, f32[2,8,512]{2,1,0:T(8,128)S(1)} %copy-done.10, f32[8,512]{1,0:T(8,128)S(1)} %get-tuple-element.100.refs_3_, ...), custom_call_target="tpu_custom_call" | custom-call | tf_op jit(solution)/shard_map/return_rows/pallas_call | solution.py:1106
  407.0 35.3 %attend_back.2 = (f32[512,768]{1,0:T(8,128)}, bf16[8,400,768]{2,1,0:T(8,128)(2,1)}, f32[12,1024]{1,0:T(8,128)}, f32[1,768]{1,0:T(1,128)}) custom-call(s32[1]{0:T(128)S(6)} %copy.45.refs_0_, f32[512,768]{1,0:T(8,128)} %get-tuple-element.82.refs_1_, f32[1,768]{1,0:T(1,128)} %get-tuple-element.175.refs_2_, bf16[8,400,768]{2,1,0:T(8,128)(2,1)} %copy-done.12, ...), custom_call_target="tpu_custom_call" | custom-call | flops 6845104128 | bytes 25165824 | tf_op jit(solution)/shard_map/attend_back/pallas_call | solution.py:324
  442.3 4.8 all-to-all-start.1
  449.3 22.8 %mlp_back.1 = (f32[512,768]{1,0:T(8,128)}, bf16[3072,768]{1,0:T(8,128)(2,1)}, bf16[8,384,768]{2,1,0:T(8,128)(2,1)}, f32[1,768]{1,0:T(1,128)}) custom-call(f32[512,768]{1,0:T(8,128)} %get-tuple-element.78.refs_0_, f32[1,768]{1,0:T(1,128)} %get-tuple-element.173.refs_1_, bf16[3072,768]{1,0:T(8,128)(2,1)} %bitcast.61, bf16[8,384,768]{2,1,0:T(8,128)(2,1)} %copy-done.15, ...), custom_call_target="tpu_custom_call" | custom-call | flops 12079595520 | bytes 25165824 | tf_op jit(solution)/shard_map/mlp_back/pallas_call | solution.py:428
  472.0 35.3 %attend_back.3 = (f32[512,768]{1,0:T(8,128)}, bf16[8,384,768]{2,1,0:T(8,128)(2,1)}, f32[12,1024]{1,0:T(8,128)}, f32[1,768]{1,0:T(1,128)}) custom-call(s32[1]{0:T(128)S(6)} %copy.45.refs_0_, f32[512,768]{1,0:T(8,128)} %convert_element_type.35.refs_1_, f32[1,768]{1,0:T(1,128)} %get-tuple-element.174.refs_2_, bf16[8,384,768]{2,1,0:T(8,128)(2,1)} %copy-done.13, ...), custom_call_target="tpu_custom_call" | custom-call | flops 6845104128 | bytes 25165824 | tf_op jit(solution)/shard_map/attend_back/pallas_call | solution.py:324
  509.2 8.7 %collect.1 = f32[2,512,768]{2,1,0:T(8,128)} custom-call(f32[2,8,512]{2,1,0:T(8,128)} %copy-done.9, bf16[16,2,96,768]{3,2,1,0:T(8,128)(2,1)} %bitcast.13.rows_ref), custom_call_target="tpu_custom_call" | custom-call | flops 2415919104 | bytes 7864320 | tf_op jit(solution)/shard_map/collect/pallas_call | solution.py:1275
  517.9 2.4 fusion.3
  522.5 106.5 %reduce_grads.1 = (f32[192,512]{1,0:T(8,128)}, f32[192,384]{1,0:T(8,128)}, f32[192,384]{1,0:T(8,128)}, f32[192,384]{1,0:T(8,128)}, f32[40,128]{1,0:T(8,128)}) custom-call(bf16[4,2,400,768]{3,2,1,0:T(8,128)(2,1)} %bitcast.62, bf16[4,2,384,768]{3,2,1,0:T(8,128)(2,1)} %bitcast.64, bf16[4,2,384,768]{3,2,1,0:T(8,128)(2,1)} %bitcast.65, ...), custom_call_target="tpu_custom_call" | custom-call | tf_op jit(solution)/shard_map/reduce_grads/pallas_call | solution.py:775
  640.8 9.8 %convert_add_fusion = (f32[2,768,768]{2,1,0:T(8,128)}, f32[2,768,768]{2,1,0:T(8,128)}) fusion(f32[2,768,768]{2,1,0:T(8,128)} %get-tuple-element.131, bf16[2,768,768]{2,1,0:T(8,128)(2,1)} %collective-permute-done.3, f32[2,768,768]{2,1,0:T(8,128)} %get-tuple-element.129, bf16[2,768,768]{2,1,0:T(8,128)(2,1)} %collective-permute-done.2), kind=kLoop, calls=%fused_computation | loop fusion | flops 4718592 | bytes 23592960 | tf_op jit(solution)/shard_map/add | solution.py:1470
  (105 shorter events, 37.3 us)
Async XLA Ops:
  0.6 140.1 %copy-start = (f32[2,12,44]{2,0,1:T(2,128)S(1)}, f32[2,12,44]{2,0,1:T(2,128)}, u32[]{:S(2)}) copy-start(f32[2,12,44]{2,0,1:T(2,128)} %param.18) | copy-start | bytes 12676
  0.7 4.5 copy-start.4
  0.7 4.5 copy-start.8
  0.7 4.5 copy-start.11
  107.2 2.2 copy-start.12
  124.0 13.7 %copy-start.21 = (bf16[512,768]{1,0:T(8,128)(2,1)S(1)}, bf16[512,768]{1,0:T(8,128)(2,1)}, u32[]{:S(2)}) copy-start(bf16[512,768]{1,0:T(8,128)(2,1)} %param.14) | copy-start | bytes 2359300
  124.0 66.7 %all-to-all-start = ((bf16[8,2,192,768]{3,2,1,0:T(8,128)(2,1)}), bf16[8,2,192,768]{3,2,1,0:T(8,128)(2,1)}, u32[]{:S(2)}, u32[]{:S(2)}) async-start(bf16[8,2,192,768]{3,2,1,0:T(8,128)(2,1)} %bitcast.63), calls=%async_computation | async-start | bytes 9437184 | tf_op jit(solution)/shard_map/all_to_all | solution.py:1319
  128.9 11.0 %copy-start.27 = (s32[21]{0:T(128)S(1)}, s32[21]{0:T(128)}, u32[]{:S(2)}) copy-start(s32[21]{0:T(128)} %constant.16.clone) | copy-start | bytes 256
  128.9 11.1 %copy-start.24 = (f32[4,768]{1,0:T(4,128)S(1)}, f32[4,768]{1,0:T(4,128)}, u32[]{:S(2)}) copy-start(f32[4,768]{1,0:T(4,128)} %param.17) | copy-start | bytes 36868
  128.9 61.7 %collective-permute-start = (bf16[2,768,768]{2,1,0:T(8,128)(2,1)}, bf16[2,768,768]{2,1,0:T(8,128)(2,1)}, u32[]{:S(2)}, u32[]{:S(2)}) collective-permute-start(bf16[2,768,768]{2,1,0:T(8,128)(2,1)} %own_up_in.1), channel_id=1, source_target_pairs={{0,1},{1,0},{2,3},{3,2},{4,5},{5,4},{6,7},{7,6},{8,9},{9,8},{10,11... | collective-permute-start | bytes 7077896 | tf_op jit(solution)/shard_map/ppermute | solution.py:1315
  172.0 18.6 %copy-start.10 = (f32[2,8,512]{2,1,0:T(8,128)S(1)}, f32[2,8,512]{2,1,0:T(8,128)}, u32[]{:S(2)}) copy-start(f32[2,8,512]{2,1,0:T(8,128)} %copy-done.9) | copy-start | bytes 98308
  272.5 68.4 %copy-start.3 = (f32[512,768]{1,0:T(8,128)S(1)}, f32[512,768]{1,0:T(8,128)}, u32[]{:S(2)}) copy-start(f32[512,768]{1,0:T(8,128)} %get-tuple-element.92.refs_0_.refs_5_) | copy-start | bytes 4718596
  340.9 2.3 copy-start.5
  442.3 66.9 %all-to-all-start.1 = ((bf16[8,2,192,768]{3,2,1,0:T(8,128)(2,1)}), bf16[8,2,192,768]{3,2,1,0:T(8,128)(2,1)}, u32[]{:S(2)}, u32[]{:S(2)}) async-start(bf16[8,2,192,768]{3,2,1,0:T(8,128)(2,1)} %get-tuple-element.109), calls=%async_computation.1 | async-start | bytes 9437184 | tf_op jit(solution)/shard_map/all_to_all | solution.py:1319
  447.2 193.6 %collective-permute-start.2 = (bf16[2,768,768]{2,1,0:T(8,128)(2,1)}, bf16[2,768,768]{2,1,0:T(8,128)(2,1)}, u32[]{:S(2)}, u32[]{:S(2)}) collective-permute-start(bf16[2,768,768]{2,1,0:T(8,128)(2,1)} %get-tuple-element.110), channel_id=1, source_target_pairs={{0,1},{1,0},{2,3},{3,2},{4,5},{5,4},{6,7},{7,6},{8,9},{9,8},{10,11... | collective-permute-start | bytes 7077896 | tf_op jit(solution)/shard_map/ppermute | solution.py:1315
  448.8 191.9 %collective-permute-start.3 = (bf16[2,768,768]{2,1,0:T(8,128)(2,1)}, bf16[2,768,768]{2,1,0:T(8,128)(2,1)}, u32[]{:S(2)}, u32[]{:S(2)}) collective-permute-start(bf16[2,768,768]{2,1,0:T(8,128)(2,1)} %get-tuple-element.111), channel_id=1, source_target_pairs={{0,1},{1,0},{2,3},{3,2},{4,5},{5,4},{6,7},{7,6},{8,9},{9,8},{10,11... | collective-permute-start | bytes 7077896 | tf_op jit(solution)/shard_map/ppermute | solution.py:1315
  472.0 35.3 %copy-start.28 = (f32[12,1024]{1,0:T(8,128)S(1)}, f32[12,1024]{1,0:T(8,128)}, u32[]{:S(2)}) copy-start(f32[12,1024]{1,0:T(8,128)} %get-tuple-element.123) | copy-start | bytes 147460
  472.0 36.5 %copy-start.25 = (f32[1,768]{1,0:T(1,128)S(1)}, f32[1,768]{1,0:T(1,128)}, u32[]{:S(2)}) copy-start(f32[1,768]{1,0:T(1,128)} %get-tuple-element.120) | copy-start | bytes 9220
  472.0 36.5 %copy-start.26 = (f32[1,768]{1,0:T(1,128)S(1)}, f32[1,768]{1,0:T(1,128)}, u32[]{:S(2)}) copy-start(f32[1,768]{1,0:T(1,128)} %get-tuple-element.119) | copy-start | bytes 9220
  520.3 119.2 %collective-permute-start.1 = (bf16[512,768]{1,0:T(8,128)(2,1)}, bf16[512,768]{1,0:T(8,128)(2,1)S(1)}, u32[]{:S(2)}, u32[]{:S(2)}) collective-permute-start(bf16[512,768]{1,0:T(8,128)(2,1)} %fusion.3), channel_id=1, source_target_pairs={{0,2},{1,3},{2,0},{3,1},{4,6},{5,7},{6,4},{7,5},{8,10},{9,11},{10,... | collective-permute-start | bytes 2359304 | tf_op jit(solution)/shard_map/ppermute | solution.py:1311
  629.0 6.8 %copy-start.22 = (f32[192,512]{1,0:T(8,128)S(1)}, f32[192,512]{1,0:T(8,128)}, u32[]{:S(2)}) copy-start(f32[192,512]{1,0:T(8,128)} %get-tuple-element.126) | copy-start | bytes 1179652
  635.8 3.7 copy-start.20
  640.8 9.8 %copy-start.23 = (f32[192,384]{1,0:T(8,128)S(1)}, f32[192,384]{1,0:T(8,128)}, u32[]{:S(2)}) copy-start(f32[192,384]{1,0:T(8,128)} %get-tuple-element.199) | copy-start | bytes 884740
  640.8 10.5 %copy-start.1 = (f32[2,12,44]{2,0,1:T(2,128)S(1)}, f32[2,12,44]{2,0,1:T(2,128)}, u32[]{:S(2)}) copy-start(f32[2,12,44]{2,0,1:T(2,128)} %param.18) | copy-start | bytes 12676
  (11 other events, 18.4 us)

commit v4 on v3

--- a/solution.py
+++ b/solution.py
@@ -57,10 +57,20 @@
     strip_ref[...] = pltpu.roll(wide, vector_row.shape[1] - 127, 1, stride=1, stride_axis=0)
 
 
-def flatten(blocks_ref, flat_ref):
+def flatten(blocks_ref, flat_ref, sems):
     rows = blocks_ref.shape[1]
-    for i in range(blocks_ref.shape[0]):
-        flat_ref[i * rows:i * rows + rows, :] = blocks_ref[i]
+    copies = [
+        pltpu.make_async_copy(blocks_ref.at[i], flat_ref.at[pl.ds(i * rows, rows), :], sems.at[i])
+        for i in range(blocks_ref.shape[0])
+    ]
+    for copy in copies:
+        copy.start()
+    return copies
+
+
+def arrive(copies):
+    for copy in copies:
+        copy.wait()
 
 
 def unflatten(flat_ref, blocks_ref, start):
@@ -73,8 +83,14 @@
 def weight_specs(weights):
     packed, qkv_rows, out_rows = weights
     if isinstance(packed, tuple):
-        return list(packed), [VMEM_SPEC, VMEM_SPEC]
-    return [packed], [VMEM_SPEC]
+        return list(packed), [HBM_SPEC, HBM_SPEC]
+    return [packed], [HBM_SPEC]
+
+
+def weight_sems(weights):
+    packed = weights[0]
+    count = 1 if isinstance(packed, tuple) else packed.shape[0]
+    return [pltpu.SemaphoreType.DMA((count,)), pltpu.SemaphoreType.DMA((count,))]
 
 
 def weight_views(weights, refs):
@@ -89,14 +105,16 @@
 ):
     w_ref, wo_ref, refs = weight_views(weights, refs)
     (vec_ref, out_ref, normed_ref, qkv_ref, mixed_ref, lse_ref,
-     mask_ref, strip_ref, score_ref, prob_ref, flat_ref, flat_out_ref) = refs
+     mask_ref, strip_ref, score_ref, prob_ref, flat_ref, flat_out_ref, w_sem, wo_sem) = refs
     length, width = x_ref.shape
-    flatten(w_ref, flat_ref)
-    flatten(wo_ref, flat_out_ref)
+    w_copies = flatten(w_ref, flat_ref, w_sem)
+    wo_copies = flatten(wo_ref, flat_out_ref, wo_sem)
     tiles = length // 128
     fill_mask(piece_ref, mask_ref)
     field = x_ref[...]
     normed_ref[...] = (field * inverse_rms(field) * gain_ref[...]).astype(BF)
+
+    arrive(w_copies)
 
     def project(c, _):
         cols = pl.ds(pl.multiple_of(c * 256, 256), 256)
@@ -139,6 +157,8 @@
 
     lax.fori_loop(0, width // 128, pair, 0)
 
+    arrive(wo_copies)
+
     def back(c, _):
         cols = pl.ds(pl.multiple_of(c * 256, 256), 256)
         out_ref[:, cols] = x_ref[:, cols] + nt(mixed_ref[...], flat_out_ref[cols, :])
@@ -147,6 +167,7 @@
     lax.fori_loop(0, width // 256, back, 0)
 
 
+HBM_SPEC = pl.BlockSpec(memory_space=pltpu.HBM)
 SMEM_SPEC = pl.BlockSpec(memory_space=pltpu.SMEM)
 VMEM_SPEC = pl.BlockSpec(memory_space=pltpu.VMEM)
 
@@ -174,7 +195,7 @@
             pltpu.VMEM((length, length), BF),
             pltpu.VMEM((3 * width, width), BF),
             pltpu.VMEM((width, width), BF),
-        ],
+        ] + weight_sems(weights),
         compiler_params=pltpu.CompilerParams(vmem_limit_bytes=VMEM_BYTES),
         cost_estimate=pl.CostEstimate(
             flops=8 * length * width * width + 4 * length * length * width,
@@ -186,22 +207,30 @@
 
 
 def attend_back_kernel(
-    tail, weights, piece_ref, x_ref, gain_ref, *refs
+    tail, weights, ride, piece_ref, x_ref, gain_ref, *refs
 ):
+    ride_refs, refs = (refs[len(refs) - ride.scratch:], refs[:len(refs) - ride.scratch]) if ride else ((), refs)
     w_ref, wo_ref, refs = weight_views(weights, refs)
     (vec_ref, normed_ref, qkv_ref, mixed_ref, lse_ref, grad_ref), refs = refs[:6], refs[6:]
     tail_ref, refs = (refs[0], refs[1:]) if tail else (None, refs)
-    grad_refs, refs = (refs[1:len(refs) - 14], refs[:1] + refs[len(refs) - 14:])
+    rides_in, refs = (refs[:ride.inputs], refs[ride.inputs:]) if ride else ((), refs)
+    rides_out, refs = (refs[:ride.outputs], refs[ride.outputs:]) if ride else ((), refs)
+    grad_refs, refs = (refs[1:len(refs) - 15], refs[:1] + refs[len(refs) - 15:])
     (dx_ref, dvec_ref, dgain_ref,
      mask_ref, strip_ref, sums_ref, prob_ref, ds_ref, low_ref, do_ref, dqkv_ref, delta_ref,
-     flat_ref, flat_out_ref, dw_ref) = refs
-    flatten(w_ref, flat_ref)
-    flatten(wo_ref, flat_out_ref)
+     flat_ref, flat_out_ref, w_sem, wo_sem) = refs
+    wo_copies = flatten(wo_ref, flat_out_ref, wo_sem)
+    w_copies = flatten(w_ref, flat_ref, w_sem)
+    turns, rows_turn, end = (
+        ride.board(rides_in, rides_out, ride_refs, dx_ref, low_ref) if ride else ([], None, None)
+    )
     length, width = x_ref.shape
     heads = vec_ref.shape[0]
     tiles = length // 128
     fill_mask(piece_ref, mask_ref)
     low_ref[...] = grad_ref[...].astype(BF)
+
+    arrive(wo_copies)
 
     def out_back(c, _):
         cols = pl.ds(pl.multiple_of(c * 256, 256), 256)
@@ -233,6 +262,10 @@
     sums_ref[...] = jnp.zeros_like(sums_ref)
 
     def pair(hp, _):
+        if rows_turn is not None:
+            pl.when(hp == 0)(rows_turn)
+        for at, turn in enumerate(turns):
+            pl.when(hp == min(1 + 3 * at, width // 128 - 1))(turn)
         base = hp * 128
         q_cols = pl.ds(pl.multiple_of(base, 128), 128)
         k_cols = pl.ds(pl.multiple_of(width + base, 128), 128)
@@ -281,12 +314,7 @@
 
     lax.fori_loop(0, width // 128, pair, 0)
 
-    def weights_back(c, _):
-        cols = pl.ds(pl.multiple_of(c * 256, 256), 256)
-        dw_ref[cols, :] = tn(dqkv_ref[:, cols], normed_ref[...]).astype(BF)
-        return 0
-
-    lax.fori_loop(0, 3 * width // 256, weights_back, 0)
+    arrive(w_copies)
 
     def rows_back(c, _):
         cols = pl.ds(pl.multiple_of(c * 256, 256), 256)
@@ -294,14 +322,23 @@
         return 0
 
     lax.fori_loop(0, width // 256, rows_back, 0)
+    def weights_back(c, _):
+        cols = pl.ds(pl.multiple_of(c * 256, 256), 256)
+        flat_ref[cols, :] = tn(dqkv_ref[:, cols], normed_ref[...]).astype(BF)
+        return 0
+
+    lax.fori_loop(0, 3 * width // 256, weights_back, 0)
+
     qkv_rows = w_ref.shape[1]
-    unflatten(dw_ref, grad_refs[0], 0)
+    unflatten(flat_ref, grad_refs[0], 0)
     unflatten(flat_out_ref, grad_refs[-1], qkv_rows if len(grad_refs) == 1 else 0)
     if tail:
         start = qkv_rows + wo_ref.shape[1]
         for i in range(tail_ref.shape[0]):
             grad_refs[0][i, start:, :] = tail_ref[i]
     norm_back(x_ref, gain_ref, dx_ref, grad_ref, dx_ref, dgain_ref)
+    if ride:
+        end()
 
 
 def norm_back(x_ref, gain_ref, upper_ref, base_ref, dx_ref, dgain_ref):
@@ -314,7 +351,7 @@
     dx_ref[...] = base_ref[...] + inverse * (scaled - unit * jnp.mean(scaled * unit, axis=1, keepdims=True))
 
 
-def attend_back(piece, x, gain, weights, vectors, normed, qkv, mixed, lse, grad, tail=None):
+def attend_back(piece, x, gain, weights, vectors, normed, qkv, mixed, lse, grad, tail=None, ride=None):
     length, width = x.shape
     heads, span = vectors.shape
     w_args, w_specs = weight_specs(weights)
@@ -322,15 +359,16 @@
     grad_shapes = packed if isinstance(packed, tuple) else (packed,)
     tails = () if tail is None else (tail,)
     return pl.pallas_call(
-        lambda *refs: attend_back_kernel(bool(tails), weights, *refs),
-        out_shape=(jax.ShapeDtypeStruct((length, width), F32),)
+        lambda *refs: attend_back_kernel(bool(tails), weights, ride, *refs),
+        out_shape=(tuple(ride.out_shape) if ride else ())
+        + (jax.ShapeDtypeStruct((length, width), F32),)
         + tuple(jax.ShapeDtypeStruct(g.shape, BF) for g in grad_shapes)
         + (
             jax.ShapeDtypeStruct((heads, span), F32),
             jax.ShapeDtypeStruct((1, width), F32),
         ),
-        in_specs=[SMEM_SPEC] + [VMEM_SPEC] * 2 + w_specs + [VMEM_SPEC] * (6 + len(tails)),
-        out_specs=[VMEM_SPEC] * (3 + len(grad_shapes)),
+        in_specs=[SMEM_SPEC] + [VMEM_SPEC] * 2 + w_specs + [VMEM_SPEC] * (6 + len(tails)) + (ride.in_specs if ride else []),
+        out_specs=(ride.out_specs if ride else []) + [VMEM_SPEC] * (3 + len(grad_shapes)),
         scratch_shapes=[
             pltpu.VMEM((length, length), F32),
             pltpu.VMEM((128, span), F32),
@@ -343,16 +381,15 @@
             pltpu.VMEM((16, length), F32),
             pltpu.VMEM((3 * width, width), BF),
             pltpu.VMEM((width, width), BF),
-            pltpu.VMEM((3 * width, width), BF),
-        ],
-        compiler_params=pltpu.CompilerParams(vmem_limit_bytes=VMEM_BYTES),
+        ] + weight_sems(weights) + (ride.scratch_shapes if ride else []),
+        compiler_params=ride.params if ride else pltpu.CompilerParams(vmem_limit_bytes=VMEM_BYTES),
         cost_estimate=pl.CostEstimate(
             flops=16 * length * width * width + 10 * length * length * width,
             bytes_accessed=40 * length * width + 16 * width * width,
             transcendentals=heads * length * length,
         ),
         name="attend_back",
-    )(piece, x, gain, *w_args, vectors, normed, qkv, mixed, lse, grad, *tails)
+    )(piece, x, gain, *w_args, vectors, normed, qkv, mixed, lse, grad, *tails, *(ride.args if ride else []))
 
 
 def mlp_chunk(c, parts, zones, up_ref, down_ref):
@@ -366,12 +403,38 @@
     return jnp.concatenate(rows, axis=0), down
 
 
-def mlp_kernel(parts, zones, x_ref, gain_ref, up_ref, down_ref, out_ref, normed_ref):
+def mlp_loads(parts, zones, up_hbm, down_hbm, up_ref, down_ref, sems):
+    piece = up_ref.shape[0] // (parts * zones)
+    span = down_ref.shape[1] // parts
+    loads = []
+    for c in range(parts):
+        chunk = [
+            pltpu.make_async_copy(
+                up_hbm.at[pl.ds((z * parts + c) * piece, piece), :],
+                up_ref.at[pl.ds((z * parts + c) * piece, piece), :], sems.at[c, z],
+            )
+            for z in range(zones)
+        ]
+        columns = pl.ds(c * span, span)
+        chunk.append(
+            pltpu.make_async_copy(down_hbm.at[:, columns, :], down_ref.at[:, columns, :], sems.at[c, zones])
+        )
+        loads.append(chunk)
+    for chunk in loads:
+        for copy in chunk:
+            copy.start()
+    return loads
+
+
+def mlp_kernel(parts, zones, x_ref, gain_ref, up_hbm, down_hbm, out_ref, normed_ref, up_ref, down_ref, sems):
+    loads = mlp_loads(parts, zones, up_hbm, down_hbm, up_ref, down_ref, sems)
     field = x_ref[...]
     normed_ref[...] = (field * inverse_rms(field) * gain_ref[...]).astype(BF)
     out_ref[...] = field
 
     def chunk(c, _):
+        for at, copies in enumerate(loads):
+            pl.when(c == at)(lambda copies=copies: arrive(copies))
         up, down = mlp_chunk(c, parts, zones, up_ref, down_ref)
         hidden = gelu_of(nt(normed_ref[...], up)).astype(BF)
         out_ref[...] += nt(hidden, down)
@@ -386,8 +449,11 @@
     return pl.pallas_call(
         lambda *refs: mlp_kernel(parts, zones, *refs),
         out_shape=(jax.ShapeDtypeStruct((length, width), F32), jax.ShapeDtypeStruct((length, width), BF)),
-        in_specs=[VMEM_SPEC] * 4,
+        in_specs=[VMEM_SPEC] * 2 + [HBM_SPEC] * 2,
         out_specs=[VMEM_SPEC] * 2,
+        scratch_shapes=[
+            pltpu.VMEM(up.shape, BF), pltpu.VMEM(down.shape, BF), pltpu.SemaphoreType.DMA((parts, zones + 1))
+        ],
         compiler_params=pltpu.CompilerParams(vmem_limit_bytes=VMEM_BYTES),
         cost_estimate=pl.CostEstimate(
             flops=4 * length * width * hidden, bytes_accessed=10 * length * width + 4 * width * hidden,
@@ -397,8 +463,9 @@
     )(x, gain, up, down)
 
 
-def mlp_back_kernel(parts, zones, x_ref, gain_ref, up_ref, down_ref, normed_ref, grad_ref,
-                    dx_ref, dup_ref, ddown_ref, dgain_ref, low_ref, acc_ref):
+def mlp_back_kernel(parts, zones, x_ref, gain_ref, up_hbm, down_hbm, normed_ref, grad_ref,
+                    dx_ref, dup_ref, ddown_ref, dgain_ref, low_ref, acc_ref, up_ref, down_ref, sems):
+    loads = mlp_loads(parts, zones, up_hbm, down_hbm, up_ref, down_ref, sems)
     low_ref[...] = grad_ref[...].astype(BF)
     acc_ref[...] = jnp.zeros_like(acc_ref)
 
@@ -406,6 +473,8 @@
     span = down_ref.shape[1] // parts
 
     def chunk(c, _):
+        for at, copies in enumerate(loads):
+            pl.when(c == at)(lambda copies=copies: arrive(copies))
         up, down = mlp_chunk(c, parts, zones, up_ref, down_ref)
         hidden, slope = gelu_parts(nt(normed_ref[...], up))
         pre_grad = (nn(low_ref[...], down) * slope).astype(BF)
@@ -433,9 +502,12 @@
             jax.ShapeDtypeStruct(down.shape, BF),
             jax.ShapeDtypeStruct((1, width), F32),
         ),
-        in_specs=[VMEM_SPEC] * 6,
+        in_specs=[VMEM_SPEC] * 2 + [HBM_SPEC] * 2 + [VMEM_SPEC] * 2,
         out_specs=[VMEM_SPEC] * 4,
-        scratch_shapes=[pltpu.VMEM((length, width), BF), pltpu.VMEM((length, width), F32)],
+        scratch_shapes=[
+            pltpu.VMEM((length, width), BF), pltpu.VMEM((length, width), F32),
+            pltpu.VMEM(up.shape, BF), pltpu.VMEM(down.shape, BF), pltpu.SemaphoreType.DMA((parts, zones + 1)),
+        ],
         compiler_params=pltpu.CompilerParams(vmem_limit_bytes=VMEM_BYTES),
         cost_estimate=pl.CostEstimate(
             flops=10 * length * width * hidden, bytes_accessed=16 * length * width + 8 * width * hidden,
@@ -515,8 +587,10 @@
 def gather_kernel(owners, zones, used_rows, experts, capacity, *refs):
     count = len(used_rows)
     blocks, (late_ref, route_ref), refs = refs[:count], refs[count:count + 2], refs[count + 2:]
-    outs, (near_ref, slot_ref), refs = refs[:count], refs[count:count + 2], refs[count + 2:]
+    outs, (slot_ref, spread_ref), refs = refs[:count], refs[count:count + 2], refs[count + 2:]
     slabs, turned = refs[:count], refs[count:2 * count]
+    direct = capacity % 16 == 0
+    near_ref, refs = (refs[2 * count], refs[:2 * count] + refs[2 * count + 1:]) if direct else (spread_ref, refs)
     slot_in_ref, send_sem, recv_sem, local_sem = refs[2 * count:]
     owner, zone = lax.axis_index("expert"), lax.axis_index("shard")
     greet(owner, zone, owners, zones)
@@ -577,30 +651,47 @@
     moving = {0: across(0)}
     states = {}
     slot_ref[0] = token_slots(route_ref[...], experts, capacity)
-    slot_copies = []
-    for d in range(1, zones // 2):
-        device = (owner, (zone + zones - 2 * d) % zones)
-        slot_copies.append(send(slot_ref.at[0], slot_in_ref.at[d - 1], device))
+    near_copies = []
+
+    def spread_zone(d):
+        if not direct:
+            return
+        take = max(1, 384 // capacity)
+        rows = late_ref if d == 0 else near_ref.at[d - 1]
+
+        def chunk(i, _):
+            hits = slot_hits(slot_ref[d], i * (take * capacity), take * capacity)
+            picked = nn(hits[0] + hits[1], rows[...]).reshape(take, capacity, rows.shape[1])
+            spread_ref[pl.ds(i * take, take), d] = picked.astype(BF)
+            return 0
+
+        lax.fori_loop(0, experts // take, chunk, 0)
+
     for g in range(count):
         states[g] = start_rows(g, moving[g])
         if g + 1 < count:
             moving[g + 1] = across(g + 1)
-        else:
+        if g == count - 1:
             for d in range(1, zones // 2):
                 device = (owner, (zone + zones - 2 * d) % zones)
-                finals.append(send(late_ref, near_ref.at[d - 1], device))
+                near_copies.append(send(slot_ref.at[0], slot_in_ref.at[d - 1], device))
+                near_copies.append(send(late_ref, near_ref.at[d - 1], device))
+        if g == 1:
+            spread_zone(0)
         if g > 0:
             for step in range(1, steps):
                 states[g - 1] = finish_rows(g - 1, states[g - 1], step)
         states[g] = finish_rows(g, states[g], 0)
     for step in range(1, steps):
         states[count - 1] = finish_rows(count - 1, states[count - 1], step)
+    for copy in near_copies:
+        copy.wait_recv()
     for d in range(1, zones // 2):
-        slot_copies[d - 1].wait_recv()
         slot_ref[d] = slot_in_ref[d - 1]
+        spread_zone(d)
     for copy in finals:
         copy.wait_recv()
-    for copy in pending + finals + slot_copies:
+    for copy in pending + finals + near_copies:
         copy.wait_send()
 
 
@@ -611,185 +702,481 @@
     copies = count * gather_copies(owners, zones) + 2 * (groups - 1)
     length = route_rows.shape[1]
     any_spec = pl.BlockSpec(memory_space=pltpu.HBM)
+    direct = capacity % 16 == 0
+    near_shape = (groups - 1,) + late.shape
+    if direct:
+        spread_shape, late_spec = (experts, groups, capacity, late.shape[1]), VMEM_SPEC
+    else:
+        spread_shape, late_spec = near_shape, any_spec
     return pl.pallas_call(
         lambda *refs: gather_kernel(owners, zones, used_rows, experts, capacity, *refs),
         out_shape=tuple(jax.ShapeDtypeStruct((owners, used, depth), BF) for used in used_rows)
         + (
-            jax.ShapeDtypeStruct((groups - 1,) + late.shape, late.dtype),
             jax.ShapeDtypeStruct((groups, 8, length), F32),
+            jax.ShapeDtypeStruct(spread_shape, BF),
         ),
-        in_specs=[VMEM_SPEC] * count + [any_spec, VMEM_SPEC],
-        out_specs=tuple([any_spec] * (count + 1)) + (VMEM_SPEC,),
+        in_specs=[VMEM_SPEC] * count + [late_spec, VMEM_SPEC],
+        out_specs=tuple([any_spec] * count) + (VMEM_SPEC, late_spec),
         scratch_shapes=[pltpu.VMEM((zones,) + b.shape, BF) for b in blocks]
         + [pltpu.VMEM((b.shape[1], depth), BF) for b in blocks]
+        + ([pltpu.VMEM(near_shape, BF)] if direct else [])
         + [pltpu.VMEM((groups - 1, 8, length), F32)]
         + [pltpu.SemaphoreType.DMA((copies,)), pltpu.SemaphoreType.DMA((copies,)), pltpu.SemaphoreType.DMA((count,))],
         compiler_params=pltpu.CompilerParams(
-            vmem_limit_bytes=24 * 1024 * 1024, collective_id=1, has_side_effects=True
+            vmem_limit_bytes=61 * 1024 * 1024, collective_id=1, has_side_effects=True
         ),
         name="gather_weights",
     )(*blocks, late, route_rows)
 
 
-def reduce_copies(owners, zones):
-    return 1 + 2 * (owners // 2 - 1) + zones - 1
-
-
 def add_rows(into, other):
     return (into.astype(F32) + other.astype(F32)).astype(BF)
 
 
-def reduce_kernel(owners, zones, used_rows, *refs):
-    count = len(used_rows)
-    parts, small = refs[:count], refs[count]
-    outs, small_out = refs[count + 1:2 * count + 1], refs[2 * count + 1]
-    scratch = refs[2 * count + 2:]
-    keep, near, far = scratch[:count], scratch[count:2 * count], scratch[2 * count:3 * count]
-    slabs, incoming = scratch[3 * count:4 * count], scratch[4 * count:5 * count]
-    small_mine, small_other, send_sem, recv_sem, local_sem = scratch[5 * count:]
-    owner, zone = lax.axis_index("expert"), lax.axis_index("shard")
+class Mail:
+    def __init__(self, at, source, target, device, sems):
+        self.at, self.source, self.target, self.device, self.sems = at, source, target, device, sems
+
+    def make(self):
+        return pltpu.make_async_remote_copy(
+            self.source(), self.target(), self.sems[0].at[self.at], self.sems[1].at[self.at],
+            device_id=self.device, device_id_type=MESH,
+        )
+
+    def start(self):
+        self.make().start()
+        return self
+
+    def wait_recv(self):
+        self.make().wait_recv()
+
+    def wait_send(self):
+        self.make().wait_send()
+
+
+class Post:
+    def __init__(self, send_sem, recv_sem):
+        self.sems, self.mails = (send_sem, recv_sem), []
+
+    def plan(self, source, target, device):
+        mail = Mail(len(self.mails), source, target, device, self.sems)
+        self.mails.append(mail)
+        return mail
+
+    def close(self):
+        for mail in self.mails:
+            mail.wait_send()
+
+
+def cross_copies(owners):
+    return 1 + 2 * (owners // 2 - 1)
+
+
+def cross_scratch(owners, used, depth):
+    chips = owners // 2
+    return [
+        pltpu.VMEM((chips, used, depth), BF),
+        pltpu.VMEM((chips, used, depth), BF),
+        pltpu.VMEM((chips - 1, used, depth), BF),
+        pltpu.SemaphoreType.DMA,
+    ]
+
+
+def cross_plan(post, part, keep, near, far, local_sem, owner, zone, owners):
+    chips = owners // 2
     chip, core = owner // 2, owner % 2
-    greet(owner, zone, owners, zones)
-    send = sender(send_sem, recv_sem)
-    chips = owners // 2
+    used = keep.shape[1]
     orders = routes_of(chips)
     steps = len(orders[0])
-    sent = []
-    small_peers = [(flip(owner, bit), zone) for bit in bits_below(owners)]
-    small_peers += [(owner, flip(zone, bit)) for bit in bits_below(zones)]
-    small_mine[0] = small[...]
-
-    def small_start(i):
-        return send(small_mine.at[i], small_other.at[i], small_peers[i])
-
-    def small_finish(i, copy):
-        copy.wait_recv()
-        sent.append(copy)
-        small_mine[i + 1] = small_mine[i] + small_other[i]
-
-    def begin(g):
-        local = pltpu.make_async_copy(parts[g].at[:, core], keep[g], local_sem.at[g])
-        local.start()
-        return send(parts[g].at[:, 1 - core], near[g], (flip(owner, 1), zone)), local
-
-    def window(g, half):
-        start, size = halves_of(used_rows[g])[half]
+    first = post.plan(lambda: part.at[:, 1 - core], lambda: near, (flip(owner, 1), zone))
+
+    def window(half):
+        start, size = halves_of(used)[half]
         return pl.ds(start, size)
 
-    def push(g, step):
-        copies = []
+    def slot_of(step, i):
+        return chips - 2 * len(masks_of(orders[0][step + 1:])) + i
+
+    pushes = []
+    for step in range(steps):
+        mails = []
         for half, order in enumerate(orders):
             bit, rest = order[step], masks_of(order[step + 1:])
-            device = (flip(owner, 2 * bit), zone)
             for i, m in enumerate(rest):
-                slot = chips - 2 * len(rest) + i
-                copies.append(send(
-                    keep[g].at[flip(chip, bit | m), window(g, half), :], far[g].at[slot, window(g, half), :], device
+                index = flip(chip, bit | m)
+                mails.append(post.plan(
+                    lambda index=index, half=half: keep.at[index, window(half), :],
+                    lambda i=i, half=half, step=step: far.at[slot_of(step, i), window(half), :],
+                    (flip(owner, 2 * bit), zone),
                 ))
-        return copies
-
-    def absorb(g, step, copies):
-        for copy in copies:
-            copy.wait_recv()
-        sent.extend(copies)
+        pushes.append(mails)
+
+    def local():
+        return pltpu.make_async_copy(part.at[:, core], keep, local_sem)
+
+    def begin():
+        local().start()
+        first.start()
+
+    def meet():
+        local().wait()
+        first.wait_recv()
+
+        def one(h, _):
+            keep[h] = add_rows(keep[h], near[h])
+            return 0
+
+        lax.fori_loop(0, chips, one, 0)
+        for mail in pushes[0]:
+            mail.start()
+
+    def absorb(step):
+        for mail in pushes[step]:
+            mail.wait_recv()
         for half, order in enumerate(orders):
-            rest = masks_of(order[step + 1:])
-            for i, m in enumerate(rest):
-                slot = chips - 2 * len(rest) + i
+            for i, m in enumerate(masks_of(order[step + 1:])):
                 index = flip(chip, m)
-                keep[g][index, window(g, half), :] = add_rows(
-                    keep[g][index, window(g, half), :], far[g][slot, window(g, half), :]
+                keep[index, window(half), :] = add_rows(
+                    keep[index, window(half), :], far[slot_of(step, i), window(half), :]
                 )
-
-    def stage_near(g, state):
-        copy, local = state
-        local.wait()
-        copy.wait_recv()
-        sent.append(copy)
-
-        def one(h, _):
-            keep[g][h] = add_rows(keep[g][h], near[g][h])
-            return 0
-
-        lax.fori_loop(0, chips, one, 0)
-        return push(g, 0)
-
-    def stage_zone(g):
-        slab = slabs[g]
-        spare = slab.shape[2] - used_rows[g]
-        own = keep[g][chip]
+        if step + 1 < steps:
+            for mail in pushes[step + 1]:
+                mail.start()
+
+    stages = [meet] + [lambda step=step: absorb(step) for step in range(steps)]
+    return begin, stages
+
+
+def zone_scratch(zones, used, depth):
+    wide = -(-used // 128) * 128
+    return [pltpu.VMEM((zones, depth // zones, wide), BF), pltpu.VMEM((zones - 1, depth // zones, wide), BF)]
+
+
+def zone_shape(zones, used, depth):
+    return jax.ShapeDtypeStruct((depth // zones, -(-used // 128) * 128), F32)
+
+
+def zone_plan(post, slab, incoming, out_ref, owner, zone, zones):
+    mails = [
+        post.plan(
+            lambda d=d: slab.at[flip(zone, d)], lambda d=d: incoming.at[d - 1], (owner, flip(zone, d))
+        )
+        for d in range(1, zones)
+    ]
+
+    def start(own):
+        spare = slab.shape[2] - own.shape[0]
         if spare:
             own = jnp.concatenate([own, jnp.zeros((spare, own.shape[1]), BF)], axis=0)
         slab[...] = own.T.reshape(slab.shape)
-        return [
-            send(slab.at[flip(zone, d)], incoming[g].at[d - 1], (owner, flip(zone, d))) for d in range(1, zones)
+        for mail in mails:
+            mail.start()
+
+    def end():
+        total = slab[zone].astype(F32)
+        for d in range(1, zones):
+            mails[d - 1].wait_recv()
+            total = total + incoming[d - 1].astype(F32)
+        out_ref[...] = total
+
+    return start, end
+
+
+class Ride:
+    def __init__(self, parts, zoned, owns, rows, owners, zones, capacity, depth, collective_id):
+        groups = zones // 2
+        self.owners, self.zones, self.capacity, self.zoned, self.count = owners, zones, capacity, zoned, len(parts)
+        self.owns = len(owns)
+        self.with_rows = rows is not None
+        hbm = pl.BlockSpec(memory_space=pltpu.HBM)
+        self.args = [p.reshape(owners // 2, 2, p.shape[1], depth) for p in parts] + list(owns)
+        self.in_specs = [hbm] * len(parts) + [VMEM_SPEC] * len(owns)
+        self.out_shape = [zone_shape(zones, p.shape[1], depth) for p in parts[:zoned]]
+        self.out_shape += [jax.ShapeDtypeStruct(p.shape[1:], BF) for p in parts[zoned:]]
+        self.out_shape += [zone_shape(zones, o.shape[0], depth) for o in owns]
+        self.scratch_shapes = []
+        for p in parts:
+            self.scratch_shapes += cross_scratch(owners, p.shape[1], depth)
+        for p in parts[:zoned]:
+            self.scratch_shapes += zone_scratch(zones, p.shape[1], depth)
+        for o in owns:
+            self.scratch_shapes += zone_scratch(zones, o.shape[0], depth)
+        copies = len(parts) * cross_copies(owners) + (zoned + len(owns)) * (zones - 1)
+        if self.with_rows:
+            y, slot_rows = rows
+            length = slot_rows.shape[2]
+            self.args += [y, slot_rows]
+            self.in_specs += [hbm, VMEM_SPEC]
+            self.out_shape += [jax.ShapeDtypeStruct((groups - 1, length, depth), BF)]
+            self.scratch_shapes += [
+                pltpu.VMEM((groups - 1,) + y.shape[:2] + (capacity, depth), BF),
+                pltpu.SemaphoreType.DMA((groups - 1,)),
+                *[pltpu.VMEM((length, depth), BF)] * (groups - 2),
+            ]
+            copies += groups - 1
+        self.out_specs = [VMEM_SPEC] * len(self.out_shape)
+        self.scratch_shapes += [pltpu.SemaphoreType.DMA((copies,)), pltpu.SemaphoreType.DMA((copies,))]
+        self.inputs, self.outputs, self.scratch = len(self.args), len(self.out_shape), len(self.scratch_shapes)
+        self.params = pltpu.CompilerParams(
+            vmem_limit_bytes=61 * 1024 * 1024, collective_id=collective_id, has_side_effects=True
+        )
+
+    def board(self, inputs, outputs, scratch, room, spare):
+        owner, zone = lax.axis_index("expert"), lax.axis_index("shard")
+        owners, zones, count, groups = self.owners, self.zones, self.count, self.zones // 2
+        greet(owner, zone, owners, zones)
+        post = Post(scratch[-2], scratch[-1])
+        plans = [cross_plan(post, inputs[g], *scratch[4 * g:4 * g + 4], owner, zone, owners) for g in range(count)]
+        keeps = [scratch[4 * g] for g in range(count)]
+        for begin, _ in plans:
+            begin()
+        zone_plans = []
+        for g in range(self.zoned):
+            slab, incoming = scratch[4 * count + 2 * g:4 * count + 2 * g + 2]
+            zone_plans.append(zone_plan(post, slab, incoming, outputs[g], owner, zone, zones))
+        for i in range(self.owns):
+            at = 4 * count + 2 * (self.zoned + i)
+            start, end = zone_plan(post, scratch[at], scratch[at + 1], outputs[count + i], owner, zone, zones)
+            start(inputs[count + i][...])
+            zone_plans.append((start, end))
+        y_mails = []
+        if self.with_rows:
+            y_ref, slot_ref = inputs[count + self.owns:count + self.owns + 2]
+            at = 4 * count + 2 * (self.zoned + self.owns)
+            y_rows, y_sem = scratch[at:at + 2]
+            y_part = [spare, *scratch[at + 2:-2]]
+
+            def load(d):
+                window = pl.ds(d * self.capacity, self.capacity)
+                return pltpu.make_async_copy(y_ref.at[:, :, window, :], y_rows.at[d - 1], y_sem.at[d - 1])
+
+            for d in range(1, groups):
+                load(d).start()
+                y_mails.append(post.plan(
+                    lambda d=d: y_part[d - 1], lambda d=d: outputs[-1].at[d - 1], (owner, (zone + 2 * d) % zones)
+                ))
+
+        def rows_turn():
+            for d in range(1, groups):
+                load(d).wait()
+                collect_rows(y_rows.at[d - 1], slot_ref[d], room)
+                y_part[d - 1][...] = room[...].astype(BF)
+                y_mails[d - 1].start()
+
+        turns = []
+        for g in range(count):
+            turns.append(lambda g=g: self.run([plans[g - 1][1][1]] if g else [], [plans[g][1][0]]))
+        if count == 1:
+            turns.append(lambda: self.run([plans[0][1][1]]))
+        longest = len(plans[0][1]) if plans else 0
+
+        def finish_part():
+            for t in range(1, count + longest - 1):
+                for g in reversed(range(count)):
+                    at = t - g
+                    if 1 <= at < longest and (at > 1 or (g == count - 1 and count > 1)):
+                        plans[g][1][at]()
+                        if at == longest - 1 and g < self.zoned:
+                            zone_plans[g][0](keeps[g][owner // 2])
+            for g in range(self.zoned, count):
+                outputs[g][...] = keeps[g][owner // 2]
+            for _, end in zone_plans:
+                end()
+            for mail in y_mails:
+                mail.wait_recv()
+            post.close()
+
+        return turns, rows_turn if self.with_rows else None, finish_part
+
+    def run(self, *groups):
+        for acts in groups:
+            for act in acts:
+                act()
+
+
+def collect_rows(rows_ref, slots, room):
+    owners, local, capacity, width = rows_ref.shape
+    span = 2 * local * capacity
+    for h in range(owners // 2):
+        hits = slot_hits(slots, jnp.int32(h * span), span)
+        added = tn(hits[0] + hits[1], rows_ref[2 * h:2 * h + 2].reshape(span, width))
+        if h == 0:
+            room[...] = added
+        else:
+            room[...] += added
+
+
+def finish_kernel(owners, zones, capacity, sizes, *refs):
+    refs = list(refs)
+
+    def take(count):
+        found = refs[:count]
+        del refs[:count]
+        return found
+
+    with_rows, chunks = sizes
+    early_refs, (down_part, part, small) = take(2), take(3)
+    own_refs, peer_refs = take(2), take(2)
+    y_ref, slot_ref, x_ref, y_in = take(4) if with_rows else (None, None, None, None)
+    *outs, small_out = take(5)
+    sum_refs = take(2)
+    y_out = take(1)[0] if with_rows else None
+    cross_refs = [take(4) for _ in range(2)]
+    zone_refs = [take(2) for _ in range(4)]
+    small_mine, small_other = take(2)
+    stages = [take(3) for _ in range(2)]
+    add_sem = take(1)[0]
+    if with_rows:
+        y_rows, y_sum, y_sem = take(3)
+    send_sem, recv_sem = take(2)
+    owner, zone = lax.axis_index("expert"), lax.axis_index("shard")
+    greet(owner, zone, owners, zones)
+    post = Post(send_sem, recv_sem)
+    plans = [
+        cross_plan(post, p, *r, owner, zone, owners) for p, r in zip((down_part, part), cross_refs)
+    ]
+    for begin, _ in plans:
+        begin()
+    down, cross = [stages for _, stages in plans]
+    if with_rows:
+        y_copy = pltpu.make_async_copy(y_ref.at[:, :, pl.ds(0, capacity), :], y_rows, y_sem)
+        y_copy.start()
+    zone_starts, zone_ends = zip(
+        *[zone_plan(post, r[0], r[1], out, owner, zone, zones) for r, out in zip(zone_refs, outs)]
+    )
+    for start, ref in zip(zone_starts, early_refs):
+        start(ref[...])
+    small_peers = [(flip(owner, bit), zone) for bit in bits_below(owners)]
+    small_peers += [(owner, flip(zone, bit)) for bit in bits_below(zones)]
+    small_mails = [
+        post.plan(lambda i=i: small_mine.at[i], lambda i=i: small_other.at[i], peer)
+        for i, peer in enumerate(small_peers)
+    ]
+    small_mine[0] = small[...]
+    small_mails[0].start()
+
+    def small_step(i):
+        if i < len(small_mails):
+            small_mails[i].wait_recv()
+            small_mine[i + 1] = small_mine[i] + small_other[i]
+            if i + 1 < len(small_mails):
+                small_mails[i + 1].start()
+
+    groups = zones // 2
+
+    def add_stage(i):
+        mine, theirs, total = stages[i]
+        count = chunks[i]
+        size = mine.shape[1]
+
+        def loads(k):
+            rows = pl.ds(k * size, size)
+            return (
+                pltpu.make_async_copy(own_refs[i].at[rows, :], mine.at[k % 2], add_sem.at[i, k % 2, 0]),
+                pltpu.make_async_copy(peer_refs[i].at[rows, :], theirs.at[k % 2], add_sem.at[i, k % 2, 1]),
+            )
+
+        def store(k):
+            return pltpu.make_async_copy(
+                total.at[k % 2], sum_refs[i].at[pl.ds(k * size, size), :], add_sem.at[i, k % 2, 2]
+            )
+
+        for copy in loads(0):
+            copy.start()
+        for k in range(count):
+            if k + 1 < count:
+                for copy in loads(k + 1):
+                    copy.start()
+            for copy in loads(k):
+                copy.wait()
+            if k >= 2:
+                store(k - 2).wait()
+            total[k % 2] = mine[k % 2] + theirs[k % 2].astype(F32)
+            store(k).start()
+        for k in range(max(0, count - 2), count):
+            store(k).wait()
+
+    down[0]()
+    small_step(0)
+    add_stage(0)
+    down[1]()
+    cross[0]()
+    small_step(1)
+    if with_rows:
+        y_copy.wait()
+        collect_rows(y_rows, slot_ref[0], y_sum)
+        total = x_ref[...] + y_sum[...]
+        for d in range(1, groups):
+            total = total + y_in[d - 1].astype(F32)
+        y_out[...] = total.astype(BF)
+    small_step(2)
+    for act in down[2:]:
+        act()
+    zone_starts[2](cross_refs[0][0][owner // 2])
+    for act in cross[1:-1]:
+        act()
+    zone_ends[0]()
+    zone_ends[1]()
+    small_step(3)
+    cross[-1]()
+    zone_starts[3](cross_refs[1][0][owner // 2])
+    small_step(4)
+    add_stage(1)
+    for i in range(5, len(small_mails)):
+        small_step(i)
+    small_out[...] = small_mine[len(small_mails)]
+    zone_ends[2]()
+    zone_ends[3]()
+    post.close()
+
+
+def finish(early, down_part, first_part, small, owns, peers, owners, zones, capacity, rows=None):
+    depth = first_part.shape[2]
+    chips = owners // 2
+    used = tuple(o.shape[0] for o in early) + (down_part.shape[1], first_part.shape[1])
+    cross_parts = [p.reshape(chips, 2, p.shape[1], depth) for p in (down_part, first_part)]
+    flat = [o.reshape(-1, o.shape[-1]) for o in owns]
+    flat_peers = [p.reshape(-1, p.shape[-1]) for p in peers]
+    chunk = 256
+    chunks = tuple(f.shape[0] // chunk for f in flat)
+    rounds = len(bits_below(owners)) + len(bits_below(zones))
+    copies = 2 * cross_copies(owners) + 4 * (zones - 1) + rounds
+    hbm = pl.BlockSpec(memory_space=pltpu.HBM)
+    args = [*early, *cross_parts, small, *flat, *flat_peers]
+    in_specs = [VMEM_SPEC, VMEM_SPEC, hbm, hbm, VMEM_SPEC] + [hbm] * 4
+    out_shape = [zone_shape(zones, u, depth) for u in used] + [jax.ShapeDtypeStruct(small.shape, F32)]
+    out_shape += [jax.ShapeDtypeStruct(f.shape, F32) for f in flat]
+    out_specs = [VMEM_SPEC] * 5 + [hbm] * 2
+    scratch = cross_scratch(owners, used[2], depth) + cross_scratch(owners, used[3], depth)
+    for u in used:
+        scratch += zone_scratch(zones, u, depth)
+    scratch += [pltpu.VMEM((rounds + 1,) + small.shape, F32), pltpu.VMEM((rounds,) + small.shape, F32)]
+    for f in flat:
+        shape = (2, chunk, f.shape[1])
+        scratch += [pltpu.VMEM(shape, F32), pltpu.VMEM(shape, BF), pltpu.VMEM(shape, F32)]
+    scratch += [pltpu.SemaphoreType.DMA((2, 2, 3))]
+    if rows is not None:
+        y, slot_rows, x, y_near = rows
+        args += [y, slot_rows, x, y_near]
+        in_specs += [hbm, VMEM_SPEC, VMEM_SPEC, VMEM_SPEC]
+        out_shape += [jax.ShapeDtypeStruct(x.shape, BF)]
+        out_specs += [VMEM_SPEC]
+        scratch += [
+            pltpu.VMEM(y.shape[:2] + (capacity, depth), BF), pltpu.VMEM(x.shape, F32), pltpu.SemaphoreType.DMA,
         ]
-
-    def stage_end(g, copies):
-        total = slabs[g][zone].astype(F32)
-        for d in range(1, zones):
-            copies[d - 1].wait_recv()
-            total = total + incoming[g][d - 1].astype(F32)
-        sent.extend(copies)
-        outs[g][...] = total
-
-    begun = [begin(g) for g in range(count)]
-    small_copy = small_start(0)
-    state = {}
-    stages = steps + 2
-    turn = 0
-    for t in range(count + stages - 1):
-        for g in reversed(range(count)):
-            at = t - g
-            if at == 0:
-                state[g] = stage_near(g, begun[g])
-            elif 1 <= at <= steps:
-                absorb(g, at - 1, state[g])
-                state[g] = push(g, at) if at < steps else stage_zone(g)
-            elif at == steps + 1:
-                stage_end(g, state[g])
-        if turn < len(small_peers):
-            small_finish(turn, small_copy)
-            turn += 1
-            if turn < len(small_peers):
-                small_copy = small_start(turn)
-    while turn < len(small_peers):
-        small_finish(turn, small_copy)
-        turn += 1
-        if turn < len(small_peers):
-            small_copy = small_start(turn)
-    small_out[...] = small_mine[len(small_peers)]
-    for copy in sent:
-        copy.wait_send()
-
-
-def reduce_grads(parts, small, owners, zones):
-    count = len(parts)
-    used_rows = tuple(p.shape[1] for p in parts)
-    depth = parts[0].shape[2]
-    chips = owners // 2
-    parts = [p.reshape(chips, 2, p.shape[1], depth) for p in parts]
-    wide = [-(-used // 128) * 128 for used in used_rows]
-    rounds = len(bits_below(owners)) + len(bits_below(zones))
-    copies = count * reduce_copies(owners, zones) + rounds
+    scratch += [pltpu.SemaphoreType.DMA((copies,)), pltpu.SemaphoreType.DMA((copies,))]
+    sizes = (rows is not None, chunks)
     return pl.pallas_call(
-        lambda *refs: reduce_kernel(owners, zones, used_rows, *refs),
-        out_shape=tuple(jax.ShapeDtypeStruct((depth // zones, w), F32) for w in wide)
-        + (jax.ShapeDtypeStruct(small.shape, F32),),
-        in_specs=[pl.BlockSpec(memory_space=pltpu.HBM)] * count + [VMEM_SPEC],
-        out_specs=tuple([VMEM_SPEC] * (count + 1)),
-        scratch_shapes=[pltpu.VMEM((chips, used, depth), BF) for used in used_rows]
-        + [pltpu.VMEM((chips, used, depth), BF) for used in used_rows]
-        + [pltpu.VMEM((chips - 1, used, depth), BF) for used in used_rows]
-        + [pltpu.VMEM((zones, depth // zones, w), BF) for w in wide]
-        + [pltpu.VMEM((zones - 1, depth // zones, w), BF) for w in wide]
-        + [pltpu.VMEM((rounds + 1,) + small.shape, F32), pltpu.VMEM((rounds,) + small.shape, F32)]
-        + [pltpu.SemaphoreType.DMA((copies,)), pltpu.SemaphoreType.DMA((copies,)), pltpu.SemaphoreType.DMA((count,))],
+        lambda *refs: finish_kernel(owners, zones, capacity, sizes, *refs),
+        out_shape=tuple(out_shape),
+        in_specs=in_specs,
+        out_specs=tuple(out_specs),
+        scratch_shapes=scratch,
         compiler_params=pltpu.CompilerParams(
-            vmem_limit_bytes=VMEM_BYTES, collective_id=2, has_side_effects=True
+            vmem_limit_bytes=61 * 1024 * 1024, collective_id=2, has_side_effects=True
         ),
-        name="reduce_grads",
-    )(*parts, small)
+        name="finish",
+    )(*args)
 
 
 def three_pieces(row):
@@ -956,7 +1343,7 @@
             pltpu.SemaphoreType.DMA((2 * groups * local,)),
         ],
         compiler_params=pltpu.CompilerParams(
-            vmem_limit_bytes=40 * 1024 * 1024, collective_id=3, has_side_effects=True
+            vmem_limit_bytes=61 * 1024 * 1024, collective_id=3, has_side_effects=True
         ),
         name="send_rows",
     )(x, gain, router, route_rows, slot_rows, slices)
@@ -1126,7 +1513,7 @@
             pltpu.SemaphoreType.DMA((2 * groups * local,)),
         ],
         compiler_params=pltpu.CompilerParams(
-            vmem_limit_bytes=40 * 1024 * 1024, collective_id=4, has_side_effects=True
+            vmem_limit_bytes=61 * 1024 * 1024, collective_id=4, has_side_effects=True
         ),
         name="return_rows",
     )(rows, dgate, slot_rows, gates, route_rows, x, gain, router, normed, top)
@@ -1253,28 +1640,28 @@
     )(slot_rows, rows)
 
 
-def collect_kernel(slot_ref, rows_ref, out_ref):
+def collect_kernel(first, slot_ref, rows_ref, out_ref):
     experts, zones, capacity, width = rows_ref.shape
     length = out_ref.shape[1]
     take = max(1, 384 // capacity)
     out_ref[...] = jnp.zeros_like(out_ref)
 
     def chunk(i, _):
-        for zone in range(zones):
+        for zone in range(first, zones):
             hits = slot_hits(slot_ref[zone], i * (take * capacity), take * capacity)
             rows = rows_ref[pl.ds(i * take, take), zone].reshape(take * capacity, width)
-            out_ref[zone] += tn(hits[0] + hits[1], rows)
+            out_ref[zone - first] += tn(hits[0] + hits[1], rows)
         return 0
 
     lax.fori_loop(0, experts // take, chunk, 0)
 
 
-def collect(slot_rows, rows):
+def collect(slot_rows, rows, first=0):
     experts, zones, capacity, width = rows.shape
     length = slot_rows.shape[2]
     return pl.pallas_call(
-        collect_kernel,
-        out_shape=jax.ShapeDtypeStruct((zones, length, width), F32),
+        lambda *refs: collect_kernel(first, *refs),
+        out_shape=jax.ShapeDtypeStruct((zones - first, length, width), F32),
         in_specs=[VMEM_SPEC] * 2,
         out_specs=VMEM_SPEC,
         compiler_params=pltpu.CompilerParams(vmem_limit_bytes=VMEM_BYTES),
@@ -1332,6 +1719,7 @@
     qkv_cols, out_cols = qkv_weight.shape[2], out_weight.shape[2]
     zones_all = 2 * zones
     router_pad = 16
+    direct = capacity % 16 == 0
     parts = mlp_down.shape[0] // qkv_weight.shape[1]
     aligned = qkv_cols % 16 == 0 and out_cols % 16 == 0 and qkv_cols % out_cols == 0
 
@@ -1341,7 +1729,7 @@
     down_block = mlp_down.reshape(parts, -1, mlp_down.shape[1]).transpose(1, 0, 2).reshape(qkv_weight.shape[1], -1)
     router_block = jnp.pad(router, ((0, 0), (0, router_pad - router.shape[1])))
     route_rows = routes.T
-    first, up_full, down_full, last, cotangent_near, slot_rows = gather_weights(
+    first, up_full, down_full, last, slot_rows, cotangent_rows = gather_weights(
         [
             padded(jnp.concatenate([qkv_weight[0], out_weight[0]], axis=1)),
             padded(mlp_up),
@@ -1366,17 +1754,20 @@
     first, up_late = lax.optimization_barrier((first, expert_up))
     weights0, weights1 = layer_weights(first), layer_weights(last)
     up_other = swap_pair(up_late)
-    direct = capacity % 16 == 0
 
     def dispatch(rows):
         packed = spread(slot_rows, rows, experts_all, capacity)
         return exchange(packed.reshape(owners, local, zones * capacity, width))
 
+    if direct:
+        cotangent_rows = exchange(cotangent_rows.reshape(owners, local, zones * capacity, width))
+    else:
+        cotangent_rows = dispatch(jnp.concatenate([cotangent[None], cotangent_rows]))
+
     def undo(rows):
         back = exchange(rows).reshape(experts_all, zones, capacity, width)
         return collect(slot_rows, back)
 
-    cotangent_rows = dispatch(jnp.concatenate([cotangent[None], cotangent_near]))
 
     onehot = bucket_onehot(length, bias_tables.shape[2])
     vectors = lax.dot_general(
@@ -1411,8 +1802,6 @@
     y_rows, dx_rows, dgate_rows, own_up, own_down, peer_up, peer_down = run_experts(
         eh_rows, cotangent_rows, gate_rows, expert_up, expert_down, up_other, down_other
     )
-    peer_up, peer_down = swap_pair(peer_up), swap_pair(peer_down)
-
     if direct:
         dx3, dgain3, grad_router = return_rows(
             dx_rows, dgate_rows, slot_rows, gates, route_rows, x3, gains[3], router_full, eh, cotangent,
@@ -1449,39 +1838,52 @@
             grads = [jnp.concatenate(pieces, axis=1)]
         return results[0], grads[0], results[-2], results[-1]
 
+    dx3, y_rows = lax.optimization_barrier((dx3, y_rows))
+    y_back = exchange(y_rows)
     dx2, last_part, dvec1, dgain2 = layer_grads(
         attend_back(
-            piece_start, x2, gains[2], weights1, vectors[1], ah1, qkv1, o1, lse1, dx3, router_rows if aligned else None
+            piece_start, x2, gains[2], weights1, vectors[1], ah1, qkv1, o1, lse1, dx3, router_rows if aligned else None,
         ),
         router_rows,
     )
-    dx2, y_rows = lax.optimization_barrier((dx2, y_rows))
-    y_back = undo(y_rows)
-    final = x3 + y_back[0]
-    for d in range(1, zones):
-        final = final + shift_to(y_back[d].astype(BF), 2 * d).astype(F32)
-    output = final.astype(BF)
-    dx1, up_part, down_part, dgain1 = mlp_back(x1, gains[1], up_full, down_full, mh, dx2, parts, zones_all)
-    dx0, first_part, dvec0, dgain0 = layer_grads(
-        attend_back(piece_start, x0, gains[0], weights0, vectors[0], ah0, qkv0, o0, lse0, dx1)
+    peer_up = swap_pair(peer_up)
+    dx2, peer_down = lax.optimization_barrier((dx2, peer_down))
+    peer_down = swap_pair(peer_down)
+    dx1, up_part, down_part, dgain1 = mlp_back(
+        x1, gains[1], up_full, down_full, mh, dx2, parts, zones_all
     )
-    dx0, output, peer_up, peer_down = lax.optimization_barrier((dx0, output, peer_up, peer_down))
-    grad_up = own_up + peer_up.astype(F32)
-    grad_down = own_down + peer_down.astype(F32)
     if mlp_down.shape[1] % 16:
         down_part = down_part.reshape(parts, owners, -1, width).transpose(1, 0, 2, 3)
+    dx1, y_back, peer_up = lax.optimization_barrier((dx1, y_back, peer_up))
+    ride = Ride(
+        [last_part, up_part.reshape(owners, -1, width)], 0, [], (y_back, slot_rows) if direct else None,
+        owners, zones_all, capacity, width, 6,
+    )
+    last_own, up_own, *results = attend_back(
+        piece_start, x0, gains[0], weights0, vectors[0], ah0, qkv0, o0, lse0, dx1, None, ride
+    )
+    y_near = results.pop(0) if direct else None
+    dx0, first_part, dvec0, dgain0 = layer_grads(results)
+    dx0, peer_down = lax.optimization_barrier((dx0, peer_down))
     dtables = lax.dot_general(
         jnp.stack([dvec0, dvec1]), onehot, (((2,), (0,)), ((), ())), precision=lax.Precision.HIGHEST
     )
     dgains = jnp.concatenate([dgain0, dgain1, dgain2, dgain3])
     small = jnp.concatenate([dgains.reshape(-1), dtables.reshape(-1)])
     small = jnp.pad(small, (0, -small.size % 1024)).reshape(-1, 128)
-    last_grad, up_grad, down_grad, first_grad, small = reduce_grads(
-        [
-            last_part, up_part.reshape(owners, -1, width), down_part.reshape(owners, -1, width), first_part
-        ],
-        small, owners, zones_all,
+    last_grad, up_grad, down_grad, first_grad, small, grad_up, grad_down, *finals = finish(
+        (last_own, up_own), down_part.reshape(owners, -1, width), first_part, small, (own_up, own_down), (peer_up, peer_down), owners, zones_all, capacity,
+        (y_back, slot_rows, x3, y_near) if direct else None,
     )
+    grad_up, grad_down = grad_up.reshape(own_up.shape), grad_down.reshape(own_down.shape)
+    if direct:
+        output = finals[0]
+    else:
+        y_zones = collect(slot_rows, y_back.reshape(experts_all, zones, capacity, width))
+        output = x3 + y_zones[0]
+        for d in range(1, zones):
+            output = output + shift_to(y_zones[d].astype(BF), 2 * d).astype(F32)
+        output = output.astype(BF)
     small = small.reshape(-1)
     grad_qkv = jnp.stack([first_grad[:, :qkv_cols], last_grad[:, :qkv_cols]])
     grad_out = jnp.stack(

time: 657 us -> 630 us (0.959)
  local copies, waits for them, and re-layouts: 40.9 us -> 27.8 us
  other arithmetic: 16.8 us -> 5.06 us
    pallas_call x5 -> x3, Pallas kernels: 192 us -> 178 us  [the longest x2 99.7 us: attend_back(): pl.pallas_call(lambda *refs: attend_back_kernel(bool(tails), weights, rid...]
    unnamed x62 -> x42, local copies, waits for them, and re-layouts: 24.6 us -> 12 us
    add x1 -> x0, other arithmetic: 9.81 us -> none  [per_device(): grad_down = own_down + peer_down.astype(F32)]
  transfers between devices with their start and end apart: 6 -> 5, of which waited for: 0 -> 0; matrix products, arithmetic and copies ran while one was open for 3% -> 1% of each run, Pallas kernels for 34% -> 27%
where the time goes in v4:
time: 630 us; the launch traced here: 621 us
  Pallas kernels  565 us (90%)
  local copies, waits for them, and re-layouts  27.8 us (4%)
  starting transfers between devices  19.6 us (3%)
    pallas_call x1, Pallas kernels, gather_weights(): pl.pallas_call(lambda *refs: gather_kernel(owners, zones, used_rows, expe...  106 us
    pallas_call x2, Pallas kernels, attend_back(): pl.pallas_call(lambda *refs: attend_back_kernel(bool(tails), weights, rid...  99.7 us
    pallas_call x1, Pallas kernels, finish(): pl.pallas_call(lambda *refs: finish_kernel(owners, zones, capacity, sizes...  78.6 us
    pallas_call x1, Pallas kernels, send_rows(): pl.pallas_call(lambda *refs: send_rows_kernel(owners, zones, capacity, *r...  77.2 us
    pallas_call x1, Pallas kernels, run_experts(): pl.pallas_call(experts_kernel, grid=(local,), out_shape=(jax.ShapeDtypeSt...  69 us
    pallas_call x1, Pallas kernels, return_rows(): pl.pallas_call(lambda *refs: return_rows_kernel(owners, zones, capacity,...  64.2 us
    pallas_call x2, Pallas kernels, attend(): pl.pallas_call(lambda *refs: attend_kernel(weights, *refs), out_shape=(ja...  37.5 us
    pallas_call x1, Pallas kernels, mlp_back(): pl.pallas_call(lambda *refs: mlp_back_kernel(parts, zones, *refs), out_sh...  21.8 us
  transfers between devices with their start and end apart: 5, of which 0 were waited for; matrix products, arithmetic and copies ran while one was open for 1% of the time, Pallas kernels for 27%

profile of v4, /device:TPU:0, one launch (start us, length us, event | category | flops | bytes accessed | tf_op | source)
XLA Modules:
  0.0 621.0 jit_solution(9194396168831963074)
XLA Ops:
  2.3 1.1 reshape.111
  7.1 106.2 %gather_weights.1 = (bf16[8,384,768]{2,1,0:T(8,128)(2,1)}, bf16[8,384,768]{2,1,0:T(8,128)(2,1)}, bf16[8,384,768]{2,1,0:T(8,128)(2,1)}, bf16[8,400,768]{2,1,0:T(8...) custom-call(bf16[192,384]{1,0:T(8,128)(2,1)} %pad_maximum_fusion.2.refs_0_, bf16[192,384]{1,0:T(8,128)(2,1)} %refs_1_.1, ...), custom_call_target="tpu_custom_call" | custom-call | tf_op jit(solution)/shard_map/gather_weights/pallas_call | solution.py:711
  113.3 5.5 all-to-all-start
  118.8 7.0 %collective-permute-start = (bf16[2,768,768]{2,1,0:T(8,128)(2,1)S(1)}, bf16[2,768,768]{2,1,0:T(8,128)(2,1)}, u32[]{:S(2)}, u32[]{:S(2)}) collective-permute-start(bf16[2,768,768]{2,1,0:T(8,128)(2,1)S(1)} %copy-done.13), channel_id=1, source_target_pairs={{0,1},{1,0},{2,3},{3,2},{4,5},{5,4},{6,7},{7,6},{8,9},{9,8},{10,11... | collective-permute-start | bytes 7077896 | tf_op jit(solution)/shard_map/ppermute | solution.py:1702
  126.5 1.3 convert_element_type.19.refs_1_
  130.9 18.8 %attend.2 = (f32[512,768]{1,0:T(8,128)}, bf16[512,768]{1,0:T(8,128)(2,1)}, bf16[512,2304]{1,0:T(8,128)(2,1)}, bf16[512,768]{1,0:T(8,128)(2,1)}, f32[12,512]{1,0:T(8,128)}) custom-call(s32[1]{0:T(128)S(6)} %copy.49.refs_0_, f32[512,768]{1,0:T(8,128)} %convert_element_type.19.refs_1_, f32[1,768]{1,0:T(1,128)} %get-tuple-element.192.refs_2_, ...), custom_call_target="tpu_custom_call" | custom-call | flops 3221225472 | bytes 12582912 | tf_op jit(solution)/shard_map/attend/pallas_call | solution.py:180
  149.7 10.8 %mlp.1 = (f32[512,768]{1,0:T(8,128)}, bf16[512,768]{1,0:T(8,128)(2,1)}) custom-call(f32[512,768]{1,0:T(8,128)} %get-tuple-element.87.refs_0_, f32[1,768]{1,0:T(1,128)} %get-tuple-element.191.refs_1_, bf16[3072,768]{1,0:T(8,128)(2,1)} %bitcast.68, bf16[8,384,768]{2,1,0:T(8,128)(2,1)} %get-tuple-element.89.refs_3_), custom_call_target="tpu_custom_call" | custom-call | flops 4831838208 | bytes 13369344 | tf_op jit(solution)/shard_map/mlp/pallas_call | solution.py:449
  160.5 18.7 %attend.3 = (f32[512,768]{1,0:T(8,128)}, bf16[512,768]{1,0:T(8,128)(2,1)}, bf16[512,2304]{1,0:T(8,128)(2,1)}, bf16[512,768]{1,0:T(8,128)(2,1)}, f32[12,512]{1,0:T(8,128)}) custom-call(s32[1]{0:T(128)S(6)} %copy.49.refs_0_, f32[512,768]{1,0:T(8,128)} %get-tuple-element.91.refs_1_, f32[1,768]{1,0:T(1,128)} %get-tuple-element.193.refs_2_, ...), custom_call_target="tpu_custom_call" | custom-call | flops 3221225472 | bytes 12582912 | tf_op jit(solution)/shard_map/attend/pallas_call | solution.py:180
  179.3 77.2 %send_rows.1 = (bf16[512,768]{1,0:T(8,128)(2,1)}, f32[8,512]{1,0:T(8,128)}, bf16[8,2,192,768]{3,2,1,0:T(8,128)(2,1)}, f32[8,2,192,1]{3,2,1,0:T(8,128)}, bf16[2,768,768]{2,1,0:T(8,128)(2,1)}) custom-call(f32[512,768]{1,0:T(8,128)} %get-tuple-element.100.refs_0_.refs_5_.refs_11_, f32[1,768]{1,0:T(1,128)} %get-tuple-element.190.refs_1_.refs_6_, ...), custom_call_target="tpu_custom_call" | custom-call | tf_op jit(solution)/shard_map/send_rows/pallas_call | solution.py:1324
  256.5 69.0 %experts.1 = (bf16[8,2,192,768]{3,2,1,0:T(8,128)(2,1)}, bf16[8,2,192,768]{3,2,1,0:T(8,128)(2,1)}, f32[8,2,192,1]{3,2,1,0:T(8,128)}, f32[2,768,768]{2,1,0:T(8,128...) custom-call(bf16[8,2,192,768]{3,2,1,0:T(8,128)(2,1)} %get-tuple-element.102.x_ref, ...), custom_call_target="tpu_custom_call" | custom-call | flops 43486543872 | bytes 37748736 | tf_op jit(solution)/shard_map/experts/pallas_call | solution.py:1586
  325.5 64.2 %return_rows.1 = (f32[512,768]{1,0:T(8,128)}, f32[1,768]{1,0:T(1,128)}, f32[16,768]{1,0:T(8,128)}) custom-call(bf16[8,2,192,768]{3,2,1,0:T(8,128)(2,1)} %get-tuple-element.107.refs_0_, f32[8,2,192,1]{3,2,1,0:T(8,128)} %get-tuple-element.108.refs_1_, f32[2,8,512]{2,1,0:T(8,128)} %get-tuple-element.101.refs_4_.refs_2_.refs_13_.refs_10_, ...), custom_call_target="tpu_custom_call" | custom-call | tf_op jit(solution)/shard_map/return_rows/pallas_call | solution.py:1493
  389.7 4.9 all-to-all-start.1
  394.7 1.2 collective-permute-start.1
  396.6 35.8 %attend_back.2 = (f32[512,768]{1,0:T(8,128)}, bf16[8,400,768]{2,1,0:T(8,128)(2,1)}, f32[12,1024]{1,0:T(8,128)}, f32[1,768]{1,0:T(1,128)}) custom-call(s32[1]{0:T(128)S(6)} %copy.49.refs_0_, f32[512,768]{1,0:T(8,128)} %get-tuple-element.91.refs_1_, f32[1,768]{1,0:T(1,128)} %get-tuple-element.193.refs_2_, bf16[8,400,768]{2,1,0:T(8,128)(2,1)} %get-tuple-element.92.refs_3_, ...), custom_call_target="tpu_custom_call" | custom-call | flops 6845104128 | bytes 25165824 | tf_op jit(solution)/shard_map/attend_back/pallas_call | solution.py:361
  433.4 21.8 %mlp_back.1 = (f32[512,768]{1,0:T(8,128)}, bf16[3072,768]{1,0:T(8,128)(2,1)}, bf16[8,384,768]{2,1,0:T(8,128)(2,1)}, f32[1,768]{1,0:T(1,128)}) custom-call(f32[512,768]{1,0:T(8,128)} %get-tuple-element.87.refs_0_, f32[1,768]{1,0:T(1,128)} %get-tuple-element.191.refs_1_, bf16[3072,768]{1,0:T(8,128)(2,1)} %bitcast.69, ...), custom_call_target="tpu_custom_call" | custom-call | flops 12079595520 | bytes 25165824 | tf_op jit(solution)/shard_map/mlp_back/pallas_call | solution.py:497
  455.3 63.9 %attend_back.3 = (bf16[400,768]{1,0:T(8,128)(2,1)}, bf16[384,768]{1,0:T(8,128)(2,1)}, bf16[1,512,768]{2,1,0:T(8,128)(2,1)}, f32[512,768]{1,0:T(8,128)}, bf16[8,3...) custom-call(s32[1]{0:T(128)S(6)} %copy.49.refs_0_, f32[512,768]{1,0:T(8,128)} %convert_element_type.19.refs_1_, ...), custom_call_target="tpu_custom_call" | custom-call | flops 6845104128 | bytes 25165824 | tf_op jit(solution)/shard_map/attend_back/pallas_call | solution.py:361
  519.2 1.1 fusion.4
  521.7 78.6 %finish.1 = (f32[192,512]{1,0:T(8,128)}, f32[192,384]{1,0:T(8,128)}, f32[192,384]{1,0:T(8,128)}, f32[192,384]{1,0:T(8,128)}, f32[40,128]{1,0:T(8,128)}, /*index=...) custom-call(bf16[400,768]{1,0:T(8,128)(2,1)} %get-tuple-element.125.refs_0_, ...), custom_call_target="tpu_custom_call" | custom-call | tf_op jit(solution)/shard_map/finish/pallas_call | solution.py:1169
  602.3 1.1 slice_bitcast_fusion
  606.7 1.2 reshape.130
  610.7 2.2 copy.50
  613.0 1.1 copy.51
  614.8 2.4 copy.53
  618.4 2.2 copy.54
  (78 shorter events, 21.5 us)
Async XLA Ops:
  0.6 129.4 %copy-start = (f32[2,12,44]{2,0,1:T(2,128)S(1)}, f32[2,12,44]{2,0,1:T(2,128)}, u32[]{:S(2)}) copy-start(f32[2,12,44]{2,0,1:T(2,128)} %param.18) | copy-start | bytes 12676
  113.3 5.5 copy-start.13
  113.3 13.2 %copy-start.5 = (bf16[512,768]{1,0:T(8,128)(2,1)S(1)}, bf16[512,768]{1,0:T(8,128)(2,1)}, u32[]{:S(2)}) copy-start(bf16[512,768]{1,0:T(8,128)(2,1)} %param.14) | copy-start | bytes 2359300
  113.3 66.0 %all-to-all-start = ((bf16[8,2,192,768]{3,2,1,0:T(8,128)(2,1)}), bf16[8,2,192,768]{3,2,1,0:T(8,128)(2,1)}, u32[]{:S(2)}, u32[]{:S(2)}) async-start(bf16[8,2,192,768]{3,2,1,0:T(8,128)(2,1)} %bitcast.55), calls=%async_computation | async-start | bytes 9437184 | tf_op jit(solution)/shard_map/all_to_all | solution.py:1706
  118.8 10.5 %copy-start.12 = (s32[21]{0:T(128)S(1)}, s32[21]{0:T(128)}, u32[]{:S(2)}) copy-start(s32[21]{0:T(128)} %constant.16.clone) | copy-start | bytes 256
  118.8 10.6 %copy-start.8 = (f32[4,768]{1,0:T(4,128)S(1)}, f32[4,768]{1,0:T(4,128)}, u32[]{:S(2)}) copy-start(f32[4,768]{1,0:T(4,128)} %param.17) | copy-start | bytes 36868
  118.8 60.5 %collective-permute-start = (bf16[2,768,768]{2,1,0:T(8,128)(2,1)S(1)}, bf16[2,768,768]{2,1,0:T(8,128)(2,1)}, u32[]{:S(2)}, u32[]{:S(2)}) collective-permute-start(bf16[2,768,768]{2,1,0:T(8,128)(2,1)S(1)} %copy-done.13), channel_id=1, source_target_pairs={{0,1},{1,0},{2,3},{3,2},{4,5},{5,4},{6,7},{7,6},{8,9},{9,8},{10,11... | collective-permute-start | bytes 7077896 | tf_op jit(solution)/shard_map/ppermute | solution.py:1702
  389.7 6.1 copy-start.7
  389.7 65.5 %all-to-all-start.1 = ((bf16[8,2,192,768]{3,2,1,0:T(8,128)(2,1)}), bf16[8,2,192,768]{3,2,1,0:T(8,128)(2,1)}, u32[]{:S(2)}, u32[]{:S(2)}) async-start(bf16[8,2,192,768]{3,2,1,0:T(8,128)(2,1)} %get-tuple-element.119), calls=%async_computation.1 | async-start | bytes 9437184 | tf_op jit(solution)/shard_map/all_to_all | solution.py:1706
  394.7 60.5 %collective-permute-start.1 = (bf16[2,768,768]{2,1,0:T(8,128)(2,1)}, bf16[2,768,768]{2,1,0:T(8,128)(2,1)S(1)}, u32[]{:S(2)}, u32[]{:S(2)}) collective-permute-start(bf16[2,768,768]{2,1,0:T(8,128)(2,1)} %get-tuple-element.120), channel_id=1, source_target_pairs={{0,1},{1,0},{2,3},{3,2},{4,5},{5,4},{6,7},{7,6},{8,9},{9,8},{10,11... | collective-permute-start | bytes 7077896 | tf_op jit(solution)/shard_map/ppermute | solution.py:1702
  432.4 88.0 %collective-permute-start.2 = (bf16[2,768,768]{2,1,0:T(8,128)(2,1)}, bf16[2,768,768]{2,1,0:T(8,128)(2,1)}, u32[]{:S(2)}, u32[]{:S(2)}) collective-permute-start(bf16[2,768,768]{2,1,0:T(8,128)(2,1)} %get-tuple-element.139), channel_id=1, source_target_pairs={{0,1},{1,0},{2,3},{3,2},{4,5},{5,4},{6,7},{7,6},{8,9},{9,8},{10,11... | collective-permute-start | bytes 7077896 | tf_op jit(solution)/shard_map/ppermute | solution.py:1702
  455.2 64.0 %copy-start.3 = (bf16[2,768,768]{2,1,0:T(8,128)(2,1)}, bf16[2,768,768]{2,1,0:T(8,128)(2,1)S(1)}, u32[]{:S(2)}) copy-start(bf16[2,768,768]{2,1,0:T(8,128)(2,1)S(1)} %collective-permute-done.1) | copy-start | bytes 7077892
  455.2 63.9 %copy-start.14 = (f32[12,1024]{1,0:T(8,128)S(1)}, f32[12,1024]{1,0:T(8,128)}, u32[]{:S(2)}) copy-start(f32[12,1024]{1,0:T(8,128)} %get-tuple-element.134) | copy-start | bytes 147460
  455.2 65.1 %copy-start.9 = (f32[1,768]{1,0:T(1,128)S(1)}, f32[1,768]{1,0:T(1,128)}, u32[]{:S(2)}) copy-start(f32[1,768]{1,0:T(1,128)} %get-tuple-element.132) | copy-start | bytes 9220
  455.3 65.1 %copy-start.10 = (f32[1,768]{1,0:T(1,128)S(1)}, f32[1,768]{1,0:T(1,128)}, u32[]{:S(2)}) copy-start(f32[1,768]{1,0:T(1,128)} %get-tuple-element.131) | copy-start | bytes 9220
  455.3 65.1 %copy-start.11 = (f32[1,768]{1,0:T(1,128)S(1)}, f32[1,768]{1,0:T(1,128)}, u32[]{:S(2)}) copy-start(f32[1,768]{1,0:T(1,128)} %get-tuple-element.130) | copy-start | bytes 9220
  608.0 5.0 copy-start.4
  610.0 4.1 copy-start.6
  610.7 4.1 copy-start.2
  614.1 3.9 slice-start
  614.8 3.5 slice-start.1
  618.4 2.2 copy-start.1

commit v5 on v4

--- a/solution.py
+++ b/solution.py
@@ -1351,10 +1351,15 @@
 
 def return_rows_kernel(
     owners, zones, capacity,
-    rows_ref, dgate_ref, slot_ref, gates_ref, route_ref, x_ref, gain_ref, router_ref, normed_ref, top_ref,
-    dx_ref, dgain_ref, drouter_ref,
-    back_ref, tags_ref, tags_in_ref, part_ref, part_in_ref, mark_ref, mark_in_ref, sum_ref, send_sem, recv_sem, local_sem,
+    rows_ref, hidden_in, pre_in, dey_in, sent_in, own_down_in, peer_down_in,
+    gate_cols_ref, dgate_ref, slot_ref, gates_ref, route_ref, x_ref, gain_ref, router_ref, normed_ref, top_ref,
+    dx_ref, dgain_ref, drouter_ref, *refs,
 ):
+    outs, y_out, refs = (refs[0:2], refs[2:4]), refs[4], refs[5:]
+    (hidden_ref, pre_ref, dey_ref, sent_ref, own_ref, peer_ref, load_sem, store_sem), refs = refs[:8], refs[8:]
+    (down_ref, y_ref, down_sem, y_sem), refs = refs[:4], refs[4:]
+    (back_ref, tags_ref, tags_in_ref, part_ref, part_in_ref, mark_ref, mark_in_ref, sum_ref, send_sem, recv_sem,
+     local_sem) = refs
     owner, zone = lax.axis_index("expert"), lax.axis_index("shard")
     tags_ref[...] = jnp.zeros_like(tags_ref)
     greet_plane(owner, zone, owners, zones)
@@ -1427,11 +1432,96 @@
                 marks[k] = marks[k] + sum_pieces(nn(pieces, hits[k]))
         return marks
 
+    def load(e):
+        return [
+            pltpu.make_async_copy(source, target.at[e], load_sem.at[e, i])
+            for i, (source, target) in enumerate((
+                (hidden_in.at[e], hidden_ref), (pre_in.at[e], pre_ref), (dey_in.at[e], dey_ref),
+                (sent_in.at[:, e], sent_ref),
+            ))
+        ]
+
+    def stores(turn):
+        e, kind, slot = turn // 2, turn % 2, turn % 2
+        return [
+            pltpu.make_async_copy(ref.at[slot], out[kind].at[e], store_sem.at[slot, i])
+            for i, (ref, out) in enumerate(((own_ref, outs[0]), (peer_ref, outs[1])))
+        ]
+
+    size = hidden_ref.shape[2] // 2
+    width = dey_ref.shape[2]
+
+    def weight_turn(turn):
+        e, kind = turn // 2, turn % 2
+        if kind == 0:
+            for copy in load(e):
+                copy.wait()
+        if turn >= 2:
+            for copy in stores(turn - 2):
+                copy.wait()
+        total = width if kind == 0 else size
+        step = 256 if total % 256 == 0 else 128
+        columns = size if kind == 0 else width
+
+        @pl.loop(0, total // step)
+        def _(i):
+            at = pl.ds(pl.multiple_of(i * step, step), step)
+            if kind == 0:
+                rows = sent_ref[e, :, :, at].reshape(-1, step)
+                own_ref[turn % 2, at, 0:columns] = tn(rows, pre_ref[e, :, 0:size])
+                peer_ref[turn % 2, at, 0:columns] = tn(rows, pre_ref[e, :, size:]).astype(BF)
+            else:
+                peer_at = pl.ds(pl.multiple_of(i * step + size, step), step)
+                own_ref[turn % 2, at, :] = tn(hidden_ref[e, :, at], dey_ref[e])
+                peer_ref[turn % 2, at, :] = tn(hidden_ref[e, :, peer_at], dey_ref[e]).astype(BF)
+
+        for copy in stores(turn):
+            copy.start()
+
+    def down_load(e):
+        return [
+            pltpu.make_async_copy(source.at[e], down_ref.at[e, i], down_sem.at[e, i])
+            for i, source in enumerate((own_down_in, peer_down_in))
+        ]
+
+    group = y_ref.shape[1]
+    tiles = owners // group
+
+    def y_store(e, i):
+        return pltpu.make_async_copy(
+            y_ref.at[i % 2], y_out.at[pl.ds(i * group, group), e], y_sem.at[i % 2]
+        )
+
+    def y_turn(e):
+        for copy in down_load(e):
+            copy.wait()
+        rows = group * sent_ref.shape[2]
+
+        @pl.loop(0, tiles)
+        def _(i):
+            pl.when(i >= 2)(lambda: y_store(e, i - 2).wait())
+            at = pl.ds(pl.multiple_of(i * rows, 16), rows)
+            y = nn(hidden_ref[e, at, 0:size], down_ref[e, 0]) + nn(hidden_ref[e, at, size:], down_ref[e, 1])
+            y = gate_cols_ref[pl.ds(i * group, group), e].reshape(rows, 1) * y
+            y_ref[i % 2] = y.astype(BF).reshape(group, sent_ref.shape[2], width)
+            y_store(e, i).start()
+
+        for i in range(max(0, tiles - 2), tiles):
+            y_store(e, i).wait()
+
+    turns = 2 * hidden_ref.shape[0]
+    for e in range(hidden_ref.shape[0]):
+        for copy in load(e) + down_load(e):
+            copy.start()
     for d in range(1, groups):
         ship(d, 0)
         ship_tags(d)
     incoming = {d: [] for d in range(1, groups)}
     for half in range(2):
+        for turn in ((0, 1), (2,))[half]:
+            weight_turn(turn)
+        if half == 1:
+            y_turn(0)
         for d in range(1, groups):
             for mask in peer_order(owners):
                 for copy in arrivals.get((d, half, mask), []):
@@ -1451,6 +1541,10 @@
             if half == 0:
                 mark_ref[d - 1] = jnp.concatenate(marks + [jnp.zeros((6, marks[0].shape[1]), F32)], axis=0)
                 incoming[d].append(send(mark_ref.at[d - 1], mark_in_ref.at[d - 1], device))
+    for turn in range(3, turns):
+        weight_turn(turn)
+    for e in range(1, hidden_ref.shape[0]):
+        y_turn(e)
     marks = collect_zone(0, None)
     for d in range(1, groups):
         for copy in incoming[d]:
@@ -1479,14 +1573,18 @@
     for (d, half, _), copies in arrivals.items():
         if d == 0 or half == "tags":
             sent.extend(copies)
+    for turn in range(max(0, turns - 2), turns):
+        for copy in stores(turn):
+            copy.wait()
     for copy in sent:
         copy.wait_send()
 
 
-def return_rows(rows, dgate, slot_rows, gates, route_rows, x, gain, router, normed, top, zones, capacity):
+def return_rows(rows, hidden, pre, dey, sent, own_down, peer_down, gate_cols, dgate, slot_rows, gates, route_rows, x, gain, router, normed, top, zones, capacity):
     length, width = x.shape
     owners, local = rows.shape[:2]
     groups = zones // 2
+    size = hidden.shape[2] // 2
     span = local * capacity
     wide = -(-span // 128) * 128
     copies = 3 * (groups - 1) + (owners - 1) * (local + 1 + (groups - 1) * (2 * local + 1))
@@ -1496,10 +1594,27 @@
             jax.ShapeDtypeStruct((length, width), F32),
             jax.ShapeDtypeStruct((1, width), F32),
             jax.ShapeDtypeStruct(router.shape, F32),
+            jax.ShapeDtypeStruct((local, width, size), F32),
+            jax.ShapeDtypeStruct((local, size, width), F32),
+            jax.ShapeDtypeStruct((local, width, size), BF),
+            jax.ShapeDtypeStruct((local, size, width), BF),
+            jax.ShapeDtypeStruct(sent.shape, BF),
         ),
-        in_specs=[pl.BlockSpec(memory_space=pltpu.HBM)] + [VMEM_SPEC] * 9,
-        out_specs=[VMEM_SPEC] * 3,
+        in_specs=[HBM_SPEC] * 7 + [VMEM_SPEC] * 10,
+        out_specs=[VMEM_SPEC] * 3 + [HBM_SPEC] * 5,
         scratch_shapes=[
+            pltpu.VMEM(hidden.shape, BF),
+            pltpu.VMEM(pre.shape, BF),
+            pltpu.VMEM(dey.shape, BF),
+            pltpu.VMEM((local, owners) + sent.shape[2:], BF),
+            pltpu.VMEM((2, max(width, size), width), F32),
+            pltpu.VMEM((2, max(width, size), width), BF),
+            pltpu.SemaphoreType.DMA((local, 4)),
+            pltpu.SemaphoreType.DMA((2, 2)),
+            pltpu.VMEM((local, 2, size, width), BF),
+            pltpu.VMEM((2, max(1, 384 // sent.shape[2])) + sent.shape[2:], BF),
+            pltpu.SemaphoreType.DMA((local, 2)),
+            pltpu.SemaphoreType.DMA((2,)),
             pltpu.VMEM((groups, owners, span, width), BF),
             pltpu.VMEM((groups, owners, 8, wide), F32),
             pltpu.VMEM((groups, owners, 8, wide), F32),
@@ -1516,7 +1631,7 @@
             vmem_limit_bytes=61 * 1024 * 1024, collective_id=4, has_side_effects=True
         ),
         name="return_rows",
-    )(rows, dgate, slot_rows, gates, route_rows, x, gain, router, normed, top)
+    )(rows, hidden, pre, dey, sent, own_down, peer_down, gate_cols, dgate, slot_rows, gates, route_rows, x, gain, router, normed, top)
 
 
 def experts_kernel(
@@ -1569,6 +1684,31 @@
         own_down_ref[at, :] = tn(hidden_ref[:, at], dey_ref[...])
         peer_at = pl.ds(pl.multiple_of(i * step + size, step), step)
         peer_down_ref[at, :] = tn(hidden_ref[:, peer_at], dey_ref[...]).astype(BF)
+
+
+def experts_rows_kernel(
+    x_ref, c_ref, gate_ref, own_up_in, own_down_in, peer_up_in, peer_down_in,
+    dx_ref, dgate_ref, hidden_ref, pre_ref, dey_ref,
+):
+    group, _, span, width = x_ref.shape
+    size = own_up_in.shape[1]
+    rows = group * span
+    x = x_ref[:, 0].reshape(rows, width)
+    c = c_ref[:, 0].reshape(rows, width)
+    gate = gate_ref[:, 0].reshape(rows, 1)
+    dey_ref[...] = (gate * c.astype(F32)).astype(BF)
+    dgate = jnp.zeros((rows, 1), F32)
+    for part, (up_ref, down_ref) in enumerate(((own_up_in, own_down_in), (peer_up_in, peer_down_in))):
+        cols = slice(part * size, part * size + size)
+        hidden, slope = gelu_parts(nn(x, up_ref[...]))
+        hidden = hidden.astype(BF)
+        hidden_ref[:, cols] = hidden
+        back = nt(c, down_ref[...])
+        dgate = dgate + jnp.sum(hidden.astype(F32) * back, axis=1, keepdims=True)
+        pre_ref[:, cols] = (gate * back * slope).astype(BF)
+    dx = nt(pre_ref[:, 0:size], own_up_in[...]) + nt(pre_ref[:, size:], peer_up_in[...])
+    dx_ref[:, 0] = dx.astype(BF).reshape(group, span, width)
+    dgate_ref[:, 0] = dgate.reshape(group, span, 1)
 
 
 def run_experts(x, c, gate, own_up, own_down, peer_up, peer_down):
@@ -1610,6 +1750,41 @@
     )(x, c, gate, own_up, own_down, peer_up, peer_down)
 
 
+def run_expert_rows(x, c, gate, own_up, own_down, peer_up, peer_down):
+    sources, local, span, width = x.shape
+    hidden = own_up.shape[2]
+    group = max(1, 384 // span)
+    rows = group * span
+    tiles = sources // group
+    row_spec = pl.BlockSpec((group, 1, span, width), lambda e, i: (i, e, 0, 0))
+    gate_spec = pl.BlockSpec((group, 1, span, 1), lambda e, i: (i, e, 0, 0))
+    sq = pl.Squeezed()
+    up_spec = pl.BlockSpec((sq, width, hidden), lambda e, i: (e, 0, 0))
+    down_spec = pl.BlockSpec((sq, hidden, width), lambda e, i: (e, 0, 0))
+    wide_spec = pl.BlockSpec((sq, rows, 2 * hidden), lambda e, i: (e, i, 0))
+    dey_spec = pl.BlockSpec((sq, rows, width), lambda e, i: (e, i, 0))
+    everything = local * sources * span
+    return pl.pallas_call(
+        experts_rows_kernel,
+        grid=(local, tiles),
+        out_shape=(
+            jax.ShapeDtypeStruct(x.shape, BF),
+            jax.ShapeDtypeStruct(gate.shape, F32),
+            jax.ShapeDtypeStruct((local, sources * span, 2 * hidden), BF),
+            jax.ShapeDtypeStruct((local, sources * span, 2 * hidden), BF),
+            jax.ShapeDtypeStruct((local, sources * span, width), BF),
+        ),
+        in_specs=[row_spec, row_spec, gate_spec, up_spec, down_spec, up_spec, down_spec],
+        out_specs=[row_spec, gate_spec, wide_spec, wide_spec, dey_spec],
+        compiler_params=pltpu.CompilerParams(vmem_limit_bytes=60 * 1024 * 1024),
+        cost_estimate=pl.CostEstimate(
+            flops=12 * everything * width * hidden, bytes_accessed=16 * everything * width,
+            transcendentals=2 * everything * hidden,
+        ),
+        name="expert_rows",
+    )(x, c, gate, own_up, own_down, peer_up, peer_down)
+
+
 def spread_kernel(slot_ref, rows_ref, out_ref):
     experts, zones, capacity, width = out_ref.shape
     take = max(1, 384 // capacity)
@@ -1799,15 +1974,19 @@
         gate_rows = exchange(
             jnp.stack([gate_slots(d) for d in range(zones)], axis=1).reshape(owners, local, zones * capacity)
         )[..., None]
-    y_rows, dx_rows, dgate_rows, own_up, own_down, peer_up, peer_down = run_experts(
-        eh_rows, cotangent_rows, gate_rows, expert_up, expert_down, up_other, down_other
-    )
+    expert_weights = (expert_up, expert_down, up_other, down_other)
     if direct:
-        dx3, dgain3, grad_router = return_rows(
-            dx_rows, dgate_rows, slot_rows, gates, route_rows, x3, gains[3], router_full, eh, cotangent,
-            zones_all, capacity,
+        dx_rows, dgate_rows, hidden_rows, pre_rows, dey_rows = run_expert_rows(
+            eh_rows, cotangent_rows, gate_rows, *expert_weights
+        )
+        dx3, dgain3, grad_router, own_up, own_down, peer_up, peer_down, y_rows = return_rows(
+            dx_rows, hidden_rows, pre_rows, dey_rows, eh_rows, expert_down, down_other, gate_rows, dgate_rows,
+            slot_rows, gates, route_rows, x3, gains[3], router_full, eh, cotangent, zones_all, capacity,
         )
     else:
+        y_rows, dx_rows, dgate_rows, own_up, own_down, peer_up, peer_down = run_experts(
+            eh_rows, cotangent_rows, gate_rows, *expert_weights
+        )
         dx_back = undo(dx_rows)
         dgate_back = exchange(dgate_rows[..., 0]).reshape(experts_all, zones, capacity)
         token_grad, gate_grad = dx_back[0], 0.0

time: 630 us -> 600 us (0.952)
  Pallas kernels: 565 us -> 535 us
    pallas_call x1, Pallas kernels: 69 us -> 37.2 us  [run_expert_rows(): pl.pallas_call(experts_rows_kernel, grid=(local, tiles), out_shape=(jax.S...]
  transfers between devices with their start and end apart: 5 -> 5, of which waited for: 0 -> 0; matrix products, arithmetic and copies ran while one was open for 1% -> 1% of each run, Pallas kernels for 27% -> 29%
where the time goes in v5:
time: 600 us; the launch traced here: 591 us
  Pallas kernels  535 us (89%)
  local copies, waits for them, and re-layouts  28 us (5%)
  starting transfers between devices  19.6 us (3%)
    pallas_call x1, Pallas kernels, gather_weights(): pl.pallas_call(lambda *refs: gather_kernel(owners, zones, used_rows, expe...  106 us
    pallas_call x2, Pallas kernels, attend_back(): pl.pallas_call(lambda *refs: attend_back_kernel(bool(tails), weights, rid...  99.7 us
    pallas_call x1, Pallas kernels, finish(): pl.pallas_call(lambda *refs: finish_kernel(owners, zones, capacity, sizes...  78.1 us
    pallas_call x1, Pallas kernels, send_rows(): pl.pallas_call(lambda *refs: send_rows_kernel(owners, zones, capacity, *r...  77.2 us
    pallas_call x1, Pallas kernels, return_rows(): pl.pallas_call(lambda *refs: return_rows_kernel(owners, zones, capacity,...  66.2 us
    pallas_call x2, Pallas kernels, attend(): pl.pallas_call(lambda *refs: attend_kernel(weights, *refs), out_shape=(ja...  37.6 us
    pallas_call x1, Pallas kernels, run_expert_rows(): pl.pallas_call(experts_rows_kernel, grid=(local, tiles), out_shape=(jax.S...  37.2 us
    pallas_call x1, Pallas kernels, mlp_back(): pl.pallas_call(lambda *refs: mlp_back_kernel(parts, zones, *refs), out_sh...  21.8 us
  transfers between devices with their start and end apart: 5, of which 0 were waited for; matrix products, arithmetic and copies ran while one was open for 1% of the time, Pallas kernels for 29%

profile of v5, /device:TPU:0, one launch (start us, length us, event | category | flops | bytes accessed | tf_op | source)
XLA Modules:
  0.0 590.8 jit_solution(16860357986479570950)
XLA Ops:
  2.3 1.1 reshape.111
  7.1 106.2 %gather_weights.1 = (bf16[8,384,768]{2,1,0:T(8,128)(2,1)}, bf16[8,384,768]{2,1,0:T(8,128)(2,1)}, bf16[8,384,768]{2,1,0:T(8,128)(2,1)}, bf16[8,400,768]{2,1,0:T(8...) custom-call(bf16[192,384]{1,0:T(8,128)(2,1)} %pad_maximum_fusion.2.refs_0_, bf16[192,384]{1,0:T(8,128)(2,1)} %refs_1_.1, ...), custom_call_target="tpu_custom_call" | custom-call | tf_op jit(solution)/shard_map/gather_weights/pallas_call | solution.py:711
  113.4 5.5 all-to-all-start
  118.8 7.0 %collective-permute-start = (bf16[2,768,768]{2,1,0:T(8,128)(2,1)S(1)}, bf16[2,768,768]{2,1,0:T(8,128)(2,1)}, u32[]{:S(2)}, u32[]{:S(2)}) collective-permute-start(bf16[2,768,768]{2,1,0:T(8,128)(2,1)S(1)} %copy-done.13), channel_id=1, source_target_pairs={{0,1},{1,0},{2,3},{3,2},{4,5},{5,4},{6,7},{7,6},{8,9},{9,8},{10,11... | collective-permute-start | bytes 7077896 | tf_op jit(solution)/shard_map/ppermute | solution.py:1877
  126.5 1.3 convert_element_type.19.refs_1_
  131.0 18.8 %attend.2 = (f32[512,768]{1,0:T(8,128)}, bf16[512,768]{1,0:T(8,128)(2,1)}, bf16[512,2304]{1,0:T(8,128)(2,1)}, bf16[512,768]{1,0:T(8,128)(2,1)}, f32[12,512]{1,0:T(8,128)}) custom-call(s32[1]{0:T(128)S(6)} %copy.49.refs_0_, f32[512,768]{1,0:T(8,128)} %convert_element_type.19.refs_1_, f32[1,768]{1,0:T(1,128)} %get-tuple-element.198.refs_2_, ...), custom_call_target="tpu_custom_call" | custom-call | flops 3221225472 | bytes 12582912 | tf_op jit(solution)/shard_map/attend/pallas_call | solution.py:180
  149.7 10.8 %mlp.1 = (f32[512,768]{1,0:T(8,128)}, bf16[512,768]{1,0:T(8,128)(2,1)}) custom-call(f32[512,768]{1,0:T(8,128)} %get-tuple-element.90.refs_0_, f32[1,768]{1,0:T(1,128)} %get-tuple-element.197.refs_1_, bf16[3072,768]{1,0:T(8,128)(2,1)} %bitcast.68, bf16[8,384,768]{2,1,0:T(8,128)(2,1)} %get-tuple-element.92.refs_3_), custom_call_target="tpu_custom_call" | custom-call | flops 4831838208 | bytes 13369344 | tf_op jit(solution)/shard_map/mlp/pallas_call | solution.py:449
  160.6 18.8 %attend.3 = (f32[512,768]{1,0:T(8,128)}, bf16[512,768]{1,0:T(8,128)(2,1)}, bf16[512,2304]{1,0:T(8,128)(2,1)}, bf16[512,768]{1,0:T(8,128)(2,1)}, f32[12,512]{1,0:T(8,128)}) custom-call(s32[1]{0:T(128)S(6)} %copy.49.refs_0_, f32[512,768]{1,0:T(8,128)} %get-tuple-element.94.refs_1_, f32[1,768]{1,0:T(1,128)} %get-tuple-element.199.refs_2_, ...), custom_call_target="tpu_custom_call" | custom-call | flops 3221225472 | bytes 12582912 | tf_op jit(solution)/shard_map/attend/pallas_call | solution.py:180
  179.4 77.2 %send_rows.1 = (bf16[512,768]{1,0:T(8,128)(2,1)}, f32[8,512]{1,0:T(8,128)}, bf16[8,2,192,768]{3,2,1,0:T(8,128)(2,1)}, f32[8,2,192,1]{3,2,1,0:T(8,128)}, bf16[2,768,768]{2,1,0:T(8,128)(2,1)}) custom-call(f32[512,768]{1,0:T(8,128)} %get-tuple-element.103.refs_0_.refs_12_.refs_11_, f32[1,768]{1,0:T(1,128)} %get-tuple-element.196.refs_1_.refs_13_, ...), custom_call_target="tpu_custom_call" | custom-call | tf_op jit(solution)/shard_map/send_rows/pallas_call | solution.py:1324
  256.6 37.2 %expert_rows.1 = (bf16[8,2,192,768]{3,2,1,0:T(8,128)(2,1)}, f32[8,2,192,1]{3,2,1,0:T(8,128)}, bf16[2,1536,1536]{2,1,0:T(8,128)(2,1)}, bf16[2,1536,1536]{2,1,0:T(8,128)(2,1)}, bf16[2,1536,768]{2,1,0:T(8,128)(2,1)}) custom-call(bf16[8,2,192,768]{3,2,1,0:T(8,128)(2,1)} %get-tuple-element.105.x_ref.refs_4_, bf16[8,2,192,768]{3,2,1,0:T(8,128)(2,1)} %all-to-all-done.c_ref, ...), custom_call_target="tpu_custom_call" | custom-call | flops 21743271936 | bytes 37748736 | tf_op jit(solution)/shard_map/expert_rows/pallas_call | solution.py:1767
  293.8 66.2 %return_rows.1 = (f32[512,768]{1,0:T(8,128)}, f32[1,768]{1,0:T(1,128)}, f32[16,768]{1,0:T(8,128)}, f32[2,768,768]{2,1,0:T(8,128)}, f32[2,768,768]{2,1,0:T(8,128)...) custom-call(bf16[8,2,192,768]{3,2,1,0:T(8,128)(2,1)} %get-tuple-element.110.refs_0_, ...), custom_call_target="tpu_custom_call" | custom-call | tf_op jit(solution)/shard_map/return_rows/pallas_call | solution.py:1591
  360.0 4.9 all-to-all-start.1
  366.3 35.8 %attend_back.2 = (f32[512,768]{1,0:T(8,128)}, bf16[8,400,768]{2,1,0:T(8,128)(2,1)}, f32[12,1024]{1,0:T(8,128)}, f32[1,768]{1,0:T(1,128)}) custom-call(s32[1]{0:T(128)S(6)} %copy.49.refs_0_, f32[512,768]{1,0:T(8,128)} %get-tuple-element.94.refs_1_, f32[1,768]{1,0:T(1,128)} %get-tuple-element.199.refs_2_, bf16[8,400,768]{2,1,0:T(8,128)(2,1)} %get-tuple-element.95.refs_3_, ...), custom_call_target="tpu_custom_call" | custom-call | flops 6845104128 | bytes 25165824 | tf_op jit(solution)/shard_map/attend_back/pallas_call | solution.py:361
  402.1 1.5 collective-permute-start.2
  403.6 21.8 %mlp_back.1 = (f32[512,768]{1,0:T(8,128)}, bf16[3072,768]{1,0:T(8,128)(2,1)}, bf16[8,384,768]{2,1,0:T(8,128)(2,1)}, f32[1,768]{1,0:T(1,128)}) custom-call(f32[512,768]{1,0:T(8,128)} %get-tuple-element.90.refs_0_, f32[1,768]{1,0:T(1,128)} %get-tuple-element.197.refs_1_, bf16[3072,768]{1,0:T(8,128)(2,1)} %bitcast.69, ...), custom_call_target="tpu_custom_call" | custom-call | flops 12079595520 | bytes 25165824 | tf_op jit(solution)/shard_map/mlp_back/pallas_call | solution.py:497
  425.5 63.9 %attend_back.3 = (bf16[400,768]{1,0:T(8,128)(2,1)}, bf16[384,768]{1,0:T(8,128)(2,1)}, bf16[1,512,768]{2,1,0:T(8,128)(2,1)}, f32[512,768]{1,0:T(8,128)}, bf16[8,3...) custom-call(s32[1]{0:T(128)S(6)} %copy.49.refs_0_, f32[512,768]{1,0:T(8,128)} %convert_element_type.19.refs_1_, ...), custom_call_target="tpu_custom_call" | custom-call | flops 6845104128 | bytes 25165824 | tf_op jit(solution)/shard_map/attend_back/pallas_call | solution.py:361
  489.4 1.1 fusion.4
  491.9 78.1 %finish.1 = (f32[192,512]{1,0:T(8,128)}, f32[192,384]{1,0:T(8,128)}, f32[192,384]{1,0:T(8,128)}, f32[192,384]{1,0:T(8,128)}, f32[40,128]{1,0:T(8,128)}, /*index=...) custom-call(bf16[400,768]{1,0:T(8,128)(2,1)} %get-tuple-element.131.refs_0_, ...), custom_call_target="tpu_custom_call" | custom-call | tf_op jit(solution)/shard_map/finish/pallas_call | solution.py:1169
  572.1 1.1 slice_bitcast_fusion
  576.6 1.2 reshape.130
  580.6 2.2 copy.50
  582.8 1.1 copy.51
  584.7 2.4 copy.53
  588.2 2.2 copy.54
  (78 shorter events, 21.3 us)
Async XLA Ops:
  0.6 129.4 %copy-start = (f32[2,12,44]{2,0,1:T(2,128)S(1)}, f32[2,12,44]{2,0,1:T(2,128)}, u32[]{:S(2)}) copy-start(f32[2,12,44]{2,0,1:T(2,128)} %param.18) | copy-start | bytes 12676
  113.3 5.5 copy-start.13
  113.3 13.2 %copy-start.5 = (bf16[512,768]{1,0:T(8,128)(2,1)S(1)}, bf16[512,768]{1,0:T(8,128)(2,1)}, u32[]{:S(2)}) copy-start(bf16[512,768]{1,0:T(8,128)(2,1)} %param.14) | copy-start | bytes 2359300
  113.3 16.0 %copy-start.12 = (s32[21]{0:T(128)S(1)}, s32[21]{0:T(128)}, u32[]{:S(2)}) copy-start(s32[21]{0:T(128)} %constant.16.clone) | copy-start | bytes 256
  113.3 16.1 %copy-start.8 = (f32[4,768]{1,0:T(4,128)S(1)}, f32[4,768]{1,0:T(4,128)}, u32[]{:S(2)}) copy-start(f32[4,768]{1,0:T(4,128)} %param.17) | copy-start | bytes 36868
  113.4 66.1 %all-to-all-start = ((bf16[8,2,192,768]{3,2,1,0:T(8,128)(2,1)}), bf16[8,2,192,768]{3,2,1,0:T(8,128)(2,1)}, u32[]{:S(2)}, u32[]{:S(2)}) async-start(bf16[8,2,192,768]{3,2,1,0:T(8,128)(2,1)} %bitcast.55), calls=%async_computation | async-start | bytes 9437184 | tf_op jit(solution)/shard_map/all_to_all | solution.py:1881
  118.8 60.6 %collective-permute-start = (bf16[2,768,768]{2,1,0:T(8,128)(2,1)S(1)}, bf16[2,768,768]{2,1,0:T(8,128)(2,1)}, u32[]{:S(2)}, u32[]{:S(2)}) collective-permute-start(bf16[2,768,768]{2,1,0:T(8,128)(2,1)S(1)} %copy-done.13), channel_id=1, source_target_pairs={{0,1},{1,0},{2,3},{3,2},{4,5},{5,4},{6,7},{7,6},{8,9},{9,8},{10,11... | collective-permute-start | bytes 7077896 | tf_op jit(solution)/shard_map/ppermute | solution.py:1877
  360.0 5.6 copy-start.7
  360.0 65.5 %all-to-all-start.1 = ((bf16[8,2,192,768]{3,2,1,0:T(8,128)(2,1)}), bf16[8,2,192,768]{3,2,1,0:T(8,128)(2,1)}, u32[]{:S(2)}, u32[]{:S(2)}) async-start(bf16[8,2,192,768]{3,2,1,0:T(8,128)(2,1)} %get-tuple-element.125), calls=%async_computation.1 | async-start | bytes 9437184 | tf_op jit(solution)/shard_map/all_to_all | solution.py:1881
  364.9 60.5 %collective-permute-start.1 = (bf16[2,768,768]{2,1,0:T(8,128)(2,1)}, bf16[2,768,768]{2,1,0:T(8,128)(2,1)S(1)}, u32[]{:S(2)}, u32[]{:S(2)}) collective-permute-start(bf16[2,768,768]{2,1,0:T(8,128)(2,1)} %get-tuple-element.126), channel_id=1, source_target_pairs={{0,1},{1,0},{2,3},{3,2},{4,5},{5,4},{6,7},{7,6},{8,9},{9,8},{10,11... | collective-permute-start | bytes 7077896 | tf_op jit(solution)/shard_map/ppermute | solution.py:1877
  402.1 88.4 %collective-permute-start.2 = (bf16[2,768,768]{2,1,0:T(8,128)(2,1)}, bf16[2,768,768]{2,1,0:T(8,128)(2,1)}, u32[]{:S(2)}, u32[]{:S(2)}) collective-permute-start(bf16[2,768,768]{2,1,0:T(8,128)(2,1)} %get-tuple-element.145), channel_id=1, source_target_pairs={{0,1},{1,0},{2,3},{3,2},{4,5},{5,4},{6,7},{7,6},{8,9},{9,8},{10,11... | collective-permute-start | bytes 7077896 | tf_op jit(solution)/shard_map/ppermute | solution.py:1877
  425.4 63.9 %copy-start.3 = (bf16[2,768,768]{2,1,0:T(8,128)(2,1)}, bf16[2,768,768]{2,1,0:T(8,128)(2,1)S(1)}, u32[]{:S(2)}) copy-start(bf16[2,768,768]{2,1,0:T(8,128)(2,1)S(1)} %collective-permute-done.1) | copy-start | bytes 7077892
  425.4 63.9 %copy-start.14 = (f32[12,1024]{1,0:T(8,128)S(1)}, f32[12,1024]{1,0:T(8,128)}, u32[]{:S(2)}) copy-start(f32[12,1024]{1,0:T(8,128)} %get-tuple-element.140) | copy-start | bytes 147460
  425.5 65.1 %copy-start.9 = (f32[1,768]{1,0:T(1,128)S(1)}, f32[1,768]{1,0:T(1,128)}, u32[]{:S(2)}) copy-start(f32[1,768]{1,0:T(1,128)} %get-tuple-element.138) | copy-start | bytes 9220
  425.5 65.1 %copy-start.10 = (f32[1,768]{1,0:T(1,128)S(1)}, f32[1,768]{1,0:T(1,128)}, u32[]{:S(2)}) copy-start(f32[1,768]{1,0:T(1,128)} %get-tuple-element.137) | copy-start | bytes 9220
  425.5 65.1 %copy-start.11 = (f32[1,768]{1,0:T(1,128)S(1)}, f32[1,768]{1,0:T(1,128)}, u32[]{:S(2)}) copy-start(f32[1,768]{1,0:T(1,128)} %get-tuple-element.136) | copy-start | bytes 9220
  570.0 12.8 %copy-start.4 = (f32[512,768]{1,0:T(8,128)S(1)}, f32[512,768]{1,0:T(8,128)}, u32[]{:S(2)}) copy-start(f32[512,768]{1,0:T(8,128)} %get-tuple-element.216) | copy-start | bytes 4718596
  572.1 11.9 %copy-start.6 = (f32[192,384]{1,0:T(8,128)S(1)}, f32[192,384]{1,0:T(8,128)}, u32[]{:S(2)}) copy-start(f32[192,384]{1,0:T(8,128)} %get-tuple-element.221) | copy-start | bytes 884740
  579.0 5.6 copy-start.2
  583.9 3.9 slice-start
  584.7 3.5 slice-start.1
  584.7 5.7 copy-start.1

commit v6 on v5

--- a/solution.py
+++ b/solution.py
@@ -111,7 +111,7 @@
     wo_copies = flatten(wo_ref, flat_out_ref, wo_sem)
     tiles = length // 128
     fill_mask(piece_ref, mask_ref)
-    field = x_ref[...]
+    field = x_ref[...].astype(F32)
     normed_ref[...] = (field * inverse_rms(field) * gain_ref[...]).astype(BF)
 
     arrive(w_copies)
@@ -161,7 +161,7 @@
 
     def back(c, _):
         cols = pl.ds(pl.multiple_of(c * 256, 256), 256)
-        out_ref[:, cols] = x_ref[:, cols] + nt(mixed_ref[...], flat_out_ref[cols, :])
+        out_ref[:, cols] = x_ref[:, cols].astype(F32) + nt(mixed_ref[...], flat_out_ref[cols, :])
         return 0
 
     lax.fori_loop(0, width // 256, back, 0)
@@ -262,10 +262,10 @@
     sums_ref[...] = jnp.zeros_like(sums_ref)
 
     def pair(hp, _):
+        for at, turn in enumerate(turns):
+            pl.when(hp == min(3 * at, width // 128 - 1))(turn)
         if rows_turn is not None:
-            pl.when(hp == 0)(rows_turn)
-        for at, turn in enumerate(turns):
-            pl.when(hp == min(1 + 3 * at, width // 128 - 1))(turn)
+            pl.when(hp == 1)(rows_turn)
         base = hp * 128
         q_cols = pl.ds(pl.multiple_of(base, 128), 128)
         k_cols = pl.ds(pl.multiple_of(width + base, 128), 128)
@@ -342,7 +342,7 @@
 
 
 def norm_back(x_ref, gain_ref, upper_ref, base_ref, dx_ref, dgain_ref):
-    field = x_ref[...]
+    field = x_ref[...].astype(F32)
     inverse = inverse_rms(field)
     unit = field * inverse
     upper = upper_ref[...]
@@ -428,7 +428,7 @@
 
 def mlp_kernel(parts, zones, x_ref, gain_ref, up_hbm, down_hbm, out_ref, normed_ref, up_ref, down_ref, sems):
     loads = mlp_loads(parts, zones, up_hbm, down_hbm, up_ref, down_ref, sems)
-    field = x_ref[...]
+    field = x_ref[...].astype(F32)
     normed_ref[...] = (field * inverse_rms(field) * gain_ref[...]).astype(BF)
     out_ref[...] = field
 
@@ -1949,7 +1949,7 @@
         bias_tables, onehot, (((2,), (1,)), ((), ())), precision=lax.Precision.HIGHEST
     )
     gains = [norm_gains[i:i + 1] for i in range(4)]
-    x0 = tokens.astype(F32)
+    x0 = tokens
     x1, ah0, qkv0, o0, lse0 = attend(piece_start, x0, gains[0], weights0, vectors[0])
     x2, mh = mlp(x1, gains[1], up_full, down_full, parts, zones_all)
     x3, ah1, qkv1, o1, lse1 = attend(piece_start, x2, gains[2], weights1, vectors[1])

time: 600 us -> 599 us (level)
  transfers between devices with their start and end apart: 5 -> 5, of which waited for: 0 -> 0; matrix products, arithmetic and copies ran while one was open for 1% -> 1% of each run, Pallas kernels for 29% -> 28%
where the time goes in v6:
time: 599 us; the launch traced here: 590 us
  Pallas kernels  535 us (89%)
  local copies, waits for them, and re-layouts  28 us (5%)
  starting transfers between devices  19.5 us (3%)
    pallas_call x1, Pallas kernels, gather_weights(): pl.pallas_call(lambda *refs: gather_kernel(owners, zones, used_rows, expe...  106 us
    pallas_call x2, Pallas kernels, attend_back(): pl.pallas_call(lambda *refs: attend_back_kernel(bool(tails), weights, rid...  98 us
    pallas_call x1, Pallas kernels, finish(): pl.pallas_call(lambda *refs: finish_kernel(owners, zones, capacity, sizes...  79.4 us
    pallas_call x1, Pallas kernels, send_rows(): pl.pallas_call(lambda *refs: send_rows_kernel(owners, zones, capacity, *r...  78.6 us
    pallas_call x1, Pallas kernels, return_rows(): pl.pallas_call(lambda *refs: return_rows_kernel(owners, zones, capacity,...  65.7 us
    pallas_call x2, Pallas kernels, attend(): pl.pallas_call(lambda *refs: attend_kernel(weights, *refs), out_shape=(ja...  37.3 us
    pallas_call x1, Pallas kernels, run_expert_rows(): pl.pallas_call(experts_rows_kernel, grid=(local, tiles), out_shape=(jax.S...  37.2 us
    pallas_call x1, Pallas kernels, mlp_back(): pl.pallas_call(lambda *refs: mlp_back_kernel(parts, zones, *refs), out_sh...  21.8 us
  transfers between devices with their start and end apart: 5, of which 0 were waited for; matrix products, arithmetic and copies ran while one was open for 1% of the time, Pallas kernels for 28%

profile of v6, /device:TPU:0, one launch (start us, length us, event | category | flops | bytes accessed | tf_op | source)
XLA Modules:
  0.0 589.8 jit_solution(1357215316606601111)
XLA Ops:
  2.3 1.1 reshape.111
  7.1 106.2 %gather_weights.1 = (bf16[8,384,768]{2,1,0:T(8,128)(2,1)}, bf16[8,384,768]{2,1,0:T(8,128)(2,1)}, bf16[8,384,768]{2,1,0:T(8,128)(2,1)}, bf16[8,400,768]{2,1,0:T(8...) custom-call(bf16[192,384]{1,0:T(8,128)(2,1)} %pad_maximum_fusion.2.refs_0_, bf16[192,384]{1,0:T(8,128)(2,1)} %refs_1_.3, ...), custom_call_target="tpu_custom_call" | custom-call | tf_op jit(solution)/shard_map/gather_weights/pallas_call | solution.py:711
  113.3 5.3 all-to-all-start
  118.7 7.0 %collective-permute-start = (bf16[2,768,768]{2,1,0:T(8,128)(2,1)S(1)}, bf16[2,768,768]{2,1,0:T(8,128)(2,1)}, u32[]{:S(2)}, u32[]{:S(2)}) collective-permute-start(bf16[2,768,768]{2,1,0:T(8,128)(2,1)S(1)} %copy-done.12), channel_id=1, source_target_pairs={{0,1},{1,0},{2,3},{3,2},{4,5},{5,4},{6,7},{7,6},{8,9},{9,8},{10,11... | collective-permute-start | bytes 7077896 | tf_op jit(solution)/shard_map/ppermute | solution.py:1877
  129.5 18.5 %attend.2 = (f32[512,768]{1,0:T(8,128)}, bf16[512,768]{1,0:T(8,128)(2,1)}, bf16[512,2304]{1,0:T(8,128)(2,1)}, bf16[512,768]{1,0:T(8,128)(2,1)}, f32[12,512]{1,0:T(8,128)}) custom-call(s32[1]{0:T(128)S(6)} %copy.49.refs_0_, bf16[512,768]{1,0:T(8,128)(2,1)} %refs_1_.5, f32[1,768]{1,0:T(1,128)} %get-tuple-element.198.refs_2_, ...), custom_call_target="tpu_custom_call" | custom-call | flops 3221225472 | bytes 12582912 | tf_op jit(solution)/shard_map/attend/pallas_call | solution.py:180
  148.0 10.8 %mlp.1 = (f32[512,768]{1,0:T(8,128)}, bf16[512,768]{1,0:T(8,128)(2,1)}) custom-call(f32[512,768]{1,0:T(8,128)} %get-tuple-element.90.refs_0_, f32[1,768]{1,0:T(1,128)} %get-tuple-element.197.refs_1_, bf16[3072,768]{1,0:T(8,128)(2,1)} %bitcast.68, bf16[8,384,768]{2,1,0:T(8,128)(2,1)} %get-tuple-element.92.refs_3_), custom_call_target="tpu_custom_call" | custom-call | flops 4831838208 | bytes 13369344 | tf_op jit(solution)/shard_map/mlp/pallas_call | solution.py:449
  158.9 18.8 %attend.3 = (f32[512,768]{1,0:T(8,128)}, bf16[512,768]{1,0:T(8,128)(2,1)}, bf16[512,2304]{1,0:T(8,128)(2,1)}, bf16[512,768]{1,0:T(8,128)(2,1)}, f32[12,512]{1,0:T(8,128)}) custom-call(s32[1]{0:T(128)S(6)} %copy.49.refs_0_, f32[512,768]{1,0:T(8,128)} %get-tuple-element.94.refs_1_, f32[1,768]{1,0:T(1,128)} %get-tuple-element.199.refs_2_, ...), custom_call_target="tpu_custom_call" | custom-call | flops 3221225472 | bytes 12582912 | tf_op jit(solution)/shard_map/attend/pallas_call | solution.py:180
  177.7 78.6 %send_rows.1 = (bf16[512,768]{1,0:T(8,128)(2,1)}, f32[8,512]{1,0:T(8,128)}, bf16[8,2,192,768]{3,2,1,0:T(8,128)(2,1)}, f32[8,2,192,1]{3,2,1,0:T(8,128)}, bf16[2,768,768]{2,1,0:T(8,128)(2,1)}) custom-call(f32[512,768]{1,0:T(8,128)} %get-tuple-element.103.refs_0_.refs_12_.refs_11_, f32[1,768]{1,0:T(1,128)} %get-tuple-element.196.refs_1_.refs_13_, ...), custom_call_target="tpu_custom_call" | custom-call | tf_op jit(solution)/shard_map/send_rows/pallas_call | solution.py:1324
  256.3 37.2 %expert_rows.1 = (bf16[8,2,192,768]{3,2,1,0:T(8,128)(2,1)}, f32[8,2,192,1]{3,2,1,0:T(8,128)}, bf16[2,1536,1536]{2,1,0:T(8,128)(2,1)}, bf16[2,1536,1536]{2,1,0:T(8,128)(2,1)}, bf16[2,1536,768]{2,1,0:T(8,128)(2,1)}) custom-call(bf16[8,2,192,768]{3,2,1,0:T(8,128)(2,1)} %get-tuple-element.105.x_ref.refs_4_, bf16[8,2,192,768]{3,2,1,0:T(8,128)(2,1)} %all-to-all-done.c_ref, ...), custom_call_target="tpu_custom_call" | custom-call | flops 21743271936 | bytes 37748736 | tf_op jit(solution)/shard_map/expert_rows/pallas_call | solution.py:1767
  293.5 65.7 %return_rows.1 = (f32[512,768]{1,0:T(8,128)}, f32[1,768]{1,0:T(1,128)}, f32[16,768]{1,0:T(8,128)}, f32[2,768,768]{2,1,0:T(8,128)}, f32[2,768,768]{2,1,0:T(8,128)...) custom-call(bf16[8,2,192,768]{3,2,1,0:T(8,128)(2,1)} %get-tuple-element.110.refs_0_, ...), custom_call_target="tpu_custom_call" | custom-call | tf_op jit(solution)/shard_map/return_rows/pallas_call | solution.py:1591
  359.2 4.9 all-to-all-start.1
  365.2 35.8 %attend_back.2 = (f32[512,768]{1,0:T(8,128)}, bf16[8,400,768]{2,1,0:T(8,128)(2,1)}, f32[12,1024]{1,0:T(8,128)}, f32[1,768]{1,0:T(1,128)}) custom-call(s32[1]{0:T(128)S(6)} %copy.49.refs_0_, f32[512,768]{1,0:T(8,128)} %get-tuple-element.94.refs_1_, f32[1,768]{1,0:T(1,128)} %get-tuple-element.199.refs_2_, bf16[8,400,768]{2,1,0:T(8,128)(2,1)} %get-tuple-element.95.refs_3_, ...), custom_call_target="tpu_custom_call" | custom-call | flops 6845104128 | bytes 25165824 | tf_op jit(solution)/shard_map/attend_back/pallas_call | solution.py:361
  401.0 1.8 collective-permute-start.2
  402.9 21.8 %mlp_back.1 = (f32[512,768]{1,0:T(8,128)}, bf16[3072,768]{1,0:T(8,128)(2,1)}, bf16[8,384,768]{2,1,0:T(8,128)(2,1)}, f32[1,768]{1,0:T(1,128)}) custom-call(f32[512,768]{1,0:T(8,128)} %get-tuple-element.90.refs_0_, f32[1,768]{1,0:T(1,128)} %get-tuple-element.197.refs_1_, bf16[3072,768]{1,0:T(8,128)(2,1)} %bitcast.69, ...), custom_call_target="tpu_custom_call" | custom-call | flops 12079595520 | bytes 25165824 | tf_op jit(solution)/shard_map/mlp_back/pallas_call | solution.py:497
  424.8 62.2 %attend_back.3 = (bf16[400,768]{1,0:T(8,128)(2,1)}, bf16[384,768]{1,0:T(8,128)(2,1)}, bf16[1,512,768]{2,1,0:T(8,128)(2,1)}, f32[512,768]{1,0:T(8,128)}, bf16[8,3...) custom-call(s32[1]{0:T(128)S(6)} %copy.49.refs_0_, bf16[512,768]{1,0:T(8,128)(2,1)} %refs_1_.5, ...), custom_call_target="tpu_custom_call" | custom-call | flops 6845104128 | bytes 25165824 | tf_op jit(solution)/shard_map/attend_back/pallas_call | solution.py:361
  487.0 1.1 fusion.4
  489.5 79.4 %finish.1 = (f32[192,512]{1,0:T(8,128)}, f32[192,384]{1,0:T(8,128)}, f32[192,384]{1,0:T(8,128)}, f32[192,384]{1,0:T(8,128)}, f32[40,128]{1,0:T(8,128)}, /*index=...) custom-call(bf16[400,768]{1,0:T(8,128)(2,1)} %get-tuple-element.131.refs_0_, ...), custom_call_target="tpu_custom_call" | custom-call | tf_op jit(solution)/shard_map/finish/pallas_call | solution.py:1169
  570.0 1.0 slice_bitcast_fusion.4
  571.0 1.1 slice_bitcast_fusion
  575.6 1.2 reshape.130
  579.5 2.2 copy.50
  581.8 1.1 copy.51
  583.6 2.4 copy.53
  587.2 2.2 copy.54
  (75 shorter events, 19.9 us)
Async XLA Ops:
  0.6 128.0 %copy-start = (f32[2,12,44]{2,0,1:T(2,128)S(1)}, f32[2,12,44]{2,0,1:T(2,128)}, u32[]{:S(2)}) copy-start(f32[2,12,44]{2,0,1:T(2,128)} %param.18) | copy-start | bytes 12676
  113.3 5.4 copy-start.12
  113.3 14.6 %copy-start.11 = (s32[21]{0:T(128)S(1)}, s32[21]{0:T(128)}, u32[]{:S(2)}) copy-start(s32[21]{0:T(128)} %constant.16.clone) | copy-start | bytes 256
  113.3 14.7 %copy-start.7 = (f32[4,768]{1,0:T(4,128)S(1)}, f32[4,768]{1,0:T(4,128)}, u32[]{:S(2)}) copy-start(f32[4,768]{1,0:T(4,128)} %param.17) | copy-start | bytes 36868
  113.3 64.4 %all-to-all-start = ((bf16[8,2,192,768]{3,2,1,0:T(8,128)(2,1)}), bf16[8,2,192,768]{3,2,1,0:T(8,128)(2,1)}, u32[]{:S(2)}, u32[]{:S(2)}) async-start(bf16[8,2,192,768]{3,2,1,0:T(8,128)(2,1)} %bitcast.55), calls=%async_computation | async-start | bytes 9437184 | tf_op jit(solution)/shard_map/all_to_all | solution.py:1881
  118.7 59.0 %collective-permute-start = (bf16[2,768,768]{2,1,0:T(8,128)(2,1)S(1)}, bf16[2,768,768]{2,1,0:T(8,128)(2,1)}, u32[]{:S(2)}, u32[]{:S(2)}) collective-permute-start(bf16[2,768,768]{2,1,0:T(8,128)(2,1)S(1)} %copy-done.12), channel_id=1, source_target_pairs={{0,1},{1,0},{2,3},{3,2},{4,5},{5,4},{6,7},{7,6},{8,9},{9,8},{10,11... | collective-permute-start | bytes 7077896 | tf_op jit(solution)/shard_map/ppermute | solution.py:1877
  359.2 5.3 copy-start.6
  359.2 65.5 %all-to-all-start.1 = ((bf16[8,2,192,768]{3,2,1,0:T(8,128)(2,1)}), bf16[8,2,192,768]{3,2,1,0:T(8,128)(2,1)}, u32[]{:S(2)}, u32[]{:S(2)}) async-start(bf16[8,2,192,768]{3,2,1,0:T(8,128)(2,1)} %get-tuple-element.125), calls=%async_computation.1 | async-start | bytes 9437184 | tf_op jit(solution)/shard_map/all_to_all | solution.py:1881
  364.2 60.5 %collective-permute-start.1 = (bf16[2,768,768]{2,1,0:T(8,128)(2,1)}, bf16[2,768,768]{2,1,0:T(8,128)(2,1)S(1)}, u32[]{:S(2)}, u32[]{:S(2)}) collective-permute-start(bf16[2,768,768]{2,1,0:T(8,128)(2,1)} %get-tuple-element.126), channel_id=1, source_target_pairs={{0,1},{1,0},{2,3},{3,2},{4,5},{5,4},{6,7},{7,6},{8,9},{9,8},{10,11... | collective-permute-start | bytes 7077896 | tf_op jit(solution)/shard_map/ppermute | solution.py:1877
  401.0 87.1 %collective-permute-start.2 = (bf16[2,768,768]{2,1,0:T(8,128)(2,1)}, bf16[2,768,768]{2,1,0:T(8,128)(2,1)}, u32[]{:S(2)}, u32[]{:S(2)}) collective-permute-start(bf16[2,768,768]{2,1,0:T(8,128)(2,1)} %get-tuple-element.145), channel_id=1, source_target_pairs={{0,1},{1,0},{2,3},{3,2},{4,5},{5,4},{6,7},{7,6},{8,9},{9,8},{10,11... | collective-permute-start | bytes 7077896 | tf_op jit(solution)/shard_map/ppermute | solution.py:1877
  424.7 62.3 %copy-start.3 = (bf16[2,768,768]{2,1,0:T(8,128)(2,1)}, bf16[2,768,768]{2,1,0:T(8,128)(2,1)S(1)}, u32[]{:S(2)}) copy-start(bf16[2,768,768]{2,1,0:T(8,128)(2,1)S(1)} %collective-permute-done.1) | copy-start | bytes 7077892
  424.7 62.3 %copy-start.13 = (f32[12,1024]{1,0:T(8,128)S(1)}, f32[12,1024]{1,0:T(8,128)}, u32[]{:S(2)}) copy-start(f32[12,1024]{1,0:T(8,128)} %get-tuple-element.140) | copy-start | bytes 147460
  424.7 63.5 %copy-start.8 = (f32[1,768]{1,0:T(1,128)S(1)}, f32[1,768]{1,0:T(1,128)}, u32[]{:S(2)}) copy-start(f32[1,768]{1,0:T(1,128)} %get-tuple-element.138) | copy-start | bytes 9220
  424.7 63.5 %copy-start.9 = (f32[1,768]{1,0:T(1,128)S(1)}, f32[1,768]{1,0:T(1,128)}, u32[]{:S(2)}) copy-start(f32[1,768]{1,0:T(1,128)} %get-tuple-element.137) | copy-start | bytes 9220
  424.7 63.5 %copy-start.10 = (f32[1,768]{1,0:T(1,128)S(1)}, f32[1,768]{1,0:T(1,128)}, u32[]{:S(2)}) copy-start(f32[1,768]{1,0:T(1,128)} %get-tuple-element.136) | copy-start | bytes 9220
  568.9 12.8 %copy-start.4 = (f32[512,768]{1,0:T(8,128)S(1)}, f32[512,768]{1,0:T(8,128)}, u32[]{:S(2)}) copy-start(f32[512,768]{1,0:T(8,128)} %get-tuple-element.216) | copy-start | bytes 4718596
  571.0 11.9 %copy-start.5 = (f32[192,384]{1,0:T(8,128)S(1)}, f32[192,384]{1,0:T(8,128)}, u32[]{:S(2)}) copy-start(f32[192,384]{1,0:T(8,128)} %get-tuple-element.221) | copy-start | bytes 884740
  578.0 5.6 copy-start.2
  582.9 3.9 slice-start
  583.6 3.5 slice-start.1
  583.6 5.7 copy-start.1
